TPU v7x, 512 devices: a whole 4x8x8 slice. The times are simulated.
512 devices in a mesh: dom: 512 (over x, z, y, core).
Axes of the slice: x: 4, y: 8, z: 8, core: 2. Of those that a mesh axis runs over, the one named last changes fastest.
Arguments:
- blocks: bfloat16 [65536, 128, 128], P('dom'), may hold values from 2.4e-05 to 0.161
- col_index: int32 [512, 128], P('dom'), may hold values from 0 to 79, as said below
- row_offsets: int32 [512, 33], P('dom'), may hold values from 0 to 128, as said below
- send_index: int32 [512, 6, 8], P('dom'), may hold values from 0 to 31, as said below
- deg_scale: float32 [2097152], P('dom'), may hold values from 0.5 to 1
- seeds: float32 [16, 2097152], P(None, 'dom'), may hold values from 0.25 to 2
Outputs:
- spread: float32 [16, 2097152], P(None, 'dom')
Inputs may be any that keep to these rules, and one draw needn't show every extreme that they name: In every partition the offsets start at 0 and rise by 1 to 4 per block row; slots from row_offsets[p, 32] on are unused; some partition uses all 128 slots. `col_index`: the first slot of block row r names the partition's own block r; entries below 32 name own blocks, the others received blocks. `send_index`: each list names 8 distinct blocks of the sending partition; its six lists together name every one of its blocks.
All inputs are finite; a program needn't handle non-finite values.
Results may differ from a plain program's by a relative error of at most 0.0003.
Values may be sent and summed in bfloat16 or wider, within the bound.
No kernel may reach another device: no remote copies, remote signals or barrier semaphores. Data moves between devices by JAX's collectives and lax.ppermute only.
A program may use at most 64 MiB of HBM per device.

v0:
```python
import jax
import jax.numpy as jnp
from jax import lax
from jax.sharding import PartitionSpec as P

ITERS = 4


OFFSETS = (1, -1, 2, -2, 4, -4)
ALPHA = 0.8


def passed_along(x, axis, by):
    count = lax.axis_size(axis)
    return lax.ppermute(x, axis, [(i, (i + by) % count) for i in range(count)])


def on_device(blocks, col_index, row_offsets, send_index, deg_scale, seeds):
    blk = blocks.shape[1]
    width = seeds.shape[0]
    nrb = deg_scale.shape[0] // blk
    columns = col_index[0]
    offsets = row_offsets[0]
    lists = send_index[0]
    slots = jnp.arange(blocks.shape[0], dtype=jnp.int32)
    row_of = jnp.sum((offsets[1:, None] <= slots[None, :]).astype(jnp.int32), axis=0)
    onehot = (row_of[None, :] == jnp.arange(nrb, dtype=jnp.int32)[:, None]).astype(jnp.float32)
    scale = deg_scale.reshape(1, nrb, blk)
    base = seeds.reshape(width, nrb, blk)
    theirs = []
    for j in range(2):
        theirs.append(passed_along(lists[j], "dom", OFFSETS[j]))
    for j in range(2, 6):
        theirs.append(passed_along(lists[j], "dom", OFFSETS[j]))
    field = base
    for step in range(ITERS):
        scaled = (field * scale).astype(jnp.bfloat16)
        pieces = [scaled]
        for j in range(2):
            pieces.append(passed_along(scaled, "dom", OFFSETS[j])[:, theirs[j]])
        for j in range(2, 6):
            pieces.append(passed_along(scaled, "dom", OFFSETS[j])[:, theirs[j]])
        extended = jnp.concatenate(pieces, axis=1)
        picked = extended[:, columns]
        prods = jnp.einsum("ckj,kij->kci", picked, blocks, preferred_element_type=jnp.float32)
        summed = jnp.einsum("rk,kci->cri", onehot, prods, precision=lax.Precision.HIGHEST)
        field = ALPHA * scale * summed + (1.0 - ALPHA) * base
    return field.reshape(width, nrb * blk)


def solution(mesh):
    in_specs = (
        P("dom", None, None),
        P("dom", None),
        P("dom", None),
        P("dom", None, None),
        P("dom"),
        P(None, "dom"),
    )
    out_specs = P(None, "dom")
    return jax.shard_map(
        on_device, mesh=mesh, in_specs=in_specs, out_specs=out_specs, check_vma=False
    )
```

profile of v0, /device:TPU:1, one launch (start us, length us, event | category | flops | bytes accessed | tf_op | source)
XLA Modules:
  0.0 235.4 jit_solution(17612176747969213735)
XLA Ops:
  1.8 17.4 %collective-permute-start.10 = (bf16[16,32,128]{2,1,0:T(8,128)(2,1)S(1)}, bf16[16,32,128]{2,1,0:T(8,128)(2,1)S(1)}, u32[]{:S(2)}, u32[]{:S(2)}) collective-permute-start(bf16[16,32,128]{2,1,0:T(8,128)(2,1)S(1)} %get-tuple-element.5), channel_id=1, source_target_pairs={{0,508},{1,509},{2,510},{3,511},{4,0},{5,1},{6,2},{7,3},{8,4},{9,5... | collective-permute-start | bytes 393224 | tf_op jit(solution)/shard_map/ppermute | solution.py:15
  19.2 1.9 collective-permute-start.8
  21.1 8.9 %collective-permute-start.6 = (bf16[16,32,128]{2,1,0:T(8,128)(2,1)S(1)}, bf16[16,32,128]{2,1,0:T(8,128)(2,1)S(1)}, u32[]{:S(2)}, u32[]{:S(2)}) collective-permute-start(bf16[16,32,128]{2,1,0:T(8,128)(2,1)S(1)} %get-tuple-element.5), channel_id=1, source_target_pairs={{0,510},{1,511},{2,0},{3,1},{4,2},{5,3},{6,4},{7,5},{8,6},{9,7},{1... | collective-permute-start | bytes 393224 | tf_op jit(solution)/shard_map/ppermute | solution.py:15
  32.7 4.1 %collective-permute-start.11 = (s32[8]{0:T(128)S(1)}, s32[8]{0:T(128)S(1)}, u32[]{:S(2)}, u32[]{:S(2)}) collective-permute-start(s32[8]{0:T(128)S(1)} %get-tuple-element.7), channel_id=1, source_target_pairs={{0,508},{1,509},{2,510},{3,511},{4,0},{5,1},{6,2},{7,3},{8,4},{9,5... | collective-permute-start | bytes 104 | tf_op jit(solution)/shard_map/ppermute | solution.py:15
  39.1 13.0 %collective-permute-start.7 = (s32[8]{0:T(128)S(1)}, s32[8]{0:T(128)S(1)}, u32[]{:S(2)}, u32[]{:S(2)}) collective-permute-start(s32[8]{0:T(128)S(1)} %get-tuple-element.8), channel_id=1, source_target_pairs={{0,510},{1,511},{2,0},{3,1},{4,2},{5,3},{6,4},{7,5},{8,6},{9,7},{1... | collective-permute-start | bytes 104 | tf_op jit(solution)/shard_map/ppermute | solution.py:15
  54.7 8.0 %collective-permute-done.5 = s32[8]{0:T(128)S(1)} collective-permute-done((s32[8]{0:T(128)S(1)}, s32[8]{0:T(128)S(1)}, u32[]{:S(2)}, u32[]{:S(2)}) %collective-permute-start.5) | collective-permute-done | bytes 64 | tf_op jit(solution)/shard_map/ppermute | solution.py:15
  62.7 6.9 %collective-permute-start.3 = (s32[8]{0:T(128)S(1)}, s32[8]{0:T(128)S(1)}, u32[]{:S(2)}, u32[]{:S(2)}) collective-permute-start(s32[8]{0:T(128)S(1)} %get-tuple-element.10), channel_id=1, source_target_pairs={{0,511},{1,0},{2,1},{3,2},{4,3},{5,4},{6,5},{7,6},{8,7},{9,8},{10,... | collective-permute-start | bytes 104 | tf_op jit(solution)/shard_map/ppermute | solution.py:15
  75.3 8.7 %collective-permute-done.9 = s32[8]{0:T(128)S(1)} collective-permute-done((s32[8]{0:T(128)S(1)}, s32[8]{0:T(128)S(1)}, u32[]{:S(2)}, u32[]{:S(2)}) %collective-permute-start.9) | collective-permute-done | bytes 64 | tf_op jit(solution)/shard_map/ppermute | solution.py:15
  84.0 10.8 %collective-permute-start.2 = (bf16[16,32,128]{2,1,0:T(8,128)(2,1)S(1)}, bf16[16,32,128]{2,1,0:T(8,128)(2,1)S(1)}, u32[]{:S(2)}, u32[]{:S(2)}) collective-permute-start(bf16[16,32,128]{2,1,0:T(8,128)(2,1)S(1)} %get-tuple-element.5), channel_id=1, source_target_pairs={{0,511},{1,0},{2,1},{3,2},{4,3},{5,4},{6,5},{7,6},{8,7},{9,8},{10,... | collective-permute-start | bytes 393224 | tf_op jit(solution)/shard_map/ppermute | solution.py:15
  101.6 4.5 %fusion.24 = f32[128,16,128]{2,1,0:T(8,128)S(1)} fusion(bf16[128,128,128]{2,1,0:T(8,128)(2,1)} %param.6, bf16[128,16,128]{2,1,0:T(8,128)(2,1)S(1)} %gather_fusion.6), kind=kOutput, calls=%fused_computation.56 | convolution fusion | flops 67108864 | bytes 5767168 | tf_op jit(solution)/shard_map/ckj,kij->kci/dot_general | solution.py:45
  108.7 4.3 %collective-permute-start.16 = (bf16[16,32,128]{2,1,0:T(8,128)(2,1)S(1)}, bf16[16,32,128]{2,1,0:T(8,128)(2,1)S(1)}, u32[]{:S(2)}, u32[]{:S(2)}) collective-permute-start(bf16[16,32,128]{2,1,0:T(8,128)(2,1)S(1)} %get-tuple-element.14), channel_id=1, source_target_pairs={{0,4},{1,5},{2,6},{3,7},{4,8},{5,9},{6,10},{7,11},{8,12},{9,13},{1... | collective-permute-start | bytes 393224 | tf_op jit(solution)/shard_map/ppermute | solution.py:15
  113.0 14.1 %collective-permute-start.15 = (bf16[16,32,128]{2,1,0:T(8,128)(2,1)S(1)}, bf16[16,32,128]{2,1,0:T(8,128)(2,1)S(1)}, u32[]{:S(2)}, u32[]{:S(2)}) collective-permute-start(bf16[16,32,128]{2,1,0:T(8,128)(2,1)S(1)} %get-tuple-element.14), channel_id=1, source_target_pairs={{0,510},{1,511},{2,0},{3,1},{4,2},{5,3},{6,4},{7,5},{8,6},{9,7},{1... | collective-permute-start | bytes 393224 | tf_op jit(solution)/shard_map/ppermute | solution.py:15
  131.0 3.6 %collective-permute-start.12 = (bf16[16,32,128]{2,1,0:T(8,128)(2,1)S(1)}, bf16[16,32,128]{2,1,0:T(8,128)(2,1)S(1)}, u32[]{:S(2)}, u32[]{:S(2)}) collective-permute-start(bf16[16,32,128]{2,1,0:T(8,128)(2,1)S(1)} %get-tuple-element.14), channel_id=1, source_target_pairs={{0,1},{1,2},{2,3},{3,4},{4,5},{5,6},{6,7},{7,8},{8,9},{9,10},{10,1... | collective-permute-start | bytes 393224 | tf_op jit(solution)/shard_map/ppermute | solution.py:15
  142.6 4.5 %fusion.22 = f32[128,16,128]{2,1,0:T(8,128)S(1)} fusion(bf16[128,128,128]{2,1,0:T(8,128)(2,1)} %param.6, bf16[128,16,128]{2,1,0:T(8,128)(2,1)S(1)} %gather_fusion.13), kind=kOutput, calls=%fused_computation.54 | convolution fusion | flops 67108864 | bytes 5767168 | tf_op jit(solution)/shard_map/ckj,kij->kci/dot_general | solution.py:45
  147.8 1.9 collective-permute-start.23
  149.7 4.3 %collective-permute-start.22 = (bf16[16,32,128]{2,1,0:T(8,128)(2,1)S(1)}, bf16[16,32,128]{2,1,0:T(8,128)(2,1)S(1)}, u32[]{:S(2)}, u32[]{:S(2)}) collective-permute-start(bf16[16,32,128]{2,1,0:T(8,128)(2,1)S(1)} %get-tuple-element.16), channel_id=1, source_target_pairs={{0,4},{1,5},{2,6},{3,7},{4,8},{5,9},{6,10},{7,11},{8,12},{9,13},{1... | collective-permute-start | bytes 393224 | tf_op jit(solution)/shard_map/ppermute | solution.py:15
  154.0 16.5 %collective-permute-start.21 = (bf16[16,32,128]{2,1,0:T(8,128)(2,1)S(1)}, bf16[16,32,128]{2,1,0:T(8,128)(2,1)S(1)}, u32[]{:S(2)}, u32[]{:S(2)}) collective-permute-start(bf16[16,32,128]{2,1,0:T(8,128)(2,1)S(1)} %get-tuple-element.16), channel_id=1, source_target_pairs={{0,510},{1,511},{2,0},{3,1},{4,2},{5,3},{6,4},{7,5},{8,6},{9,7},{1... | collective-permute-start | bytes 393224 | tf_op jit(solution)/shard_map/ppermute | solution.py:15
  174.4 3.6 %collective-permute-start.18 = (bf16[16,32,128]{2,1,0:T(8,128)(2,1)S(1)}, bf16[16,32,128]{2,1,0:T(8,128)(2,1)S(1)}, u32[]{:S(2)}, u32[]{:S(2)}) collective-permute-start(bf16[16,32,128]{2,1,0:T(8,128)(2,1)S(1)} %get-tuple-element.16), channel_id=1, source_target_pairs={{0,1},{1,2},{2,3},{3,4},{4,5},{5,6},{6,7},{7,8},{8,9},{9,10},{10,1... | collective-permute-start | bytes 393224 | tf_op jit(solution)/shard_map/ppermute | solution.py:15
  185.9 4.5 %fusion.20 = f32[128,16,128]{2,1,0:T(8,128)S(1)} fusion(bf16[128,128,128]{2,1,0:T(8,128)(2,1)} %param.6, bf16[128,16,128]{2,1,0:T(8,128)(2,1)S(1)} %gather_fusion.20), kind=kOutput, calls=%fused_computation.52 | convolution fusion | flops 67108864 | bytes 5767168 | tf_op jit(solution)/shard_map/ckj,kij->kci/dot_general | solution.py:45
  191.2 1.9 collective-permute-start.29
  193.1 4.3 %collective-permute-start.28 = (bf16[16,32,128]{2,1,0:T(8,128)(2,1)S(1)}, bf16[16,32,128]{2,1,0:T(8,128)(2,1)S(1)}, u32[]{:S(2)}, u32[]{:S(2)}) collective-permute-start(bf16[16,32,128]{2,1,0:T(8,128)(2,1)S(1)} %get-tuple-element.18), channel_id=1, source_target_pairs={{0,4},{1,5},{2,6},{3,7},{4,8},{5,9},{6,10},{7,11},{8,12},{9,13},{1... | collective-permute-start | bytes 393224 | tf_op jit(solution)/shard_map/ppermute | solution.py:15
  197.4 16.5 %collective-permute-start.27 = (bf16[16,32,128]{2,1,0:T(8,128)(2,1)S(1)}, bf16[16,32,128]{2,1,0:T(8,128)(2,1)S(1)}, u32[]{:S(2)}, u32[]{:S(2)}) collective-permute-start(bf16[16,32,128]{2,1,0:T(8,128)(2,1)S(1)} %get-tuple-element.18), channel_id=1, source_target_pairs={{0,510},{1,511},{2,0},{3,1},{4,2},{5,3},{6,4},{7,5},{8,6},{9,7},{1... | collective-permute-start | bytes 393224 | tf_op jit(solution)/shard_map/ppermute | solution.py:15
  217.7 3.8 %collective-permute-start.24 = (bf16[16,32,128]{2,1,0:T(8,128)(2,1)S(1)}, bf16[16,32,128]{2,1,0:T(8,128)(2,1)S(1)}, u32[]{:S(2)}, u32[]{:S(2)}) collective-permute-start(bf16[16,32,128]{2,1,0:T(8,128)(2,1)S(1)} %get-tuple-element.18), channel_id=1, source_target_pairs={{0,1},{1,2},{2,3},{3,4},{4,5},{5,6},{6,7},{7,8},{8,9},{9,10},{10,1... | collective-permute-start | bytes 393224 | tf_op jit(solution)/shard_map/ppermute | solution.py:15
  229.3 4.5 %fusion.18 = f32[128,16,128]{2,1,0:T(8,128)S(1)} fusion(bf16[128,128,128]{2,1,0:T(8,128)(2,1)} %param.6, bf16[128,16,128]{2,1,0:T(8,128)(2,1)S(1)} %gather_fusion.27), kind=kOutput, calls=%fused_computation.50 | convolution fusion | flops 67108864 | bytes 5767168 | tf_op jit(solution)/shard_map/ckj,kij->kci/dot_general | solution.py:45
  (148 shorter events, 62.2 us)
Async XLA Ops:
  1.8 93.0 %collective-permute-start.10 = (bf16[16,32,128]{2,1,0:T(8,128)(2,1)S(1)}, bf16[16,32,128]{2,1,0:T(8,128)(2,1)S(1)}, u32[]{:S(2)}, u32[]{:S(2)}) collective-permute-start(bf16[16,32,128]{2,1,0:T(8,128)(2,1)S(1)} %get-tuple-element.5), channel_id=1, source_target_pairs={{0,508},{1,509},{2,510},{3,511},{4,0},{5,1},{6,2},{7,3},{8,4},{9,5... | collective-permute-start | bytes 393224 | tf_op jit(solution)/shard_map/ppermute | solution.py:15
  19.2 78.2 %collective-permute-start.8 = (bf16[16,32,128]{2,1,0:T(8,128)(2,1)S(1)}, bf16[16,32,128]{2,1,0:T(8,128)(2,1)S(1)}, u32[]{:S(2)}, u32[]{:S(2)}) collective-permute-start(bf16[16,32,128]{2,1,0:T(8,128)(2,1)S(1)} %get-tuple-element.5), channel_id=1, source_target_pairs={{0,4},{1,5},{2,6},{3,7},{4,8},{5,9},{6,10},{7,11},{8,12},{9,13},{1... | collective-permute-start | bytes 393224 | tf_op jit(solution)/shard_map/ppermute | solution.py:15
  21.1 77.0 %collective-permute-start.6 = (bf16[16,32,128]{2,1,0:T(8,128)(2,1)S(1)}, bf16[16,32,128]{2,1,0:T(8,128)(2,1)S(1)}, u32[]{:S(2)}, u32[]{:S(2)}) collective-permute-start(bf16[16,32,128]{2,1,0:T(8,128)(2,1)S(1)} %get-tuple-element.5), channel_id=1, source_target_pairs={{0,510},{1,511},{2,0},{3,1},{4,2},{5,3},{6,4},{7,5},{8,6},{9,7},{1... | collective-permute-start | bytes 393224 | tf_op jit(solution)/shard_map/ppermute | solution.py:15
  30.0 68.7 %collective-permute-start.4 = (bf16[16,32,128]{2,1,0:T(8,128)(2,1)S(1)}, bf16[16,32,128]{2,1,0:T(8,128)(2,1)S(1)}, u32[]{:S(2)}, u32[]{:S(2)}) collective-permute-start(bf16[16,32,128]{2,1,0:T(8,128)(2,1)S(1)} %get-tuple-element.5), channel_id=1, source_target_pairs={{0,2},{1,3},{2,4},{3,5},{4,6},{5,7},{6,8},{7,9},{8,10},{9,11},{10,... | collective-permute-start | bytes 393224 | tf_op jit(solution)/shard_map/ppermute | solution.py:15
  39.1 13.7 %collective-permute-start.7 = (s32[8]{0:T(128)S(1)}, s32[8]{0:T(128)S(1)}, u32[]{:S(2)}, u32[]{:S(2)}) collective-permute-start(s32[8]{0:T(128)S(1)} %get-tuple-element.8), channel_id=1, source_target_pairs={{0,510},{1,511},{2,0},{3,1},{4,2},{5,3},{6,4},{7,5},{8,6},{9,7},{1... | collective-permute-start | bytes 104 | tf_op jit(solution)/shard_map/ppermute | solution.py:15
  52.8 9.9 %collective-permute-start.5 = (s32[8]{0:T(128)S(1)}, s32[8]{0:T(128)S(1)}, u32[]{:S(2)}, u32[]{:S(2)}) collective-permute-start(s32[8]{0:T(128)S(1)} %get-tuple-element.9), channel_id=1, source_target_pairs={{0,2},{1,3},{2,4},{3,5},{4,6},{5,7},{6,8},{7,9},{8,10},{9,11},{10,... | collective-permute-start | bytes 104 | tf_op jit(solution)/shard_map/ppermute | solution.py:15
  73.4 10.6 %collective-permute-start.9 = (s32[8]{0:T(128)S(1)}, s32[8]{0:T(128)S(1)}, u32[]{:S(2)}, u32[]{:S(2)}) collective-permute-start(s32[8]{0:T(128)S(1)} %get-tuple-element.12), channel_id=1, source_target_pairs={{0,4},{1,5},{2,6},{3,7},{4,8},{5,9},{6,10},{7,11},{8,12},{9,13},{1... | collective-permute-start | bytes 104 | tf_op jit(solution)/shard_map/ppermute | solution.py:15
  84.0 15.4 %collective-permute-start.2 = (bf16[16,32,128]{2,1,0:T(8,128)(2,1)S(1)}, bf16[16,32,128]{2,1,0:T(8,128)(2,1)S(1)}, u32[]{:S(2)}, u32[]{:S(2)}) collective-permute-start(bf16[16,32,128]{2,1,0:T(8,128)(2,1)S(1)} %get-tuple-element.5), channel_id=1, source_target_pairs={{0,511},{1,0},{2,1},{3,2},{4,3},{5,4},{6,5},{7,6},{8,7},{9,8},{10,... | collective-permute-start | bytes 393224 | tf_op jit(solution)/shard_map/ppermute | solution.py:15
  106.8 24.2 %collective-permute-start.17 = (bf16[16,32,128]{2,1,0:T(8,128)(2,1)S(1)}, bf16[16,32,128]{2,1,0:T(8,128)(2,1)S(1)}, u32[]{:S(2)}, u32[]{:S(2)}) collective-permute-start(bf16[16,32,128]{2,1,0:T(8,128)(2,1)S(1)} %get-tuple-element.14), channel_id=1, source_target_pairs={{0,508},{1,509},{2,510},{3,511},{4,0},{5,1},{6,2},{7,3},{8,4},{9,5... | collective-permute-start | bytes 393224 | tf_op jit(solution)/shard_map/ppermute | solution.py:15
  108.7 26.5 %collective-permute-start.16 = (bf16[16,32,128]{2,1,0:T(8,128)(2,1)S(1)}, bf16[16,32,128]{2,1,0:T(8,128)(2,1)S(1)}, u32[]{:S(2)}, u32[]{:S(2)}) collective-permute-start(bf16[16,32,128]{2,1,0:T(8,128)(2,1)S(1)} %get-tuple-element.14), channel_id=1, source_target_pairs={{0,4},{1,5},{2,6},{3,7},{4,8},{5,9},{6,10},{7,11},{8,12},{9,13},{1... | collective-permute-start | bytes 393224 | tf_op jit(solution)/shard_map/ppermute | solution.py:15
  113.0 22.9 %collective-permute-start.15 = (bf16[16,32,128]{2,1,0:T(8,128)(2,1)S(1)}, bf16[16,32,128]{2,1,0:T(8,128)(2,1)S(1)}, u32[]{:S(2)}, u32[]{:S(2)}) collective-permute-start(bf16[16,32,128]{2,1,0:T(8,128)(2,1)S(1)} %get-tuple-element.14), channel_id=1, source_target_pairs={{0,510},{1,511},{2,0},{3,1},{4,2},{5,3},{6,4},{7,5},{8,6},{9,7},{1... | collective-permute-start | bytes 393224 | tf_op jit(solution)/shard_map/ppermute | solution.py:15
  127.1 11.1 %collective-permute-start.14 = (bf16[16,32,128]{2,1,0:T(8,128)(2,1)S(1)}, bf16[16,32,128]{2,1,0:T(8,128)(2,1)S(1)}, u32[]{:S(2)}, u32[]{:S(2)}) collective-permute-start(bf16[16,32,128]{2,1,0:T(8,128)(2,1)S(1)} %get-tuple-element.14), channel_id=1, source_target_pairs={{0,2},{1,3},{2,4},{3,5},{4,6},{5,7},{6,8},{7,9},{8,10},{9,11},{10,... | collective-permute-start | bytes 393224 | tf_op jit(solution)/shard_map/ppermute | solution.py:15
  129.1 9.8 %collective-permute-start.13 = (bf16[16,32,128]{2,1,0:T(8,128)(2,1)S(1)}, bf16[16,32,128]{2,1,0:T(8,128)(2,1)S(1)}, u32[]{:S(2)}, u32[]{:S(2)}) collective-permute-start(bf16[16,32,128]{2,1,0:T(8,128)(2,1)S(1)} %get-tuple-element.14), channel_id=1, source_target_pairs={{0,511},{1,0},{2,1},{3,2},{4,3},{5,4},{6,5},{7,6},{8,7},{9,8},{10,... | collective-permute-start | bytes 393224 | tf_op jit(solution)/shard_map/ppermute | solution.py:15
  131.0 10.0 %collective-permute-start.12 = (bf16[16,32,128]{2,1,0:T(8,128)(2,1)S(1)}, bf16[16,32,128]{2,1,0:T(8,128)(2,1)S(1)}, u32[]{:S(2)}, u32[]{:S(2)}) collective-permute-start(bf16[16,32,128]{2,1,0:T(8,128)(2,1)S(1)} %get-tuple-element.14), channel_id=1, source_target_pairs={{0,1},{1,2},{2,3},{3,4},{4,5},{5,6},{6,7},{7,8},{8,9},{9,10},{10,1... | collective-permute-start | bytes 393224 | tf_op jit(solution)/shard_map/ppermute | solution.py:15
  147.8 26.5 %collective-permute-start.23 = (bf16[16,32,128]{2,1,0:T(8,128)(2,1)S(1)}, bf16[16,32,128]{2,1,0:T(8,128)(2,1)S(1)}, u32[]{:S(2)}, u32[]{:S(2)}) collective-permute-start(bf16[16,32,128]{2,1,0:T(8,128)(2,1)S(1)} %get-tuple-element.16), channel_id=1, source_target_pairs={{0,508},{1,509},{2,510},{3,511},{4,0},{5,1},{6,2},{7,3},{8,4},{9,5... | collective-permute-start | bytes 393224 | tf_op jit(solution)/shard_map/ppermute | solution.py:15
  149.7 28.9 %collective-permute-start.22 = (bf16[16,32,128]{2,1,0:T(8,128)(2,1)S(1)}, bf16[16,32,128]{2,1,0:T(8,128)(2,1)S(1)}, u32[]{:S(2)}, u32[]{:S(2)}) collective-permute-start(bf16[16,32,128]{2,1,0:T(8,128)(2,1)S(1)} %get-tuple-element.16), channel_id=1, source_target_pairs={{0,4},{1,5},{2,6},{3,7},{4,8},{5,9},{6,10},{7,11},{8,12},{9,13},{1... | collective-permute-start | bytes 393224 | tf_op jit(solution)/shard_map/ppermute | solution.py:15
  154.0 25.3 %collective-permute-start.21 = (bf16[16,32,128]{2,1,0:T(8,128)(2,1)S(1)}, bf16[16,32,128]{2,1,0:T(8,128)(2,1)S(1)}, u32[]{:S(2)}, u32[]{:S(2)}) collective-permute-start(bf16[16,32,128]{2,1,0:T(8,128)(2,1)S(1)} %get-tuple-element.16), channel_id=1, source_target_pairs={{0,510},{1,511},{2,0},{3,1},{4,2},{5,3},{6,4},{7,5},{8,6},{9,7},{1... | collective-permute-start | bytes 393224 | tf_op jit(solution)/shard_map/ppermute | solution.py:15
  170.5 11.1 %collective-permute-start.20 = (bf16[16,32,128]{2,1,0:T(8,128)(2,1)S(1)}, bf16[16,32,128]{2,1,0:T(8,128)(2,1)S(1)}, u32[]{:S(2)}, u32[]{:S(2)}) collective-permute-start(bf16[16,32,128]{2,1,0:T(8,128)(2,1)S(1)} %get-tuple-element.16), channel_id=1, source_target_pairs={{0,2},{1,3},{2,4},{3,5},{4,6},{5,7},{6,8},{7,9},{8,10},{9,11},{10,... | collective-permute-start | bytes 393224 | tf_op jit(solution)/shard_map/ppermute | solution.py:15
  174.4 10.0 %collective-permute-start.18 = (bf16[16,32,128]{2,1,0:T(8,128)(2,1)S(1)}, bf16[16,32,128]{2,1,0:T(8,128)(2,1)S(1)}, u32[]{:S(2)}, u32[]{:S(2)}) collective-permute-start(bf16[16,32,128]{2,1,0:T(8,128)(2,1)S(1)} %get-tuple-element.16), channel_id=1, source_target_pairs={{0,1},{1,2},{2,3},{3,4},{4,5},{5,6},{6,7},{7,8},{8,9},{9,10},{10,1... | collective-permute-start | bytes 393224 | tf_op jit(solution)/shard_map/ppermute | solution.py:15
  191.2 26.5 %collective-permute-start.29 = (bf16[16,32,128]{2,1,0:T(8,128)(2,1)S(1)}, bf16[16,32,128]{2,1,0:T(8,128)(2,1)S(1)}, u32[]{:S(2)}, u32[]{:S(2)}) collective-permute-start(bf16[16,32,128]{2,1,0:T(8,128)(2,1)S(1)} %get-tuple-element.18), channel_id=1, source_target_pairs={{0,508},{1,509},{2,510},{3,511},{4,0},{5,1},{6,2},{7,3},{8,4},{9,5... | collective-permute-start | bytes 393224 | tf_op jit(solution)/shard_map/ppermute | solution.py:15
  193.1 29.1 %collective-permute-start.28 = (bf16[16,32,128]{2,1,0:T(8,128)(2,1)S(1)}, bf16[16,32,128]{2,1,0:T(8,128)(2,1)S(1)}, u32[]{:S(2)}, u32[]{:S(2)}) collective-permute-start(bf16[16,32,128]{2,1,0:T(8,128)(2,1)S(1)} %get-tuple-element.18), channel_id=1, source_target_pairs={{0,4},{1,5},{2,6},{3,7},{4,8},{5,9},{6,10},{7,11},{8,12},{9,13},{1... | collective-permute-start | bytes 393224 | tf_op jit(solution)/shard_map/ppermute | solution.py:15
  197.4 25.5 %collective-permute-start.27 = (bf16[16,32,128]{2,1,0:T(8,128)(2,1)S(1)}, bf16[16,32,128]{2,1,0:T(8,128)(2,1)S(1)}, u32[]{:S(2)}, u32[]{:S(2)}) collective-permute-start(bf16[16,32,128]{2,1,0:T(8,128)(2,1)S(1)} %get-tuple-element.18), channel_id=1, source_target_pairs={{0,510},{1,511},{2,0},{3,1},{4,2},{5,3},{6,4},{7,5},{8,6},{9,7},{1... | collective-permute-start | bytes 393224 | tf_op jit(solution)/shard_map/ppermute | solution.py:15
  213.9 11.1 %collective-permute-start.26 = (bf16[16,32,128]{2,1,0:T(8,128)(2,1)S(1)}, bf16[16,32,128]{2,1,0:T(8,128)(2,1)S(1)}, u32[]{:S(2)}, u32[]{:S(2)}) collective-permute-start(bf16[16,32,128]{2,1,0:T(8,128)(2,1)S(1)} %get-tuple-element.18), channel_id=1, source_target_pairs={{0,2},{1,3},{2,4},{3,5},{4,6},{5,7},{6,8},{7,9},{8,10},{9,11},{10,... | collective-permute-start | bytes 393224 | tf_op jit(solution)/shard_map/ppermute | solution.py:15
  217.7 10.0 %collective-permute-start.24 = (bf16[16,32,128]{2,1,0:T(8,128)(2,1)S(1)}, bf16[16,32,128]{2,1,0:T(8,128)(2,1)S(1)}, u32[]{:S(2)}, u32[]{:S(2)}) collective-permute-start(bf16[16,32,128]{2,1,0:T(8,128)(2,1)S(1)} %get-tuple-element.18), channel_id=1, source_target_pairs={{0,1},{1,2},{2,3},{3,4},{4,5},{5,6},{6,7},{7,8},{8,9},{9,10},{10,1... | collective-permute-start | bytes 393224 | tf_op jit(solution)/shard_map/ppermute | solution.py:15
  (7 other events, 48.5 us)
where the time goes:
time: 239 us; the launch traced here: 235 us
  starting transfers between devices  161 us (67%)
  waiting for transfers between devices  28.6 us (12%)
  local copies, waits for them, and re-layouts  21.8 us (9%)
  matrix products  20.9 us (9%)
    ppermute x30, starting transfers between devices, passed_along(): return lax.ppermute(x, axis, [(i, (i + by) % count) for i in range(count)])  161 us
    ppermute x30, waiting for transfers between devices, passed_along(): return lax.ppermute(x, axis, [(i, (i + by) % count) for i in range(count)])  28.6 us
    dot_general x4, matrix products, on_device(): jnp.einsum('ckj,kij->kci', picked, blocks, preferred_element_type=jnp.flo...  17.8 us
    gather x24, local copies, waits for them, and re-layouts, on_device(): pieces.append(passed_along(scaled, 'dom', OFFSETS[j])[:, theirs[j]])  13.5 us
  transfers between devices with their start and end apart: 30, of which 11 were waited for; matrix products, arithmetic and copies ran while one was open for 7% of the time, Pallas kernels for 0%

commit v1 on v0

v1 whole, which is shorter than its diff:
```python
import functools

import jax
import jax.numpy as jnp
from jax import lax
from jax.experimental import pallas as pl
from jax.experimental.pallas import tpu as pltpu
from jax.sharding import PartitionSpec as P

ITERS = 4
ALPHA = 0.8

SRC_NEAR, SRC_FAR, SRC_SIDE, SRC_SIB, SRC_ZERO = 32, 56, 72, 96, 128


def chip_groups(count):
    return [[2 * c, 2 * c + 1] for c in range(count // 2)]


def matching(count, step):
    chips = count // 2
    pairs = []
    for c in range(chips):
        k = (c // step) % 2
        for core, other in ((k, c + step), (1 - k, c - step)):
            pairs.append((2 * c + core, 2 * (other % chips) + core))
    return pairs


def tables(me, lists, columns):
    k = me & 1
    chip = me >> 1
    first = k == 0
    up1 = ((chip ^ k) & 1) == 0
    up2 = (((chip >> 1) ^ k) & 1) == 0
    sel = jnp.where
    seq = jnp.arange(lists.shape[1], dtype=jnp.int32)

    def own(j):
        pick = (jnp.arange(6, dtype=jnp.int32) == j)[:, None]
        return jnp.sum(sel(pick, lists, 0), axis=0)

    def sib(u):
        return 32 + 8 * u + seq

    near = sel(up1, 3, 2)
    third = sel(first & up1, 1, sel(first | up1, near, 0))
    give = jnp.concatenate([own(k), own(near), own(third), own(sel(up2, 5, 4))])
    send = jnp.concatenate(
        [
            sel(first & ~up1, own(1), sib(1)),
            sel(first, sel(up1, own(2), sib(1)), sel(up1, own(0), sib(2))),
            sel(first & up1, sib(2), sel(up1, own(2), own(3))),
            sib(3),
            own(sel(up2, 4, 5)),
        ]
    )
    near1, near2 = SRC_NEAR + 8, SRC_NEAR + 16
    side0, side1, side2 = SRC_SIDE, SRC_SIDE + 8, SRC_SIDE + 16
    base = [
        sel(first, sel(up1, side1, near2), SRC_SIB),
        sel(first, SRC_SIB, sel(up1, near1, side0)),
        sel(up1, side0, sel(first, near1, near2)),
        sel(up1, near2, sel(first, side0, side1)),
        sel(up2, side2, SRC_FAR + 8),
        sel(up2, SRC_FAR + 8, side2),
    ]
    unit = (columns - 32) >> 3
    at = columns
    for j in range(6):
        at = sel(unit == j, base[j] + ((columns - 32) & 7), at)
    return give.astype(jnp.int32), send.astype(jnp.int32), at.astype(jnp.int32), k.reshape(1)


def first_kernel(give, seeds, scale, x_out, give_out):
    nrb = x_out.shape[0]
    for r in range(nrb):
        field = seeds[:, r * 128 : (r + 1) * 128]
        x_out[r] = (field * scale[r : r + 1, :]).astype(jnp.bfloat16)
    for i in range(32):
        give_out[i] = x_out[give[i]]


def pack_kernel(core, send, x, chip, near, far, src):
    src[0:32] = x[...]
    src[32:64] = chip[1 - core[0]]
    for i in range(24):
        near[i] = src[send[i]]
    for i in range(16):
        far[i] = src[send[24 + i]]


def step_kernel(last, core, give, at, offsets, x, chip, near, far, side, seeds, scale, blocks, *rest):
    if last:
        out, src = rest
    else:
        x_out, give_out, src = rest
    other = 1 - core[0]
    src[0:32] = x[...]
    src[SRC_NEAR : SRC_NEAR + 24] = near[...]
    src[SRC_FAR : SRC_FAR + 16] = far[...]
    src[SRC_SIDE : SRC_SIDE + 24] = side[other]
    src[SRC_SIB : SRC_SIB + 8] = chip[other, 0:8]
    src[SRC_ZERO] = jnp.zeros((16, 128), jnp.bfloat16)

    def row(r):
        start, end = offsets[r], offsets[r + 1]
        lhs, rhs = [], []
        for s in range(4):
            slot = jnp.minimum(start + s, 127)
            lhs.append(src[jnp.where(start + s < end, at[slot], SRC_ZERO)])
            rhs.append(blocks[slot])
        total = None
        for h in range(2):
            part = lax.dot_general(
                jnp.concatenate(lhs[2 * h : 2 * h + 2], axis=1),
                jnp.concatenate(rhs[2 * h : 2 * h + 2], axis=1),
                (((1,), (1,)), ((), ())),
                preferred_element_type=jnp.float32,
            )
            total = part if total is None else total + part
        s = scale[pl.ds(r, 1), :]
        where = pl.ds(pl.multiple_of(r * 128, 128), 128)
        field = ALPHA * s * total + (1.0 - ALPHA) * seeds[:, where]
        if last:
            out[:, where] = field
        else:
            x_out[r] = (field * s).astype(jnp.bfloat16)

    def group(g, carry):
        for i in range(4):
            row(g * 4 + i)
        return carry

    lax.fori_loop(0, 8, group, 0)
    if not last:
        for i in range(32):
            give_out[i] = x_out[give[i]]


SMEM = pl.BlockSpec(memory_space=pltpu.SMEM)
VMEM = pl.BlockSpec(memory_space=pltpu.VMEM)


def bf16(*shape):
    return jax.ShapeDtypeStruct(shape, jnp.bfloat16)


def on_device(count, blocks, col_index, row_offsets, send_index, deg_scale, seeds):
    me = lax.axis_index("dom")
    nrb = deg_scale.shape[0] // 128
    give, send, at, core = tables(me, send_index[0], col_index[0])
    offsets = row_offsets[0]
    scale = deg_scale.reshape(nrb, 128)
    groups = chip_groups(count)
    near_pairs, far_pairs = matching(count, 1), matching(count, 2)
    params = pltpu.CompilerParams(vmem_limit_bytes=16 << 20)

    x, gift = pl.pallas_call(
        first_kernel,
        out_shape=(bf16(nrb, 16, 128), bf16(32, 16, 128)),
        in_specs=[SMEM, VMEM, VMEM],
        out_specs=(VMEM, VMEM),
        compiler_params=params,
        name="first",
    )(give, seeds, scale)
    for step in range(ITERS):
        chip = lax.all_gather(gift, "dom", axis=0, axis_index_groups=groups, tiled=False)
        near, far = pl.pallas_call(
            pack_kernel,
            out_shape=(bf16(24, 16, 128), bf16(16, 16, 128)),
            in_specs=[SMEM, SMEM, VMEM, VMEM],
            out_specs=(VMEM, VMEM),
            scratch_shapes=[pltpu.VMEM((64, 16, 128), jnp.bfloat16)],
            compiler_params=params,
            name="pack",
        )(core, send, x, chip)
        far = lax.ppermute(far, "dom", far_pairs)
        near = lax.ppermute(near, "dom", near_pairs)
        side = lax.all_gather(
            jnp.concatenate([near[:16], far[:8]]), "dom", axis=0, axis_index_groups=groups, tiled=False
        )
        last = step == ITERS - 1
        out_shape = jax.ShapeDtypeStruct(seeds.shape, jnp.float32) if last else (bf16(nrb, 16, 128), bf16(32, 16, 128))
        result = pl.pallas_call(
            functools.partial(step_kernel, last),
            out_shape=out_shape,
            in_specs=[SMEM] * 4 + [VMEM] * 8,
            out_specs=VMEM if last else (VMEM, VMEM),
            scratch_shapes=[pltpu.VMEM((SRC_ZERO + 1, 16, 128), jnp.bfloat16)],
            compiler_params=params,
            name="last" if last else "step",
        )(core, give, at, offsets, x, chip, near, far, side, seeds, scale, blocks)
        if not last:
            x, gift = result
    return result


def solution(mesh):
    in_specs = (
        P("dom", None, None),
        P("dom", None),
        P("dom", None),
        P("dom", None, None),
        P("dom"),
        P(None, "dom"),
    )
    out_specs = P(None, "dom")
    return jax.shard_map(
        functools.partial(on_device, mesh.size), mesh=mesh, in_specs=in_specs, out_specs=out_specs, check_vma=False
    )
```

time: 239 us -> 113 us (0.47); the launches traced: 235 us -> 113 us
  starting transfers between devices: 161 us -> 31.5 us
  blocking collectives: 0 us -> 22.4 us
  matrix products: 20.9 us -> 0 us
  local copies, waits for them, and re-layouts: 21.8 us -> 6.32 us
  Pallas kernels: 0 us -> 14.2 us
  waiting for transfers between devices: 28.6 us -> 36.4 us
    ppermute x30 -> x8, starting transfers between devices: 161 us -> 31.5 us  [the longest x4 17 us: on_device(): far = lax.ppermute(far, 'dom', far_pairs)]
    all_gather x0 -> x8, blocking collectives: none -> 22.4 us  [the longest x4 14.6 us: on_device(): lax.all_gather(gift, 'dom', axis=0, axis_index_groups=groups, tiled=False)]
    dot_general x8 -> x0, matrix products: 20.9 us -> none  [the longest x4 17.8 us: on_device(): jnp.einsum('ckj,kij->kci', picked, blocks, preferred_element_type=jnp.flo...]
    gather x28 -> x0, local copies, waits for them, and re-layouts: 16.3 us -> none  [the longest x24 13.5 us: on_device(): pieces.append(passed_along(scaled, 'dom', OFFSETS[j])[:, theirs[j]])]
    pallas_call x0 -> x9, Pallas kernels: none -> 14.2 us  [the longest x4 11.3 us: on_device(): pl.pallas_call(functools.partial(step_kernel, last), out_shape=out_shape,...]
    ppermute x30 -> x8, waiting for transfers between devices: 28.6 us -> 36.4 us  [the longest x4 28.2 us: on_device(): far = lax.ppermute(far, 'dom', far_pairs)]
    unnamed x25 -> x20, local copies, waits for them, and re-layouts: 2.24 us -> 6.2 us
  transfers between devices with their start and end apart: 30 -> 8, of which waited for: 11 -> 4; matrix products, arithmetic and copies ran while one was open for 7% -> 1% of each run, Pallas kernels for 0% -> 0%
where the time goes in v1:
time: 113 us
  waiting for transfers between devices  36.4 us (32%)
  starting transfers between devices  31.5 us (28%)
  blocking collectives  22.4 us (20%)
  Pallas kernels  14.2 us (13%)
  local copies, waits for them, and re-layouts  6.32 us (6%)
  other arithmetic  1.63 us (1%)
    ppermute x4, waiting for transfers between devices, on_device(): far = lax.ppermute(far, 'dom', far_pairs)  28.2 us
    ppermute x4, starting transfers between devices, on_device(): far = lax.ppermute(far, 'dom', far_pairs)  17 us
    all_gather x4, blocking collectives, on_device(): lax.all_gather(gift, 'dom', axis=0, axis_index_groups=groups, tiled=False)  14.6 us
    ppermute x4, starting transfers between devices, on_device(): near = lax.ppermute(near, 'dom', near_pairs)  14.6 us
    pallas_call x4, Pallas kernels, on_device(): pl.pallas_call(functools.partial(step_kernel, last), out_shape=out_shape,...  11.3 us
    ppermute x4, waiting for transfers between devices, on_device(): near = lax.ppermute(near, 'dom', near_pairs)  8.16 us
    all_gather x4, blocking collectives, on_device(): lax.all_gather(jnp.concatenate([near[:16], far[:8]]), 'dom', axis=0, axis...  7.79 us
    unnamed x20, local copies, waits for them, and re-layouts  6.2 us
  transfers between devices with their start and end apart: 8, of which 4 were waited for; matrix products, arithmetic and copies ran while one was open for 1% of the time, Pallas kernels for 0%

profile of v1, /device:TPU:1, one launch (start us, length us, event | category | flops | bytes accessed | tf_op | source)
XLA Modules:
  0.0 112.8 jit_solution(10004679557719798833)
XLA Ops:
  3.3 8.6 %all-gather = bf16[64,16,128]{2,1,0:T(8,128)(2,1)S(1)} all-gather(bf16[32,16,128]{2,1,0:T(8,128)(2,1)S(1)} %get-tuple-element.22), channel_id=2, replica_groups={{0,1},{2,3},{4,5},{6,7},{8,9},{10,11},{12,13},{14,15},{16,17},{18,19},{..., dimensions={0}, use_global_device_ids=true | all-gather | bytes 393216 | tf_op jit(solution)/shard_map/all_gather | solution.py:168
  12.6 11.2 %collective-permute-start.1 = (bf16[16,16,128]{2,1,0:T(8,128)(2,1)S(1)}, bf16[16,16,128]{2,1,0:T(8,128)(2,1)S(1)}, u32[]{:S(2)}, u32[]{:S(2)}) collective-permute-start(bf16[16,16,128]{2,1,0:T(8,128)(2,1)S(1)} %get-tuple-element.24), channel_id=1, source_target_pairs={{0,4},{1,509},{2,6},{3,511},{5,9},{4,0},{7,11},{6,2},{8,12},{9,5},... | collective-permute-start | bytes 196616 | tf_op jit(solution)/shard_map/ppermute | solution.py:178
  23.8 1.9 %collective-permute-start = (bf16[24,16,128]{2,1,0:T(8,128)(2,1)S(1)}, bf16[24,16,128]{2,1,0:T(8,128)(2,1)S(1)}, u32[]{:S(2)}, u32[]{:S(2)}) collective-permute-start(bf16[24,16,128]{2,1,0:T(8,128)(2,1)S(1)} %get-tuple-element.23), channel_id=1, source_target_pairs={{0,2},{1,511},{3,5},{2,0},{4,6},{5,3},{7,9},{6,4},{8,10},{9,7},{11... | collective-permute-start | bytes 294920 | tf_op jit(solution)/shard_map/ppermute | solution.py:179
  26.4 8.1 %collective-permute-done.near = bf16[24,16,128]{2,1,0:T(8,128)(2,1)S(1)} collective-permute-done((bf16[24,16,128]{2,1,0:T(8,128)(2,1)S(1)}, bf16[24,16,128]{2,1,0:T(8,128)(2,1)S(1)}, u32[]{:S(2)}, u32[]{:S(2)}) %collective-permute-start) | collective-permute-done | bytes 98336 | tf_op jit(solution)/shard_map/ppermute | solution.py:179
  34.6 1.9 %all-gather.1 = bf16[48,16,128]{2,1,0:T(8,128)(2,1)S(1)} all-gather(bf16[24,16,128]{2,1,0:T(8,128)(2,1)S(1)} %pad_maximum_fusion), channel_id=3, replica_groups={{0,1},{2,3},{4,5},{6,7},{8,9},{10,11},{12,13},{14,15},{16,17},{18,19},{..., dimensions={0}, use_global_device_ids=true | all-gather | bytes 294912 | tf_op jit(solution)/shard_map/all_gather | solution.py:180
  36.5 2.2 %copy-done = bf16[128,128,128]{2,1,0:T(8,128)(2,1)S(1)} copy-done((bf16[128,128,128]{2,1,0:T(8,128)(2,1)S(1)}, bf16[128,128,128]{2,1,0:T(8,128)(2,1)}, u32[]{:S(2)}) %copy-start) | copy-done | bytes 4194328
  41.0 2.7 %step.3 = (bf16[32,16,128]{2,1,0:T(8,128)(2,1)S(1)}, bf16[32,16,128]{2,1,0:T(8,128)(2,1)S(1)}) custom-call(s32[1]{0:T(128)} %bitcast.core, s32[32]{0:T(128)S(1)} %pad_add_fusion.give, s32[128]{0:T(128)S(1)} %compare_select_fusion.5.at, s32[33]{0:T(128)S(1)} %bitcast.61, bf16[32,16,128]{2,1,0:T(8,128)(2,1)S(1)} %get-tuple-element.21.x, ...), custom_call_target="tpu_custom_call" | custom-call | tf_op jit(solution)/shard_map/step/pallas_call | solution.py:185
  43.7 2.0 %all-gather.2 = bf16[64,16,128]{2,1,0:T(8,128)(2,1)S(1)} all-gather(bf16[32,16,128]{2,1,0:T(8,128)(2,1)S(1)} %get-tuple-element.26), channel_id=4, replica_groups={{0,1},{2,3},{4,5},{6,7},{8,9},{10,11},{12,13},{14,15},{16,17},{18,19},{..., dimensions={0}, use_global_device_ids=true | all-gather | bytes 393216 | tf_op jit(solution)/shard_map/all_gather | solution.py:168
  46.3 1.9 %collective-permute-start.2 = (bf16[24,16,128]{2,1,0:T(8,128)(2,1)S(1)}, bf16[24,16,128]{2,1,0:T(8,128)(2,1)S(1)}, u32[]{:S(2)}, u32[]{:S(2)}) collective-permute-start(bf16[24,16,128]{2,1,0:T(8,128)(2,1)S(1)} %get-tuple-element.27), channel_id=1, source_target_pairs={{0,2},{1,511},{3,5},{2,0},{4,6},{5,3},{7,9},{6,4},{8,10},{9,7},{11... | collective-permute-start | bytes 294920 | tf_op jit(solution)/shard_map/ppermute | solution.py:179
  48.2 1.9 %collective-permute-start.3 = (bf16[16,16,128]{2,1,0:T(8,128)(2,1)S(1)}, bf16[16,16,128]{2,1,0:T(8,128)(2,1)S(1)}, u32[]{:S(2)}, u32[]{:S(2)}) collective-permute-start(bf16[16,16,128]{2,1,0:T(8,128)(2,1)S(1)} %get-tuple-element.28), channel_id=1, source_target_pairs={{0,4},{1,509},{2,6},{3,511},{5,9},{4,0},{7,11},{6,2},{8,12},{9,5},... | collective-permute-start | bytes 196616 | tf_op jit(solution)/shard_map/ppermute | solution.py:178
  50.2 9.4 %collective-permute-done.3.far = bf16[16,16,128]{2,1,0:T(8,128)(2,1)S(1)} collective-permute-done((bf16[16,16,128]{2,1,0:T(8,128)(2,1)S(1)}, bf16[16,16,128]{2,1,0:T(8,128)(2,1)S(1)}, u32[]{:S(2)}, u32[]{:S(2)}) %collective-permute-start.3) | collective-permute-done | bytes 65568 | tf_op jit(solution)/shard_map/ppermute | solution.py:178
  59.6 1.9 %all-gather.3 = bf16[48,16,128]{2,1,0:T(8,128)(2,1)S(1)} all-gather(bf16[24,16,128]{2,1,0:T(8,128)(2,1)S(1)} %pad_maximum_fusion.1), channel_id=5, replica_groups={{0,1},{2,3},{4,5},{6,7},{8,9},{10,11},{12,13},{14,15},{16,17},{18,19},{..., dimensions={0}, use_global_device_ids=true | all-gather | bytes 294912 | tf_op jit(solution)/shard_map/all_gather | solution.py:180
  61.6 2.7 %step.4 = (bf16[32,16,128]{2,1,0:T(8,128)(2,1)S(1)}, bf16[32,16,128]{2,1,0:T(8,128)(2,1)S(1)}) custom-call(s32[1]{0:T(128)} %bitcast.core, s32[32]{0:T(128)S(1)} %pad_add_fusion.give, s32[128]{0:T(128)S(1)} %compare_select_fusion.5.at, s32[33]{0:T(128)S(1)} %bitcast.62, bf16[32,16,128]{2,1,0:T(8,128)(2,1)S(1)} %get-tuple-element.25.x, ...), custom_call_target="tpu_custom_call" | custom-call | tf_op jit(solution)/shard_map/step/pallas_call | solution.py:185
  64.2 2.0 %all-gather.4 = bf16[64,16,128]{2,1,0:T(8,128)(2,1)S(1)} all-gather(bf16[32,16,128]{2,1,0:T(8,128)(2,1)S(1)} %get-tuple-element.30), channel_id=6, replica_groups={{0,1},{2,3},{4,5},{6,7},{8,9},{10,11},{12,13},{14,15},{16,17},{18,19},{..., dimensions={0}, use_global_device_ids=true | all-gather | bytes 393216 | tf_op jit(solution)/shard_map/all_gather | solution.py:168
  66.8 8.8 %collective-permute-start.4 = (bf16[24,16,128]{2,1,0:T(8,128)(2,1)S(1)}, bf16[24,16,128]{2,1,0:T(8,128)(2,1)S(1)}, u32[]{:S(2)}, u32[]{:S(2)}) collective-permute-start(bf16[24,16,128]{2,1,0:T(8,128)(2,1)S(1)} %get-tuple-element.31), channel_id=1, source_target_pairs={{0,2},{1,511},{3,5},{2,0},{4,6},{5,3},{7,9},{6,4},{8,10},{9,7},{11... | collective-permute-start | bytes 294920 | tf_op jit(solution)/shard_map/ppermute | solution.py:179
  77.6 9.4 %collective-permute-done.5.far = bf16[16,16,128]{2,1,0:T(8,128)(2,1)S(1)} collective-permute-done((bf16[16,16,128]{2,1,0:T(8,128)(2,1)S(1)}, bf16[16,16,128]{2,1,0:T(8,128)(2,1)S(1)}, u32[]{:S(2)}, u32[]{:S(2)}) %collective-permute-start.5) | collective-permute-done | bytes 65568 | tf_op jit(solution)/shard_map/ppermute | solution.py:178
  87.0 1.9 %all-gather.5 = bf16[48,16,128]{2,1,0:T(8,128)(2,1)S(1)} all-gather(bf16[24,16,128]{2,1,0:T(8,128)(2,1)S(1)} %pad_maximum_fusion.2), channel_id=7, replica_groups={{0,1},{2,3},{4,5},{6,7},{8,9},{10,11},{12,13},{14,15},{16,17},{18,19},{..., dimensions={0}, use_global_device_ids=true | all-gather | bytes 294912 | tf_op jit(solution)/shard_map/all_gather | solution.py:180
  88.9 2.7 %step.5 = (bf16[32,16,128]{2,1,0:T(8,128)(2,1)S(1)}, bf16[32,16,128]{2,1,0:T(8,128)(2,1)S(1)}) custom-call(s32[1]{0:T(128)} %bitcast.core, s32[32]{0:T(128)S(1)} %pad_add_fusion.give, s32[128]{0:T(128)S(1)} %compare_select_fusion.5.at, s32[33]{0:T(128)S(1)} %bitcast.63, bf16[32,16,128]{2,1,0:T(8,128)(2,1)S(1)} %get-tuple-element.29.x, ...), custom_call_target="tpu_custom_call" | custom-call | tf_op jit(solution)/shard_map/step/pallas_call | solution.py:185
  91.6 2.0 %all-gather.6 = bf16[64,16,128]{2,1,0:T(8,128)(2,1)S(1)} all-gather(bf16[32,16,128]{2,1,0:T(8,128)(2,1)S(1)} %get-tuple-element.34), channel_id=8, replica_groups={{0,1},{2,3},{4,5},{6,7},{8,9},{10,11},{12,13},{14,15},{16,17},{18,19},{..., dimensions={0}, use_global_device_ids=true | all-gather | bytes 393216 | tf_op jit(solution)/shard_map/all_gather | solution.py:168
  94.2 1.9 %collective-permute-start.6 = (bf16[24,16,128]{2,1,0:T(8,128)(2,1)S(1)}, bf16[24,16,128]{2,1,0:T(8,128)(2,1)S(1)}, u32[]{:S(2)}, u32[]{:S(2)}) collective-permute-start(bf16[24,16,128]{2,1,0:T(8,128)(2,1)S(1)} %get-tuple-element.35), channel_id=1, source_target_pairs={{0,2},{1,511},{3,5},{2,0},{4,6},{5,3},{7,9},{6,4},{8,10},{9,7},{11... | collective-permute-start | bytes 294920 | tf_op jit(solution)/shard_map/ppermute | solution.py:179
  96.1 1.9 %collective-permute-start.7 = (bf16[16,16,128]{2,1,0:T(8,128)(2,1)S(1)}, bf16[16,16,128]{2,1,0:T(8,128)(2,1)S(1)}, u32[]{:S(2)}, u32[]{:S(2)}) collective-permute-start(bf16[16,16,128]{2,1,0:T(8,128)(2,1)S(1)} %get-tuple-element.36), channel_id=1, source_target_pairs={{0,4},{1,509},{2,6},{3,511},{5,9},{4,0},{7,11},{6,2},{8,12},{9,5},... | collective-permute-start | bytes 196616 | tf_op jit(solution)/shard_map/ppermute | solution.py:178
  98.1 9.4 %collective-permute-done.7.far = bf16[16,16,128]{2,1,0:T(8,128)(2,1)S(1)} collective-permute-done((bf16[16,16,128]{2,1,0:T(8,128)(2,1)S(1)}, bf16[16,16,128]{2,1,0:T(8,128)(2,1)S(1)}, u32[]{:S(2)}, u32[]{:S(2)}) %collective-permute-start.7) | collective-permute-done | bytes 65568 | tf_op jit(solution)/shard_map/ppermute | solution.py:178
  107.5 1.9 %all-gather.7 = bf16[48,16,128]{2,1,0:T(8,128)(2,1)S(1)} all-gather(bf16[24,16,128]{2,1,0:T(8,128)(2,1)S(1)} %pad_maximum_fusion.3), channel_id=9, replica_groups={{0,1},{2,3},{4,5},{6,7},{8,9},{10,11},{12,13},{14,15},{16,17},{18,19},{..., dimensions={0}, use_global_device_ids=true | all-gather | bytes 294912 | tf_op jit(solution)/shard_map/all_gather | solution.py:180
  109.4 3.3 %last.1 = f32[16,4096]{1,0:T(8,128)} custom-call(s32[1]{0:T(128)} %bitcast.core, s32[32]{0:T(128)S(1)} %pad_add_fusion.give, s32[128]{0:T(128)S(1)} %compare_select_fusion.5.at, s32[33]{0:T(128)S(1)} %bitcast.64, bf16[32,16,128]{2,1,0:T(8,128)(2,1)S(1)} %get-tuple-element.33.x, bf16[2,32,16,128]{3,2,1,0:T(8,128)(2,1)S(1)} %bitcast.47, ...), custom_call_target="tpu_custom_call" | custom-call | tf_op jit(solution)/shard_map/last/pallas_call | solution.py:185
  (53 shorter events, 10.6 us)
Async XLA Ops:
  1.0 1.0 copy-start.2
  1.9 0.7 copy-start.5
  3.2 58.3 %copy-start.4 = (f32[16,4096]{1,0:T(8,128)S(1)}, f32[16,4096]{1,0:T(8,128)}, u32[]{:S(2)}) copy-start(f32[16,4096]{1,0:T(8,128)} %seeds.9) | copy-start | bytes 786436
  3.2 58.3 %copy-start.7 = (f32[4096]{0:T(1024)S(1)}, f32[4096]{0:T(1024)}, u32[]{:S(2)}) copy-start(f32[4096]{0:T(1024)} %param.10) | copy-start | bytes 49156
  3.2 58.3 %copy-start.9 = (s32[1,33]{1,0:T(1,128)S(1)}, s32[1,33]{1,0:T(1,128)}, u32[]{:S(2)}) copy-start(s32[1,33]{1,0:T(1,128)} %param.8) | copy-start | bytes 400
  12.6 13.8 %collective-permute-start.1 = (bf16[16,16,128]{2,1,0:T(8,128)(2,1)S(1)}, bf16[16,16,128]{2,1,0:T(8,128)(2,1)S(1)}, u32[]{:S(2)}, u32[]{:S(2)}) collective-permute-start(bf16[16,16,128]{2,1,0:T(8,128)(2,1)S(1)} %get-tuple-element.24), channel_id=1, source_target_pairs={{0,4},{1,509},{2,6},{3,511},{5,9},{4,0},{7,11},{6,2},{8,12},{9,5},... | collective-permute-start | bytes 196616 | tf_op jit(solution)/shard_map/ppermute | solution.py:178
  23.8 10.8 %collective-permute-start = (bf16[24,16,128]{2,1,0:T(8,128)(2,1)S(1)}, bf16[24,16,128]{2,1,0:T(8,128)(2,1)S(1)}, u32[]{:S(2)}, u32[]{:S(2)}) collective-permute-start(bf16[24,16,128]{2,1,0:T(8,128)(2,1)S(1)} %get-tuple-element.23), channel_id=1, source_target_pairs={{0,2},{1,511},{3,5},{2,0},{4,6},{5,3},{7,9},{6,4},{8,10},{9,7},{11... | collective-permute-start | bytes 294920 | tf_op jit(solution)/shard_map/ppermute | solution.py:179
  36.5 2.2 %copy-start = (bf16[128,128,128]{2,1,0:T(8,128)(2,1)S(1)}, bf16[128,128,128]{2,1,0:T(8,128)(2,1)}, u32[]{:S(2)}) copy-start(bf16[128,128,128]{2,1,0:T(8,128)(2,1)} %blocks.7) | copy-start | bytes 12582916
  38.7 0.9 copy-start.3
  39.7 0.7 copy-start.6
  40.4 0.7 copy-start.8
  41.0 20.5 %copy-start.1 = (bf16[128,128,128]{2,1,0:T(8,128)(2,1)S(1)}, bf16[128,128,128]{2,1,0:T(8,128)(2,1)}, u32[]{:S(2)}) copy-start(bf16[128,128,128]{2,1,0:T(8,128)(2,1)} %blocks.7) | copy-start | bytes 12582916
  46.3 13.3 %collective-permute-start.2 = (bf16[24,16,128]{2,1,0:T(8,128)(2,1)S(1)}, bf16[24,16,128]{2,1,0:T(8,128)(2,1)S(1)}, u32[]{:S(2)}, u32[]{:S(2)}) collective-permute-start(bf16[24,16,128]{2,1,0:T(8,128)(2,1)S(1)} %get-tuple-element.27), channel_id=1, source_target_pairs={{0,2},{1,511},{3,5},{2,0},{4,6},{5,3},{7,9},{6,4},{8,10},{9,7},{11... | collective-permute-start | bytes 294920 | tf_op jit(solution)/shard_map/ppermute | solution.py:179
  48.2 11.3 %collective-permute-start.3 = (bf16[16,16,128]{2,1,0:T(8,128)(2,1)S(1)}, bf16[16,16,128]{2,1,0:T(8,128)(2,1)S(1)}, u32[]{:S(2)}, u32[]{:S(2)}) collective-permute-start(bf16[16,16,128]{2,1,0:T(8,128)(2,1)S(1)} %get-tuple-element.28), channel_id=1, source_target_pairs={{0,4},{1,509},{2,6},{3,511},{5,9},{4,0},{7,11},{6,2},{8,12},{9,5},... | collective-permute-start | bytes 196616 | tf_op jit(solution)/shard_map/ppermute | solution.py:178
  66.8 20.1 %collective-permute-start.4 = (bf16[24,16,128]{2,1,0:T(8,128)(2,1)S(1)}, bf16[24,16,128]{2,1,0:T(8,128)(2,1)S(1)}, u32[]{:S(2)}, u32[]{:S(2)}) collective-permute-start(bf16[24,16,128]{2,1,0:T(8,128)(2,1)S(1)} %get-tuple-element.31), channel_id=1, source_target_pairs={{0,2},{1,511},{3,5},{2,0},{4,6},{5,3},{7,9},{6,4},{8,10},{9,7},{11... | collective-permute-start | bytes 294920 | tf_op jit(solution)/shard_map/ppermute | solution.py:179
  75.6 11.3 %collective-permute-start.5 = (bf16[16,16,128]{2,1,0:T(8,128)(2,1)S(1)}, bf16[16,16,128]{2,1,0:T(8,128)(2,1)S(1)}, u32[]{:S(2)}, u32[]{:S(2)}) collective-permute-start(bf16[16,16,128]{2,1,0:T(8,128)(2,1)S(1)} %get-tuple-element.32), channel_id=1, source_target_pairs={{0,4},{1,509},{2,6},{3,511},{5,9},{4,0},{7,11},{6,2},{8,12},{9,5},... | collective-permute-start | bytes 196616 | tf_op jit(solution)/shard_map/ppermute | solution.py:178
  94.2 13.3 %collective-permute-start.6 = (bf16[24,16,128]{2,1,0:T(8,128)(2,1)S(1)}, bf16[24,16,128]{2,1,0:T(8,128)(2,1)S(1)}, u32[]{:S(2)}, u32[]{:S(2)}) collective-permute-start(bf16[24,16,128]{2,1,0:T(8,128)(2,1)S(1)} %get-tuple-element.35), channel_id=1, source_target_pairs={{0,2},{1,511},{3,5},{2,0},{4,6},{5,3},{7,9},{6,4},{8,10},{9,7},{11... | collective-permute-start | bytes 294920 | tf_op jit(solution)/shard_map/ppermute | solution.py:179
  96.1 11.3 %collective-permute-start.7 = (bf16[16,16,128]{2,1,0:T(8,128)(2,1)S(1)}, bf16[16,16,128]{2,1,0:T(8,128)(2,1)S(1)}, u32[]{:S(2)}, u32[]{:S(2)}) collective-permute-start(bf16[16,16,128]{2,1,0:T(8,128)(2,1)S(1)} %get-tuple-element.36), channel_id=1, source_target_pairs={{0,4},{1,509},{2,6},{3,511},{5,9},{4,0},{7,11},{6,2},{8,12},{9,5},... | collective-permute-start | bytes 196616 | tf_op jit(solution)/shard_map/ppermute | solution.py:178

commit v2 on v0

v2 whole, which is shorter than its diff:
```python
import functools

import jax
import jax.numpy as jnp
from jax import lax
from jax.experimental import pallas as pl
from jax.experimental.pallas import tpu as pltpu
from jax.sharding import PartitionSpec as P

ITERS = 4
ALPHA = 0.8
RB, C, BLK, HB = 32, 16, 128, 8


SMEM = pl.BlockSpec(memory_space=pltpu.SMEM)
VMEM = pl.BlockSpec(memory_space=pltpu.VMEM)
ANY = pl.BlockSpec(memory_space=pl.ANY)
HBM = pl.BlockSpec(memory_space=pltpu.HBM)


def bf16(*shape):
    return jax.ShapeDtypeStruct(shape, jnp.bfloat16)


def f32(*shape):
    return jax.ShapeDtypeStruct(shape, jnp.float32)


def role():
    me = lax.axis_index("dom")
    k = me & 1
    chip = me >> 1
    return k, ((chip ^ k) & 1) == 0, (((chip >> 1) ^ k) & 1) == 0


def units():
    k, up1, up2 = role()
    sel = jnp.where
    first = k == 0
    mine = [
        sel(first & ~up1, 1, -1),
        sel(up1, sel(first, 2, 0), -1),
        sel(first & up1, -1, sel(up1, 2, 3)),
        sel(up2, 4, 5),
    ]
    gift = [
        sel(first, sel(up1, 3, 2), sel(up1, -1, 2)),
        sel(first, sel(up1, 1, -1), sel(up1, 3, -1)),
        sel(first | up1, -1, 0),
        sel(up2, 5, 4),
        k,
    ]
    return mine, gift


def pack(lists, x, mine_out, gift_out):
    for out, which in zip((mine_out, gift_out), units()):
        for at, unit in enumerate(which):
            for h in range(HB):
                block = jnp.where(unit < 0, RB, lists[jnp.maximum(unit, 0), 0, h])
                out[at * HB + h] = x[block]


def first_kernel(lists_any, seeds_any, scale_any, x_out, mine_out, gift_out, base_out, scale_out, lists, seeds, x, sems):
    copies = [
        pltpu.make_async_copy(lists_any, lists, sems.at[0]),
        pltpu.make_async_copy(seeds_any, seeds, sems.at[1]),
        pltpu.make_async_copy(scale_any, scale_out, sems.at[2]),
    ]
    for copy in copies:
        copy.start()
    for copy in copies[::-1]:
        copy.wait()
    for r in range(RB):
        field = seeds[:, r * BLK : (r + 1) * BLK]
        base_out[r] = (1.0 - ALPHA) * field
        x[r] = (field * scale_out[r : r + 1, :]).astype(jnp.bfloat16)
    x[RB] = jnp.zeros((C, BLK), jnp.bfloat16)
    x_out[...] = x[0:RB]
    pack(lists, x, mine_out, gift_out)


def merge_kernel(mine, chip, near, far, direct):
    sib = chip.at[1 - role()[0]]
    near[...] = mine[0:24] + sib[0:24]
    far[0:8] = sib[24:32]
    far[8:16] = mine[24:32]
    direct[...] = sib[32:40]


def arrange_kernel(offsets, blocks, out):
    def row(r, carry):
        for s in range(4):
            slot = jnp.minimum(offsets[0, r] + s, BLK - 1)
            out[r, s * BLK : (s + 1) * BLK, :] = blocks[slot].T
        return carry

    lax.fori_loop(0, RB, row, 0)


def early_kernel(index, x, direct, blocks, acc, src):
    src[0:RB] = x[...]
    src[RB : RB + HB] = direct[...]
    src[RB + HB] = jnp.zeros((C, BLK), jnp.bfloat16)
    for r in range(RB):
        lhs = jnp.concatenate([src[index[r, s]] for s in range(4)], axis=1)
        acc[r] = jnp.dot(lhs, blocks[r], preferred_element_type=jnp.float32)


def late_kernel(last, index, lists_any, near, far, side, acc, base, scale, blocks, *rest):
    if last:
        out, src = rest
    else:
        x_out, mine_out, gift_out, src, x, lists, sem = rest
        copy = pltpu.make_async_copy(lists_any, lists, sem)
        copy.start()
    src[0:24] = near[...]
    src[24:40] = far[...]
    src[40:64] = side[1 - role()[0]]
    src[64] = jnp.zeros((C, BLK), jnp.bfloat16)
    at = [index[s : s + 1, :] for s in range(3)]
    for r in range(RB):
        lhs = jnp.concatenate([src[at[s][0, r]] for s in range(3)], axis=1)
        total = acc[r] + jnp.dot(lhs, blocks[r, BLK:, :], preferred_element_type=jnp.float32)
        s = scale[r : r + 1, :]
        field = ALPHA * s * total + base[r]
        if last:
            out[:, r * BLK : (r + 1) * BLK] = field
        else:
            x[r] = (field * s).astype(jnp.bfloat16)
    if not last:
        x[RB] = jnp.zeros((C, BLK), jnp.bfloat16)
        x_out[...] = x[0:RB]
        copy.wait()
        pack(lists, x, mine_out, gift_out)


def indices(columns, offsets):
    k, up1, up2 = role()
    sel = jnp.where
    first = k == 0
    base = [
        sel(first, sel(up1, 48, 16), -1),
        sel(first, -1, sel(up1, 8, 40)),
        sel(up1, 40, sel(first, 8, 16)),
        sel(up1, 16, sel(first, 40, 48)),
        sel(up2, 56, 32),
        sel(up2, 32, 56),
    ]
    inner = (columns - RB) & (HB - 1)
    own, got = columns, jnp.full_like(columns, 64)
    for j in range(6):
        here = (columns - RB) >> 3 == j
        own = sel(here, sel(base[j] < 0, RB + inner, RB + HB), own)
        got = sel(here & (base[j] >= 0), base[j] + inner, got)
    slots = jnp.arange(BLK, dtype=jnp.int32)
    start, end = offsets[:RB], offsets[1:]
    at = start[:, None] + jnp.arange(4, dtype=jnp.int32)[None, :]
    pick = (at[:, :, None] == slots) & (at < end[:, None])[:, :, None]
    own4 = jnp.sum(sel(pick, own - (RB + HB), 0), axis=2) + (RB + HB)
    got4 = jnp.sum(sel(pick, got - 64, 0), axis=2) + 64
    return own4.astype(jnp.int32), got4[:, 1:].T.astype(jnp.int32)


def on_device(count, blocks, col_index, row_offsets, send_index, deg_scale, seeds):
    groups = [[2 * c, 2 * c + 1] for c in range(count // 2)]

    def matching(step):
        chips = count // 2
        pairs = []
        for c in range(chips):
            k = (c // step) % 2
            for core, other in ((k, c + step), (1 - k, c - step)):
                pairs.append((2 * c + core, 2 * (other % chips) + core))
        return pairs

    def gather(value):
        return lax.all_gather(value, "dom", axis=0, axis_index_groups=groups, tiled=False)

    params = pltpu.CompilerParams(vmem_limit_bytes=16 << 20)
    call = functools.partial(pl.pallas_call, compiler_params=params)
    lists = jnp.transpose(send_index, (1, 0, 2))
    score = (C, BLK)

    x, mine, gift, base, scale = call(
        first_kernel,
        out_shape=(bf16(RB, *score), bf16(32, *score), bf16(40, *score), f32(RB, *score), f32(RB, BLK)),
        in_specs=[HBM] * 3,
        out_specs=(VMEM,) * 5,
        scratch_shapes=[
            pltpu.SMEM(lists.shape, jnp.int32),
            pltpu.VMEM(seeds.shape, jnp.float32),
            pltpu.VMEM((RB + 1, *score), jnp.bfloat16),
            pltpu.SemaphoreType.DMA((3,)),
        ],
        name="first",
    )(lists, seeds, deg_scale.reshape(RB, BLK))
    own_index, got_index = indices(col_index[0], row_offsets[0])
    arranged = None
    for step in range(ITERS):
        chip = gather(gift)
        near, far, direct = call(
            merge_kernel,
            out_shape=(bf16(24, *score), bf16(16, *score), bf16(HB, *score)),
            in_specs=[VMEM] * 2,
            out_specs=(VMEM,) * 3,
            name="merge",
        )(mine, chip)
        far = lax.ppermute(far, "dom", matching(2))
        near = lax.ppermute(near, "dom", matching(1))
        if arranged is None:
            arranged = call(
                arrange_kernel,
                out_shape=bf16(RB, 4 * BLK, BLK),
                in_specs=[SMEM, VMEM],
                out_specs=VMEM,
                cost_estimate=pl.CostEstimate(flops=0, bytes_accessed=16 << 20, transcendentals=0),
                name="arrange",
            )(row_offsets, blocks)
        acc = call(
            early_kernel,
            out_shape=f32(RB, *score),
            in_specs=[SMEM] + [VMEM] * 3,
            out_specs=VMEM,
            scratch_shapes=[pltpu.VMEM((RB + HB + 1, *score), jnp.bfloat16)],
            cost_estimate=pl.CostEstimate(flops=1 << 30, bytes_accessed=8 << 20, transcendentals=0),
            name="early",
        )(own_index, x, direct, arranged)
        side = gather(jnp.concatenate([near[:16], far[:8]]))
        last = step == ITERS - 1
        scratch = [pltpu.VMEM((65, *score), jnp.bfloat16)]
        if not last:
            scratch += [
                pltpu.VMEM((RB + 1, *score), jnp.bfloat16),
                pltpu.SMEM(lists.shape, jnp.int32),
                pltpu.SemaphoreType.DMA,
            ]
        result = call(
            functools.partial(late_kernel, last),
            out_shape=f32(*seeds.shape) if last else (bf16(RB, *score), bf16(32, *score), bf16(40, *score)),
            in_specs=[VMEM, ANY] + [VMEM] * 7,
            out_specs=VMEM if last else (VMEM,) * 3,
            scratch_shapes=scratch,
            name="last" if last else "late",
        )(got_index, lists, near, far, side, acc, base, scale, arranged)
        if not last:
            x, mine, gift = result
    return result


def solution(mesh):
    in_specs = (
        P("dom", None, None),
        P("dom", None),
        P("dom", None),
        P("dom", None, None),
        P("dom"),
        P(None, "dom"),
    )
    out_specs = P(None, "dom")
    return jax.shard_map(
        functools.partial(on_device, mesh.size), mesh=mesh, in_specs=in_specs, out_specs=out_specs, check_vma=False
    )
```

time: 239 us -> 98.2 us (0.41); the launches traced: 235 us -> 97.6 us
  starting transfers between devices: 161 us -> 44.4 us
  blocking collectives: 0 us -> 22.5 us
  waiting for transfers between devices: 28.6 us -> 7.48 us
  matrix products: 20.9 us -> 0 us
  Pallas kernels: 0 us -> 15.8 us
  local copies, waits for them, and re-layouts: 21.8 us -> 6.15 us
    ppermute x30 -> x8, starting transfers between devices: 161 us -> 44.4 us  [the longest x4 22.5 us: on_device(): near = lax.ppermute(near, 'dom', matching(1))]
    all_gather x0 -> x8, blocking collectives: none -> 22.5 us  [gather(): lax.all_gather(value, 'dom', axis=0, axis_index_groups=groups, tiled=False)]
    ppermute x30 -> x8, waiting for transfers between devices: 28.6 us -> 7.48 us  [the longest x4 7.3 us: on_device(): near = lax.ppermute(near, 'dom', matching(1))]
    dot_general x8 -> x0, matrix products: 20.9 us -> none  [the longest x4 17.8 us: on_device(): jnp.einsum('ckj,kij->kci', picked, blocks, preferred_element_type=jnp.flo...]
    gather x28 -> x0, local copies, waits for them, and re-layouts: 16.3 us -> none  [the longest x24 13.5 us: on_device(): pieces.append(passed_along(scaled, 'dom', OFFSETS[j])[:, theirs[j]])]
    pallas_call x0 -> x14, Pallas kernels: none -> 15.8 us  [the longest x4 5.87 us: on_device(): call(early_kernel, out_shape=f32(RB, *score), in_specs=[SMEM] + [VMEM] *...]
    unnamed x25 -> x12, local copies, waits for them, and re-layouts: 2.24 us -> 5.2 us
  transfers between devices with their start and end apart: 30 -> 8, of which waited for: 11 -> 4; matrix products, arithmetic and copies ran while one was open for 7% -> 2% of each run, Pallas kernels for 0% -> 10%
where the time goes in v2:
time: 98.2 us; the launch traced here: 97.6 us
  starting transfers between devices  44.4 us (45%)
  blocking collectives  22.5 us (23%)
  Pallas kernels  15.8 us (16%)
  waiting for transfers between devices  7.48 us (8%)
  local copies, waits for them, and re-layouts  6.15 us (6%)
  other arithmetic  1.05 us (1%)
    ppermute x4, starting transfers between devices, on_device(): near = lax.ppermute(near, 'dom', matching(1))  22.5 us
    all_gather x8, blocking collectives, gather(): lax.all_gather(value, 'dom', axis=0, axis_index_groups=groups, tiled=False)  22.5 us
    ppermute x4, starting transfers between devices, on_device(): far = lax.ppermute(far, 'dom', matching(2))  22 us
    ppermute x4, waiting for transfers between devices, on_device(): near = lax.ppermute(near, 'dom', matching(1))  7.3 us
    pallas_call x4, Pallas kernels, on_device(): call(early_kernel, out_shape=f32(RB, *score), in_specs=[SMEM] + [VMEM] *...  5.87 us
    pallas_call x4, Pallas kernels, on_device(): call(functools.partial(late_kernel, last), out_shape=f32(*seeds.shape) if...  5.63 us
    unnamed x12, local copies, waits for them, and re-layouts  5.2 us
    pallas_call x1, Pallas kernels, on_device(): call(arrange_kernel, out_shape=bf16(RB, 4 * BLK, BLK), in_specs=[SMEM, VM...  3.42 us
  transfers between devices with their start and end apart: 8, of which 4 were waited for; matrix products, arithmetic and copies ran while one was open for 2% of the time, Pallas kernels for 10%

profile of v2, /device:TPU:1, one launch (start us, length us, event | category | flops | bytes accessed | tf_op | source)
XLA Modules:
  0.0 97.6 jit_solution(1464160977362508761)
XLA Ops:
  3.1 8.6 %all-gather = bf16[80,16,128]{2,1,0:T(8,128)(2,1)S(1)} all-gather(bf16[40,16,128]{2,1,0:T(8,128)(2,1)S(1)} %get-tuple-element.32), channel_id=2, replica_groups={{0,1},{2,3},{4,5},{6,7},{8,9},{10,11},{12,13},{14,15},{16,17},{18,19},{..., dimensions={0}, use_global_device_ids=true | all-gather | bytes 491520 | tf_op jit(solution)/shard_map/all_gather | solution.py:178
  11.7 11.2 %collective-permute-start.1 = (bf16[16,16,128]{2,1,0:T(8,128)(2,1)S(1)}, bf16[16,16,128]{2,1,0:T(8,128)(2,1)S(1)}, u32[]{:S(2)}, u32[]{:S(2)}) collective-permute-start(bf16[16,16,128]{2,1,0:T(8,128)(2,1)S(1)} %get-tuple-element.34), channel_id=1, source_target_pairs={{0,4},{1,509},{2,6},{3,511},{5,9},{4,0},{7,11},{6,2},{8,12},{9,5},... | collective-permute-start | bytes 196616 | tf_op jit(solution)/shard_map/ppermute | solution.py:209
  22.9 1.9 %collective-permute-start = (bf16[24,16,128]{2,1,0:T(8,128)(2,1)S(1)}, bf16[24,16,128]{2,1,0:T(8,128)(2,1)S(1)}, u32[]{:S(2)}, u32[]{:S(2)}) collective-permute-start(bf16[24,16,128]{2,1,0:T(8,128)(2,1)S(1)} %get-tuple-element.33), channel_id=1, source_target_pairs={{0,2},{1,511},{3,5},{2,0},{4,6},{5,3},{7,9},{6,4},{8,10},{9,7},{11... | collective-permute-start | bytes 294920 | tf_op jit(solution)/shard_map/ppermute | solution.py:210
  26.8 2.2 %copy-done = bf16[128,128,128]{2,1,0:T(8,128)(2,1)S(1)} copy-done((bf16[128,128,128]{2,1,0:T(8,128)(2,1)S(1)}, bf16[128,128,128]{2,1,0:T(8,128)(2,1)}, u32[]{:S(2)}) %copy-start) | copy-done | bytes 4194328
  29.6 3.4 %arrange.1.blocks = bf16[32,512,128]{2,1,0:T(8,128)(2,1)S(1)} custom-call(s32[1,33]{1,0:T(1,128)S(1)} %copy-done.5, bf16[128,128,128]{2,1,0:T(8,128)(2,1)S(1)} %copy-done), custom_call_target="tpu_custom_call" | custom-call | bytes 16777216 | tf_op jit(solution)/shard_map/arrange/pallas_call | solution.py:212
  33.0 1.5 %early.4.acc = f32[32,16,128]{2,1,0:T(8,128)S(1)} custom-call(s32[32,4]{1,0:T(8,128)S(1)} %broadcast_add_fusion.index, bf16[32,16,128]{2,1,0:T(8,128)(2,1)S(1)} %get-tuple-element.35.x, bf16[8,16,128]{2,1,0:T(8,128)(2,1)S(1)} %get-tuple-element.36.direct, bf16[32,512,128]{2,1,0:T(8,128)(2,1)S(1)} %arrange.1.blocks), custom_call_target="tpu_custom_call" | custom-call | flops 1073741824 | bytes 8388608 | tf_op jit(solution)/shard_map/early/pallas_call | solution.py:220
  34.6 1.9 %all-gather.1 = bf16[48,16,128]{2,1,0:T(8,128)(2,1)S(1)} all-gather(bf16[24,16,128]{2,1,0:T(8,128)(2,1)S(1)} %pad_maximum_fusion), channel_id=3, replica_groups={{0,1},{2,3},{4,5},{6,7},{8,9},{10,11},{12,13},{14,15},{16,17},{18,19},{..., dimensions={0}, use_global_device_ids=true | all-gather | bytes 294912 | tf_op jit(solution)/shard_map/all_gather | solution.py:178
  37.9 2.0 %all-gather.2 = bf16[80,16,128]{2,1,0:T(8,128)(2,1)S(1)} all-gather(bf16[40,16,128]{2,1,0:T(8,128)(2,1)S(1)} %get-tuple-element.40), channel_id=4, replica_groups={{0,1},{2,3},{4,5},{6,7},{8,9},{10,11},{12,13},{14,15},{16,17},{18,19},{..., dimensions={0}, use_global_device_ids=true | all-gather | bytes 491520 | tf_op jit(solution)/shard_map/all_gather | solution.py:178
  40.0 4.7 %collective-permute-start.3 = (bf16[16,16,128]{2,1,0:T(8,128)(2,1)S(1)}, bf16[16,16,128]{2,1,0:T(8,128)(2,1)S(1)}, u32[]{:S(2)}, u32[]{:S(2)}) collective-permute-start(bf16[16,16,128]{2,1,0:T(8,128)(2,1)S(1)} %get-tuple-element.42), channel_id=1, source_target_pairs={{0,4},{1,509},{2,6},{3,511},{5,9},{4,0},{7,11},{6,2},{8,12},{9,5},... | collective-permute-start | bytes 196616 | tf_op jit(solution)/shard_map/ppermute | solution.py:209
  44.7 6.1 %collective-permute-start.2 = (bf16[24,16,128]{2,1,0:T(8,128)(2,1)S(1)}, bf16[24,16,128]{2,1,0:T(8,128)(2,1)S(1)}, u32[]{:S(2)}, u32[]{:S(2)}) collective-permute-start(bf16[24,16,128]{2,1,0:T(8,128)(2,1)S(1)} %get-tuple-element.41), channel_id=1, source_target_pairs={{0,2},{1,511},{3,5},{2,0},{4,6},{5,3},{7,9},{6,4},{8,10},{9,7},{11... | collective-permute-start | bytes 294920 | tf_op jit(solution)/shard_map/ppermute | solution.py:210
  50.8 1.5 %early.5.acc = f32[32,16,128]{2,1,0:T(8,128)S(1)} custom-call(s32[32,4]{1,0:T(8,128)S(1)} %broadcast_add_fusion.index, bf16[32,16,128]{2,1,0:T(8,128)(2,1)S(1)} %get-tuple-element.43.x, bf16[8,16,128]{2,1,0:T(8,128)(2,1)S(1)} %get-tuple-element.44.direct, bf16[32,512,128]{2,1,0:T(8,128)(2,1)S(1)} %arrange.1.blocks), custom_call_target="tpu_custom_call" | custom-call | flops 1073741824 | bytes 8388608 | tf_op jit(solution)/shard_map/early/pallas_call | solution.py:220
  52.3 3.2 %collective-permute-done.2.near = bf16[24,16,128]{2,1,0:T(8,128)(2,1)S(1)} collective-permute-done((bf16[24,16,128]{2,1,0:T(8,128)(2,1)S(1)}, bf16[24,16,128]{2,1,0:T(8,128)(2,1)S(1)}, u32[]{:S(2)}, u32[]{:S(2)}) %collective-permute-start.2) | collective-permute-done | bytes 98336 | tf_op jit(solution)/shard_map/ppermute | solution.py:210
  55.5 1.9 %all-gather.3 = bf16[48,16,128]{2,1,0:T(8,128)(2,1)S(1)} all-gather(bf16[24,16,128]{2,1,0:T(8,128)(2,1)S(1)} %pad_maximum_fusion.1), channel_id=5, replica_groups={{0,1},{2,3},{4,5},{6,7},{8,9},{10,11},{12,13},{14,15},{16,17},{18,19},{..., dimensions={0}, use_global_device_ids=true | all-gather | bytes 294912 | tf_op jit(solution)/shard_map/all_gather | solution.py:178
  58.8 2.0 %all-gather.4 = bf16[80,16,128]{2,1,0:T(8,128)(2,1)S(1)} all-gather(bf16[40,16,128]{2,1,0:T(8,128)(2,1)S(1)} %get-tuple-element.46), channel_id=6, replica_groups={{0,1},{2,3},{4,5},{6,7},{8,9},{10,11},{12,13},{14,15},{16,17},{18,19},{..., dimensions={0}, use_global_device_ids=true | all-gather | bytes 491520 | tf_op jit(solution)/shard_map/all_gather | solution.py:178
  60.9 1.9 %collective-permute-start.5 = (bf16[16,16,128]{2,1,0:T(8,128)(2,1)S(1)}, bf16[16,16,128]{2,1,0:T(8,128)(2,1)S(1)}, u32[]{:S(2)}, u32[]{:S(2)}) collective-permute-start(bf16[16,16,128]{2,1,0:T(8,128)(2,1)S(1)} %get-tuple-element.48), channel_id=1, source_target_pairs={{0,4},{1,509},{2,6},{3,511},{5,9},{4,0},{7,11},{6,2},{8,12},{9,5},... | collective-permute-start | bytes 196616 | tf_op jit(solution)/shard_map/ppermute | solution.py:209
  62.8 8.3 %collective-permute-start.4 = (bf16[24,16,128]{2,1,0:T(8,128)(2,1)S(1)}, bf16[24,16,128]{2,1,0:T(8,128)(2,1)S(1)}, u32[]{:S(2)}, u32[]{:S(2)}) collective-permute-start(bf16[24,16,128]{2,1,0:T(8,128)(2,1)S(1)} %get-tuple-element.47), channel_id=1, source_target_pairs={{0,2},{1,511},{3,5},{2,0},{4,6},{5,3},{7,9},{6,4},{8,10},{9,7},{11... | collective-permute-start | bytes 294920 | tf_op jit(solution)/shard_map/ppermute | solution.py:210
  71.2 1.5 %early.6.acc = f32[32,16,128]{2,1,0:T(8,128)S(1)} custom-call(s32[32,4]{1,0:T(8,128)S(1)} %broadcast_add_fusion.index, bf16[32,16,128]{2,1,0:T(8,128)(2,1)S(1)} %get-tuple-element.49.x, bf16[8,16,128]{2,1,0:T(8,128)(2,1)S(1)} %get-tuple-element.50.direct, bf16[32,512,128]{2,1,0:T(8,128)(2,1)S(1)} %arrange.1.blocks), custom_call_target="tpu_custom_call" | custom-call | flops 1073741824 | bytes 8388608 | tf_op jit(solution)/shard_map/early/pallas_call | solution.py:220
  73.8 1.9 %all-gather.5 = bf16[48,16,128]{2,1,0:T(8,128)(2,1)S(1)} all-gather(bf16[24,16,128]{2,1,0:T(8,128)(2,1)S(1)} %pad_maximum_fusion.2), channel_id=7, replica_groups={{0,1},{2,3},{4,5},{6,7},{8,9},{10,11},{12,13},{14,15},{16,17},{18,19},{..., dimensions={0}, use_global_device_ids=true | all-gather | bytes 294912 | tf_op jit(solution)/shard_map/all_gather | solution.py:178
  77.1 2.0 %all-gather.6 = bf16[80,16,128]{2,1,0:T(8,128)(2,1)S(1)} all-gather(bf16[40,16,128]{2,1,0:T(8,128)(2,1)S(1)} %get-tuple-element.52), channel_id=8, replica_groups={{0,1},{2,3},{4,5},{6,7},{8,9},{10,11},{12,13},{14,15},{16,17},{18,19},{..., dimensions={0}, use_global_device_ids=true | all-gather | bytes 491520 | tf_op jit(solution)/shard_map/all_gather | solution.py:178
  79.2 4.1 %collective-permute-start.7 = (bf16[16,16,128]{2,1,0:T(8,128)(2,1)S(1)}, bf16[16,16,128]{2,1,0:T(8,128)(2,1)S(1)}, u32[]{:S(2)}, u32[]{:S(2)}) collective-permute-start(bf16[16,16,128]{2,1,0:T(8,128)(2,1)S(1)} %get-tuple-element.54), channel_id=1, source_target_pairs={{0,4},{1,509},{2,6},{3,511},{5,9},{4,0},{7,11},{6,2},{8,12},{9,5},... | collective-permute-start | bytes 196616 | tf_op jit(solution)/shard_map/ppermute | solution.py:209
  83.3 6.1 %collective-permute-start.6 = (bf16[24,16,128]{2,1,0:T(8,128)(2,1)S(1)}, bf16[24,16,128]{2,1,0:T(8,128)(2,1)S(1)}, u32[]{:S(2)}, u32[]{:S(2)}) collective-permute-start(bf16[24,16,128]{2,1,0:T(8,128)(2,1)S(1)} %get-tuple-element.53), channel_id=1, source_target_pairs={{0,2},{1,511},{3,5},{2,0},{4,6},{5,3},{7,9},{6,4},{8,10},{9,7},{11... | collective-permute-start | bytes 294920 | tf_op jit(solution)/shard_map/ppermute | solution.py:210
  90.9 3.2 %collective-permute-done.6.near = bf16[24,16,128]{2,1,0:T(8,128)(2,1)S(1)} collective-permute-done((bf16[24,16,128]{2,1,0:T(8,128)(2,1)S(1)}, bf16[24,16,128]{2,1,0:T(8,128)(2,1)S(1)}, u32[]{:S(2)}, u32[]{:S(2)}) %collective-permute-start.6) | collective-permute-done | bytes 98336 | tf_op jit(solution)/shard_map/ppermute | solution.py:210
  94.1 1.9 %all-gather.7 = bf16[48,16,128]{2,1,0:T(8,128)(2,1)S(1)} all-gather(bf16[24,16,128]{2,1,0:T(8,128)(2,1)S(1)} %pad_maximum_fusion.3), channel_id=9, replica_groups={{0,1},{2,3},{4,5},{6,7},{8,9},{10,11},{12,13},{14,15},{16,17},{18,19},{..., dimensions={0}, use_global_device_ids=true | all-gather | bytes 294912 | tf_op jit(solution)/shard_map/all_gather | solution.py:178
  96.1 1.5 %last.1 = f32[16,4096]{1,0:T(8,128)} custom-call(s32[3,32]{1,0:T(4,128)S(1)} %slice_bitcast_fusion.index, s32[6,1,8]{2,1,0:T(1,128)S(1)} %bitcast.45, bf16[24,16,128]{2,1,0:T(8,128)(2,1)S(1)} %collective-permute-done.6.near, bf16[16,16,128]{2,1,0:T(8,128)(2,1)S(1)} %collective-permute-done.7.far, bf16[2,24,16,128]{3,2,1,0:T(8,128)(2,1)S(1)} %bitcast.38, ...), custom_call_target="tpu_custom_call" | custom-call | tf_op jit(solution)/shard_map/last/pallas_call | solution.py:238
  (47 shorter events, 12.5 us)
Async XLA Ops:
  0.0 0.9 copy-start.1
  1.0 0.7 copy-start.2
  1.6 0.7 copy-start.4
  11.7 22.8 %collective-permute-start.1 = (bf16[16,16,128]{2,1,0:T(8,128)(2,1)S(1)}, bf16[16,16,128]{2,1,0:T(8,128)(2,1)S(1)}, u32[]{:S(2)}, u32[]{:S(2)}) collective-permute-start(bf16[16,16,128]{2,1,0:T(8,128)(2,1)S(1)} %get-tuple-element.34), channel_id=1, source_target_pairs={{0,4},{1,509},{2,6},{3,511},{5,9},{4,0},{7,11},{6,2},{8,12},{9,5},... | collective-permute-start | bytes 196616 | tf_op jit(solution)/shard_map/ppermute | solution.py:209
  22.9 11.7 %collective-permute-start = (bf16[24,16,128]{2,1,0:T(8,128)(2,1)S(1)}, bf16[24,16,128]{2,1,0:T(8,128)(2,1)S(1)}, u32[]{:S(2)}, u32[]{:S(2)}) collective-permute-start(bf16[24,16,128]{2,1,0:T(8,128)(2,1)S(1)} %get-tuple-element.33), channel_id=1, source_target_pairs={{0,2},{1,511},{3,5},{2,0},{4,6},{5,3},{7,9},{6,4},{8,10},{9,7},{11... | collective-permute-start | bytes 294920 | tf_op jit(solution)/shard_map/ppermute | solution.py:210
  26.8 2.2 %copy-start = (bf16[128,128,128]{2,1,0:T(8,128)(2,1)S(1)}, bf16[128,128,128]{2,1,0:T(8,128)(2,1)}, u32[]{:S(2)}) copy-start(bf16[128,128,128]{2,1,0:T(8,128)(2,1)} %blocks.1) | copy-start | bytes 12582916
  29.0 0.7 copy-start.5
  33.0 3.5 %copy-start.3 = (s32[1,6,8]{2,0,1:T(1,128)S(1)}, s32[1,6,8]{2,0,1:T(1,128)}, u32[]{:S(2)}) copy-start(s32[1,6,8]{2,0,1:T(1,128)} %param.9) | copy-start | bytes 580
  40.0 12.3 %collective-permute-start.3 = (bf16[16,16,128]{2,1,0:T(8,128)(2,1)S(1)}, bf16[16,16,128]{2,1,0:T(8,128)(2,1)S(1)}, u32[]{:S(2)}, u32[]{:S(2)}) collective-permute-start(bf16[16,16,128]{2,1,0:T(8,128)(2,1)S(1)} %get-tuple-element.42), channel_id=1, source_target_pairs={{0,4},{1,509},{2,6},{3,511},{5,9},{4,0},{7,11},{6,2},{8,12},{9,5},... | collective-permute-start | bytes 196616 | tf_op jit(solution)/shard_map/ppermute | solution.py:209
  44.7 10.8 %collective-permute-start.2 = (bf16[24,16,128]{2,1,0:T(8,128)(2,1)S(1)}, bf16[24,16,128]{2,1,0:T(8,128)(2,1)S(1)}, u32[]{:S(2)}, u32[]{:S(2)}) collective-permute-start(bf16[24,16,128]{2,1,0:T(8,128)(2,1)S(1)} %get-tuple-element.41), channel_id=1, source_target_pairs={{0,2},{1,511},{3,5},{2,0},{4,6},{5,3},{7,9},{6,4},{8,10},{9,7},{11... | collective-permute-start | bytes 294920 | tf_op jit(solution)/shard_map/ppermute | solution.py:210
  60.9 11.9 %collective-permute-start.5 = (bf16[16,16,128]{2,1,0:T(8,128)(2,1)S(1)}, bf16[16,16,128]{2,1,0:T(8,128)(2,1)S(1)}, u32[]{:S(2)}, u32[]{:S(2)}) collective-permute-start(bf16[16,16,128]{2,1,0:T(8,128)(2,1)S(1)} %get-tuple-element.48), channel_id=1, source_target_pairs={{0,4},{1,509},{2,6},{3,511},{5,9},{4,0},{7,11},{6,2},{8,12},{9,5},... | collective-permute-start | bytes 196616 | tf_op jit(solution)/shard_map/ppermute | solution.py:209
  62.8 10.9 %collective-permute-start.4 = (bf16[24,16,128]{2,1,0:T(8,128)(2,1)S(1)}, bf16[24,16,128]{2,1,0:T(8,128)(2,1)S(1)}, u32[]{:S(2)}, u32[]{:S(2)}) collective-permute-start(bf16[24,16,128]{2,1,0:T(8,128)(2,1)S(1)} %get-tuple-element.47), channel_id=1, source_target_pairs={{0,2},{1,511},{3,5},{2,0},{4,6},{5,3},{7,9},{6,4},{8,10},{9,7},{11... | collective-permute-start | bytes 294920 | tf_op jit(solution)/shard_map/ppermute | solution.py:210
  79.2 11.7 %collective-permute-start.7 = (bf16[16,16,128]{2,1,0:T(8,128)(2,1)S(1)}, bf16[16,16,128]{2,1,0:T(8,128)(2,1)S(1)}, u32[]{:S(2)}, u32[]{:S(2)}) collective-permute-start(bf16[16,16,128]{2,1,0:T(8,128)(2,1)S(1)} %get-tuple-element.54), channel_id=1, source_target_pairs={{0,4},{1,509},{2,6},{3,511},{5,9},{4,0},{7,11},{6,2},{8,12},{9,5},... | collective-permute-start | bytes 196616 | tf_op jit(solution)/shard_map/ppermute | solution.py:209
  83.3 10.8 %collective-permute-start.6 = (bf16[24,16,128]{2,1,0:T(8,128)(2,1)S(1)}, bf16[24,16,128]{2,1,0:T(8,128)(2,1)S(1)}, u32[]{:S(2)}, u32[]{:S(2)}) collective-permute-start(bf16[24,16,128]{2,1,0:T(8,128)(2,1)S(1)} %get-tuple-element.53), channel_id=1, source_target_pairs={{0,2},{1,511},{3,5},{2,0},{4,6},{5,3},{7,9},{6,4},{8,10},{9,7},{11... | collective-permute-start | bytes 294920 | tf_op jit(solution)/shard_map/ppermute | solution.py:210

commit v3 on v2

--- a/solution.py
+++ b/solution.py
@@ -10,6 +10,7 @@
 ITERS = 4
 ALPHA = 0.8
 RB, C, BLK, HB = 32, 16, 128, 8
+ZERO = 72
 
 
 SMEM = pl.BlockSpec(memory_space=pltpu.SMEM)
@@ -18,6 +19,10 @@
 HBM = pl.BlockSpec(memory_space=pltpu.HBM)
 
 
+def in_hbm(value):
+    return pltpu.with_memory_space_constraint(value, pltpu.HBM)
+
+
 def bf16(*shape):
     return jax.ShapeDtypeStruct(shape, jnp.bfloat16)
 
@@ -30,7 +35,7 @@
     me = lax.axis_index("dom")
     k = me & 1
     chip = me >> 1
-    return k, ((chip ^ k) & 1) == 0, (((chip >> 1) ^ k) & 1) == 0
+    return k, ((chip ^ k) & 1) == 1, (((chip >> 1) ^ k) & 1) == 0
 
 
 def units():
@@ -80,22 +85,45 @@
     pack(lists, x, mine_out, gift_out)
 
 
-def merge_kernel(mine, chip, near, far, direct):
-    sib = chip.at[1 - role()[0]]
-    near[...] = mine[0:24] + sib[0:24]
-    far[0:8] = sib[24:32]
-    far[8:16] = mine[24:32]
+def merge_kernel(mine, chip, early, later, direct, both):
+    k = role()[0]
+    sib = chip.at[1 - k]
+    both[0:24] = mine[0:24] + sib[0:24]
+    both[24:32] = sib[24:32]
+    both[32:40] = mine[24:32]
+    both[40:48] = mine[24:32]
+    early[...] = both[pl.ds(24 * k, 24)]
+    later[...] = both[pl.ds(24 - 24 * k, 24)]
     direct[...] = sib[32:40]
 
 
-def arrange_kernel(offsets, blocks, out):
-    def row(r, carry):
-        for s in range(4):
-            slot = jnp.minimum(offsets[0, r] + s, BLK - 1)
-            out[r, s * BLK : (s + 1) * BLK, :] = blocks[slot].T
-        return carry
-
-    lax.fori_loop(0, RB, row, 0)
+def owe_kernel(early, later, out, both):
+    k = role()[0]
+    both[0:24] = early[...]
+    both[24:48] = later[...]
+    out[0:16] = both[pl.ds(24 * k, 16)]
+    out[16:24] = both[pl.ds(24 - 24 * k, 8)]
+
+
+def arrange_kernel(offsets_hbm, blocks_hbm, out, offsets, blocks, sems):
+    first = pltpu.make_async_copy(offsets_hbm, offsets, sems.at[8])
+    first.start()
+    copies = []
+    for g in range(8):
+        part = pl.ds(16 * g, 16)
+        copies.append(pltpu.make_async_copy(blocks_hbm.at[part], blocks.at[part], sems.at[g]))
+        copies[-1].start()
+    first.wait()
+    for g in range(8):
+        copies[g].wait()
+
+        def row(r, carry):
+            for s in range(4):
+                slot = jnp.minimum(offsets[0, r] + s, 4 * r + 3)
+                out[r, s * BLK : (s + 1) * BLK, :] = blocks[slot].T
+            return carry
+
+        lax.fori_loop(4 * g, 4 * g + 4, row, 0)
 
 
 def early_kernel(index, x, direct, blocks, acc, src):
@@ -107,17 +135,17 @@
         acc[r] = jnp.dot(lhs, blocks[r], preferred_element_type=jnp.float32)
 
 
-def late_kernel(last, index, lists_any, near, far, side, acc, base, scale, blocks, *rest):
+def late_kernel(last, index, lists_any, early, later, side, acc, base, scale, blocks, *rest):
     if last:
         out, src = rest
     else:
         x_out, mine_out, gift_out, src, x, lists, sem = rest
         copy = pltpu.make_async_copy(lists_any, lists, sem)
         copy.start()
-    src[0:24] = near[...]
-    src[24:40] = far[...]
-    src[40:64] = side[1 - role()[0]]
-    src[64] = jnp.zeros((C, BLK), jnp.bfloat16)
+    src[0:24] = early[...]
+    src[24:48] = later[...]
+    src[48:72] = side[1 - role()[0]]
+    src[ZERO] = jnp.zeros((C, BLK), jnp.bfloat16)
     at = [index[s : s + 1, :] for s in range(3)]
     for r in range(RB):
         lhs = jnp.concatenate([src[at[s][0, r]] for s in range(3)], axis=1)
@@ -139,16 +167,17 @@
     k, up1, up2 = role()
     sel = jnp.where
     first = k == 0
+    near, far, side = 24 * k, 24 - 24 * k, 48
     base = [
-        sel(first, sel(up1, 48, 16), -1),
-        sel(first, -1, sel(up1, 8, 40)),
-        sel(up1, 40, sel(first, 8, 16)),
-        sel(up1, 16, sel(first, 40, 48)),
-        sel(up2, 56, 32),
-        sel(up2, 32, 56),
+        sel(first, sel(up1, side + 8, near + 16), -1),
+        sel(first, -1, sel(up1, near + 8, side)),
+        sel(up1, side, sel(first, near + 8, near + 16)),
+        sel(up1, near + 16, sel(first, side, side + 8)),
+        sel(up2, side + 16, far + 8),
+        sel(up2, far + 8, side + 16),
     ]
     inner = (columns - RB) & (HB - 1)
-    own, got = columns, jnp.full_like(columns, 64)
+    own, got = columns, jnp.full_like(columns, ZERO)
     for j in range(6):
         here = (columns - RB) >> 3 == j
         own = sel(here, sel(base[j] < 0, RB + inner, RB + HB), own)
@@ -158,21 +187,22 @@
     at = start[:, None] + jnp.arange(4, dtype=jnp.int32)[None, :]
     pick = (at[:, :, None] == slots) & (at < end[:, None])[:, :, None]
     own4 = jnp.sum(sel(pick, own - (RB + HB), 0), axis=2) + (RB + HB)
-    got4 = jnp.sum(sel(pick, got - 64, 0), axis=2) + 64
+    got4 = jnp.sum(sel(pick, got - ZERO, 0), axis=2) + ZERO
     return own4.astype(jnp.int32), got4[:, 1:].T.astype(jnp.int32)
 
 
 def on_device(count, blocks, col_index, row_offsets, send_index, deg_scale, seeds):
     groups = [[2 * c, 2 * c + 1] for c in range(count // 2)]
 
-    def matching(step):
+    def pairs(crossing):
         chips = count // 2
-        pairs = []
+        found = []
         for c in range(chips):
-            k = (c // step) % 2
-            for core, other in ((k, c + step), (1 - k, c - step)):
-                pairs.append((2 * c + core, 2 * (other % chips) + core))
-        return pairs
+            if (c & 1) == crossing:
+                found.append((2 * c + 1 - crossing, 2 * ((c + 1) % chips) + 1 - crossing))
+            if (c >> 1 & 1) == crossing:
+                found.append((2 * c + crossing, 2 * ((c + 2) % chips) + crossing))
+        return found + [(b, a) for a, b in found]
 
     def gather(value):
         return lax.all_gather(value, "dom", axis=0, axis_index_groups=groups, tiled=False)
@@ -194,29 +224,35 @@
             pltpu.SemaphoreType.DMA((3,)),
         ],
         name="first",
-    )(lists, seeds, deg_scale.reshape(RB, BLK))
+    )(in_hbm(lists), in_hbm(seeds), in_hbm(deg_scale.reshape(RB, BLK)))
     own_index, got_index = indices(col_index[0], row_offsets[0])
     arranged = None
     for step in range(ITERS):
         chip = gather(gift)
-        near, far, direct = call(
+        early, later, direct = call(
             merge_kernel,
-            out_shape=(bf16(24, *score), bf16(16, *score), bf16(HB, *score)),
+            out_shape=(bf16(24, *score), bf16(24, *score), bf16(HB, *score)),
             in_specs=[VMEM] * 2,
             out_specs=(VMEM,) * 3,
+            scratch_shapes=[pltpu.VMEM((48, *score), jnp.bfloat16)],
             name="merge",
         )(mine, chip)
-        far = lax.ppermute(far, "dom", matching(2))
-        near = lax.ppermute(near, "dom", matching(1))
+        early = lax.ppermute(early, "dom", pairs(1))
+        later = lax.ppermute(later, "dom", pairs(0))
         if arranged is None:
             arranged = call(
                 arrange_kernel,
                 out_shape=bf16(RB, 4 * BLK, BLK),
-                in_specs=[SMEM, VMEM],
+                in_specs=[HBM, HBM],
                 out_specs=VMEM,
+                scratch_shapes=[
+                    pltpu.SMEM(row_offsets.shape, jnp.int32),
+                    pltpu.VMEM(blocks.shape, jnp.bfloat16),
+                    pltpu.SemaphoreType.DMA((9,)),
+                ],
                 cost_estimate=pl.CostEstimate(flops=0, bytes_accessed=16 << 20, transcendentals=0),
                 name="arrange",
-            )(row_offsets, blocks)
+            )(in_hbm(row_offsets), in_hbm(blocks))
         acc = call(
             early_kernel,
             out_shape=f32(RB, *score),
@@ -226,9 +262,17 @@
             cost_estimate=pl.CostEstimate(flops=1 << 30, bytes_accessed=8 << 20, transcendentals=0),
             name="early",
         )(own_index, x, direct, arranged)
-        side = gather(jnp.concatenate([near[:16], far[:8]]))
+        owed = call(
+            owe_kernel,
+            out_shape=bf16(24, *score),
+            in_specs=[VMEM] * 2,
+            out_specs=VMEM,
+            scratch_shapes=[pltpu.VMEM((48, *score), jnp.bfloat16)],
+            name="owe",
+        )(early, later)
+        side = gather(owed)
         last = step == ITERS - 1
-        scratch = [pltpu.VMEM((65, *score), jnp.bfloat16)]
+        scratch = [pltpu.VMEM((ZERO + 1, *score), jnp.bfloat16)]
         if not last:
             scratch += [
                 pltpu.VMEM((RB + 1, *score), jnp.bfloat16),
@@ -242,7 +286,7 @@
             out_specs=VMEM if last else (VMEM,) * 3,
             scratch_shapes=scratch,
             name="last" if last else "late",
-        )(got_index, lists, near, far, side, acc, base, scale, arranged)
+        )(got_index, lists, early, later, side, acc, base, scale, arranged)
         if not last:
             x, mine, gift = result
     return result

time: 98.2 us -> 92.4 us (0.941)
  starting transfers between devices: 44.4 us -> 35.3 us
  blocking collectives: 22.5 us -> 28.5 us
  local copies, waits for them, and re-layouts: 6.15 us -> 0.9 us
  waiting for transfers between devices: 7.48 us -> 9.1 us
  Pallas kernels: 15.8 us -> 16.9 us
    ppermute x8, starting transfers between devices: 44.4 us -> 35.3 us  [the longest x4 23 us: on_device(): early = lax.ppermute(early, 'dom', pairs(1))]
    all_gather x8, blocking collectives: 22.5 us -> 28.5 us  [gather(): lax.all_gather(value, 'dom', axis=0, axis_index_groups=groups, tiled=False)]
    unnamed x12 -> x2, local copies, waits for them, and re-layouts: 5.2 us -> 0.01 us
    ppermute x8, waiting for transfers between devices: 7.48 us -> 9.1 us  [the longest x4 9.09 us: on_device(): early = lax.ppermute(early, 'dom', pairs(1))]
    pallas_call x5 -> x9, Pallas kernels: 3.54 us -> 4.3 us  [the longest x1 4.01 us: on_device(): call(arrange_kernel, out_shape=bf16(RB, 4 * BLK, BLK), in_specs=[HBM, HBM...]
  transfers between devices with their start and end apart: 8 -> 8, of which waited for: 4 -> 3; matrix products, arithmetic and copies ran while one was open for 2% -> 2% of each run, Pallas kernels for 10% -> 11%
where the time goes in v3:
time: 92.4 us; the launch traced here: 91.9 us
  starting transfers between devices  35.3 us (38%)
  blocking collectives  28.5 us (31%)
  Pallas kernels  16.9 us (18%)
  waiting for transfers between devices  9.1 us (10%)
  other arithmetic  1.01 us (1%)
    all_gather x8, blocking collectives, gather(): lax.all_gather(value, 'dom', axis=0, axis_index_groups=groups, tiled=False)  28.5 us
    ppermute x4, starting transfers between devices, on_device(): early = lax.ppermute(early, 'dom', pairs(1))  23 us
    ppermute x4, starting transfers between devices, on_device(): later = lax.ppermute(later, 'dom', pairs(0))  12.4 us
    ppermute x4, waiting for transfers between devices, on_device(): early = lax.ppermute(early, 'dom', pairs(1))  9.09 us
    pallas_call x4, Pallas kernels, on_device(): call(early_kernel, out_shape=f32(RB, *score), in_specs=[SMEM] + [VMEM] *...  5.87 us
    pallas_call x4, Pallas kernels, on_device(): call(functools.partial(late_kernel, last), out_shape=f32(*seeds.shape) if...  5.62 us
    pallas_call x1, Pallas kernels, on_device(): call(arrange_kernel, out_shape=bf16(RB, 4 * BLK, BLK), in_specs=[HBM, HBM...  4.01 us
  transfers between devices with their start and end apart: 8, of which 3 were waited for; matrix products, arithmetic and copies ran while one was open for 2% of the time, Pallas kernels for 11%

profile of v3, /device:TPU:1, one launch (start us, length us, event | category | flops | bytes accessed | tf_op | source)
XLA Modules:
  0.0 91.9 jit_solution(8660225869149672687)
XLA Ops:
  1.1 8.6 %all-gather = bf16[80,16,128]{2,1,0:T(8,128)(2,1)S(1)} all-gather(bf16[40,16,128]{2,1,0:T(8,128)(2,1)S(1)} %get-tuple-element.32), channel_id=2, replica_groups={{0,1},{2,3},{4,5},{6,7},{8,9},{10,11},{12,13},{14,15},{16,17},{18,19},{..., dimensions={0}, use_global_device_ids=true | all-gather | bytes 491520 | tf_op jit(solution)/shard_map/all_gather | solution.py:208
  9.7 11.2 %collective-permute-start = (bf16[24,16,128]{2,1,0:T(8,128)(2,1)S(1)}, bf16[24,16,128]{2,1,0:T(8,128)(2,1)S(1)}, u32[]{:S(2)}, u32[]{:S(2)}) collective-permute-start(bf16[24,16,128]{2,1,0:T(8,128)(2,1)S(1)} %get-tuple-element.33), channel_id=1, source_target_pairs={{2,4},{5,9},{6,8},{7,11},{10,12},{13,17},{14,16},{15,19},{18,20},{... | collective-permute-start | bytes 294920 | tf_op jit(solution)/shard_map/ppermute | solution.py:240
  20.9 2.3 %collective-permute-start.1 = (bf16[24,16,128]{2,1,0:T(8,128)(2,1)S(1)}, bf16[24,16,128]{2,1,0:T(8,128)(2,1)S(1)}, u32[]{:S(2)}, u32[]{:S(2)}) collective-permute-start(bf16[24,16,128]{2,1,0:T(8,128)(2,1)S(1)} %get-tuple-element.34), channel_id=1, source_target_pairs={{1,3},{0,4},{2,6},{5,7},{9,11},{8,12},{10,14},{13,15},{17,19},{16,... | collective-permute-start | bytes 294920 | tf_op jit(solution)/shard_map/ppermute | solution.py:241
  25.2 4.0 %arrange.1.blocks = bf16[32,512,128]{2,1,0:T(8,128)(2,1)S(1)} custom-call(s32[1,33]{1,0:T(1,128)} %offsets_hbm.1, bf16[128,128,128]{2,1,0:T(8,128)(2,1)} %blocks_hbm.1), custom_call_target="tpu_custom_call" | custom-call | bytes 16777216 | tf_op jit(solution)/shard_map/arrange/pallas_call | solution.py:243
  29.2 1.5 %early.4.acc = f32[32,16,128]{2,1,0:T(8,128)S(1)} custom-call(s32[32,4]{1,0:T(8,128)S(1)} %broadcast_add_fusion.index, bf16[32,16,128]{2,1,0:T(8,128)(2,1)S(1)} %get-tuple-element.35.x, bf16[8,16,128]{2,1,0:T(8,128)(2,1)S(1)} %get-tuple-element.36.direct, bf16[32,512,128]{2,1,0:T(8,128)(2,1)S(1)} %arrange.1.blocks), custom_call_target="tpu_custom_call" | custom-call | flops 1073741824 | bytes 8388608 | tf_op jit(solution)/shard_map/early/pallas_call | solution.py:256
  30.7 1.9 %all-gather.1 = bf16[48,16,128]{2,1,0:T(8,128)(2,1)S(1)} all-gather(bf16[24,16,128]{2,1,0:T(8,128)(2,1)S(1)} %owe.4), channel_id=3, replica_groups={{0,1},{2,3},{4,5},{6,7},{8,9},{10,11},{12,13},{14,15},{16,17},{18,19},{..., dimensions={0}, use_global_device_ids=true | all-gather | bytes 294912 | tf_op jit(solution)/shard_map/all_gather | solution.py:208
  34.1 2.0 %all-gather.2 = bf16[80,16,128]{2,1,0:T(8,128)(2,1)S(1)} all-gather(bf16[40,16,128]{2,1,0:T(8,128)(2,1)S(1)} %get-tuple-element.40), channel_id=4, replica_groups={{0,1},{2,3},{4,5},{6,7},{8,9},{10,11},{12,13},{14,15},{16,17},{18,19},{..., dimensions={0}, use_global_device_ids=true | all-gather | bytes 491520 | tf_op jit(solution)/shard_map/all_gather | solution.py:208
  36.2 4.1 %collective-permute-start.2 = (bf16[24,16,128]{2,1,0:T(8,128)(2,1)S(1)}, bf16[24,16,128]{2,1,0:T(8,128)(2,1)S(1)}, u32[]{:S(2)}, u32[]{:S(2)}) collective-permute-start(bf16[24,16,128]{2,1,0:T(8,128)(2,1)S(1)} %get-tuple-element.41), channel_id=1, source_target_pairs={{2,4},{5,9},{6,8},{7,11},{10,12},{13,17},{14,16},{15,19},{18,20},{... | collective-permute-start | bytes 294920 | tf_op jit(solution)/shard_map/ppermute | solution.py:240
  40.3 2.5 %collective-permute-start.3 = (bf16[24,16,128]{2,1,0:T(8,128)(2,1)S(1)}, bf16[24,16,128]{2,1,0:T(8,128)(2,1)S(1)}, u32[]{:S(2)}, u32[]{:S(2)}) collective-permute-start(bf16[24,16,128]{2,1,0:T(8,128)(2,1)S(1)} %get-tuple-element.42), channel_id=1, source_target_pairs={{1,3},{0,4},{2,6},{5,7},{9,11},{8,12},{10,14},{13,15},{17,19},{16,... | collective-permute-start | bytes 294920 | tf_op jit(solution)/shard_map/ppermute | solution.py:241
  42.8 1.5 %early.5.acc = f32[32,16,128]{2,1,0:T(8,128)S(1)} custom-call(s32[32,4]{1,0:T(8,128)S(1)} %broadcast_add_fusion.index, bf16[32,16,128]{2,1,0:T(8,128)(2,1)S(1)} %get-tuple-element.43.x, bf16[8,16,128]{2,1,0:T(8,128)(2,1)S(1)} %get-tuple-element.44.direct, bf16[32,512,128]{2,1,0:T(8,128)(2,1)S(1)} %arrange.1.blocks), custom_call_target="tpu_custom_call" | custom-call | flops 1073741824 | bytes 8388608 | tf_op jit(solution)/shard_map/early/pallas_call | solution.py:256
  44.3 3.7 %collective-permute-done.2.early = bf16[24,16,128]{2,1,0:T(8,128)(2,1)S(1)} collective-permute-done((bf16[24,16,128]{2,1,0:T(8,128)(2,1)S(1)}, bf16[24,16,128]{2,1,0:T(8,128)(2,1)S(1)}, u32[]{:S(2)}, u32[]{:S(2)}) %collective-permute-start.2) | collective-permute-done | bytes 98336 | tf_op jit(solution)/shard_map/ppermute | solution.py:240
  48.0 3.8 %all-gather.3 = bf16[48,16,128]{2,1,0:T(8,128)(2,1)S(1)} all-gather(bf16[24,16,128]{2,1,0:T(8,128)(2,1)S(1)} %owe.5), channel_id=5, replica_groups={{0,1},{2,3},{4,5},{6,7},{8,9},{10,11},{12,13},{14,15},{16,17},{18,19},{..., dimensions={0}, use_global_device_ids=true | all-gather | bytes 294912 | tf_op jit(solution)/shard_map/all_gather | solution.py:208
  53.2 2.0 %all-gather.4 = bf16[80,16,128]{2,1,0:T(8,128)(2,1)S(1)} all-gather(bf16[40,16,128]{2,1,0:T(8,128)(2,1)S(1)} %get-tuple-element.46), channel_id=6, replica_groups={{0,1},{2,3},{4,5},{6,7},{8,9},{10,11},{12,13},{14,15},{16,17},{18,19},{..., dimensions={0}, use_global_device_ids=true | all-gather | bytes 491520 | tf_op jit(solution)/shard_map/all_gather | solution.py:208
  55.3 4.0 %collective-permute-start.4 = (bf16[24,16,128]{2,1,0:T(8,128)(2,1)S(1)}, bf16[24,16,128]{2,1,0:T(8,128)(2,1)S(1)}, u32[]{:S(2)}, u32[]{:S(2)}) collective-permute-start(bf16[24,16,128]{2,1,0:T(8,128)(2,1)S(1)} %get-tuple-element.47), channel_id=1, source_target_pairs={{2,4},{5,9},{6,8},{7,11},{10,12},{13,17},{14,16},{15,19},{18,20},{... | collective-permute-start | bytes 294920 | tf_op jit(solution)/shard_map/ppermute | solution.py:240
  59.3 3.7 %collective-permute-start.5 = (bf16[24,16,128]{2,1,0:T(8,128)(2,1)S(1)}, bf16[24,16,128]{2,1,0:T(8,128)(2,1)S(1)}, u32[]{:S(2)}, u32[]{:S(2)}) collective-permute-start(bf16[24,16,128]{2,1,0:T(8,128)(2,1)S(1)} %get-tuple-element.48), channel_id=1, source_target_pairs={{1,3},{0,4},{2,6},{5,7},{9,11},{8,12},{10,14},{13,15},{17,19},{16,... | collective-permute-start | bytes 294920 | tf_op jit(solution)/shard_map/ppermute | solution.py:241
  63.0 1.5 %early.6.acc = f32[32,16,128]{2,1,0:T(8,128)S(1)} custom-call(s32[32,4]{1,0:T(8,128)S(1)} %broadcast_add_fusion.index, bf16[32,16,128]{2,1,0:T(8,128)(2,1)S(1)} %get-tuple-element.49.x, bf16[8,16,128]{2,1,0:T(8,128)(2,1)S(1)} %get-tuple-element.50.direct, bf16[32,512,128]{2,1,0:T(8,128)(2,1)S(1)} %arrange.1.blocks), custom_call_target="tpu_custom_call" | custom-call | flops 1073741824 | bytes 8388608 | tf_op jit(solution)/shard_map/early/pallas_call | solution.py:256
  64.4 2.6 %collective-permute-done.4.early = bf16[24,16,128]{2,1,0:T(8,128)(2,1)S(1)} collective-permute-done((bf16[24,16,128]{2,1,0:T(8,128)(2,1)S(1)}, bf16[24,16,128]{2,1,0:T(8,128)(2,1)S(1)}, u32[]{:S(2)}, u32[]{:S(2)}) %collective-permute-start.4) | collective-permute-done | bytes 98336 | tf_op jit(solution)/shard_map/ppermute | solution.py:240
  67.1 4.1 %all-gather.5 = bf16[48,16,128]{2,1,0:T(8,128)(2,1)S(1)} all-gather(bf16[24,16,128]{2,1,0:T(8,128)(2,1)S(1)} %owe.6), channel_id=7, replica_groups={{0,1},{2,3},{4,5},{6,7},{8,9},{10,11},{12,13},{14,15},{16,17},{18,19},{..., dimensions={0}, use_global_device_ids=true | all-gather | bytes 294912 | tf_op jit(solution)/shard_map/all_gather | solution.py:208
  72.6 2.0 %all-gather.6 = bf16[80,16,128]{2,1,0:T(8,128)(2,1)S(1)} all-gather(bf16[40,16,128]{2,1,0:T(8,128)(2,1)S(1)} %get-tuple-element.52), channel_id=8, replica_groups={{0,1},{2,3},{4,5},{6,7},{8,9},{10,11},{12,13},{14,15},{16,17},{18,19},{..., dimensions={0}, use_global_device_ids=true | all-gather | bytes 491520 | tf_op jit(solution)/shard_map/all_gather | solution.py:208
  74.7 3.7 %collective-permute-start.6 = (bf16[24,16,128]{2,1,0:T(8,128)(2,1)S(1)}, bf16[24,16,128]{2,1,0:T(8,128)(2,1)S(1)}, u32[]{:S(2)}, u32[]{:S(2)}) collective-permute-start(bf16[24,16,128]{2,1,0:T(8,128)(2,1)S(1)} %get-tuple-element.53), channel_id=1, source_target_pairs={{2,4},{5,9},{6,8},{7,11},{10,12},{13,17},{14,16},{15,19},{18,20},{... | collective-permute-start | bytes 294920 | tf_op jit(solution)/shard_map/ppermute | solution.py:240
  78.4 3.8 %collective-permute-start.7 = (bf16[24,16,128]{2,1,0:T(8,128)(2,1)S(1)}, bf16[24,16,128]{2,1,0:T(8,128)(2,1)S(1)}, u32[]{:S(2)}, u32[]{:S(2)}) collective-permute-start(bf16[24,16,128]{2,1,0:T(8,128)(2,1)S(1)} %get-tuple-element.54), channel_id=1, source_target_pairs={{1,3},{0,4},{2,6},{5,7},{9,11},{8,12},{10,14},{13,15},{17,19},{16,... | collective-permute-start | bytes 294920 | tf_op jit(solution)/shard_map/ppermute | solution.py:241
  83.7 2.8 %collective-permute-done.6.early = bf16[24,16,128]{2,1,0:T(8,128)(2,1)S(1)} collective-permute-done((bf16[24,16,128]{2,1,0:T(8,128)(2,1)S(1)}, bf16[24,16,128]{2,1,0:T(8,128)(2,1)S(1)}, u32[]{:S(2)}, u32[]{:S(2)}) %collective-permute-start.6) | collective-permute-done | bytes 98336 | tf_op jit(solution)/shard_map/ppermute | solution.py:240
  86.5 3.9 %all-gather.7 = bf16[48,16,128]{2,1,0:T(8,128)(2,1)S(1)} all-gather(bf16[24,16,128]{2,1,0:T(8,128)(2,1)S(1)} %owe.7), channel_id=9, replica_groups={{0,1},{2,3},{4,5},{6,7},{8,9},{10,11},{12,13},{14,15},{16,17},{18,19},{..., dimensions={0}, use_global_device_ids=true | all-gather | bytes 294912 | tf_op jit(solution)/shard_map/all_gather | solution.py:208
  90.4 1.5 %last.1 = f32[16,4096]{1,0:T(8,128)} custom-call(s32[3,32]{1,0:T(4,128)S(1)} %slice_bitcast_fusion.index, s32[6,1,8]{2,1,0:T(1,128)S(1)} %bitcast.45, bf16[24,16,128]{2,1,0:T(8,128)(2,1)S(1)} %collective-permute-done.6.early, bf16[24,16,128]{2,1,0:T(8,128)(2,1)S(1)} %collective-permute-done.7.later, bf16[2,24,16,128]{3,2,1,0:T(8,128)(2,1)S(1)} %bitcast.38, ...), custom_call_target="tpu_custom_call" | custom-call | tf_op jit(solution)/shard_map/last/pallas_call | solution.py:282
  (29 shorter events, 8.9 us)
Async XLA Ops:
  9.7 21.0 %collective-permute-start = (bf16[24,16,128]{2,1,0:T(8,128)(2,1)S(1)}, bf16[24,16,128]{2,1,0:T(8,128)(2,1)S(1)}, u32[]{:S(2)}, u32[]{:S(2)}) collective-permute-start(bf16[24,16,128]{2,1,0:T(8,128)(2,1)S(1)} %get-tuple-element.33), channel_id=1, source_target_pairs={{2,4},{5,9},{6,8},{7,11},{10,12},{13,17},{14,16},{15,19},{18,20},{... | collective-permute-start | bytes 294920 | tf_op jit(solution)/shard_map/ppermute | solution.py:240
  20.9 9.8 %collective-permute-start.1 = (bf16[24,16,128]{2,1,0:T(8,128)(2,1)S(1)}, bf16[24,16,128]{2,1,0:T(8,128)(2,1)S(1)}, u32[]{:S(2)}, u32[]{:S(2)}) collective-permute-start(bf16[24,16,128]{2,1,0:T(8,128)(2,1)S(1)} %get-tuple-element.34), channel_id=1, source_target_pairs={{1,3},{0,4},{2,6},{5,7},{9,11},{8,12},{10,14},{13,15},{17,19},{16,... | collective-permute-start | bytes 294920 | tf_op jit(solution)/shard_map/ppermute | solution.py:241
  29.2 3.5 %copy-start = (s32[1,6,8]{2,0,1:T(1,128)S(1)}, s32[1,6,8]{2,0,1:T(1,128)}, u32[]{:S(2)}) copy-start(s32[1,6,8]{2,0,1:T(1,128)} %param.9) | copy-start | bytes 580
  36.2 11.8 %collective-permute-start.2 = (bf16[24,16,128]{2,1,0:T(8,128)(2,1)S(1)}, bf16[24,16,128]{2,1,0:T(8,128)(2,1)S(1)}, u32[]{:S(2)}, u32[]{:S(2)}) collective-permute-start(bf16[24,16,128]{2,1,0:T(8,128)(2,1)S(1)} %get-tuple-element.41), channel_id=1, source_target_pairs={{2,4},{5,9},{6,8},{7,11},{10,12},{13,17},{14,16},{15,19},{18,20},{... | collective-permute-start | bytes 294920 | tf_op jit(solution)/shard_map/ppermute | solution.py:240
  40.3 7.7 %collective-permute-start.3 = (bf16[24,16,128]{2,1,0:T(8,128)(2,1)S(1)}, bf16[24,16,128]{2,1,0:T(8,128)(2,1)S(1)}, u32[]{:S(2)}, u32[]{:S(2)}) collective-permute-start(bf16[24,16,128]{2,1,0:T(8,128)(2,1)S(1)} %get-tuple-element.42), channel_id=1, source_target_pairs={{1,3},{0,4},{2,6},{5,7},{9,11},{8,12},{10,14},{13,15},{17,19},{16,... | collective-permute-start | bytes 294920 | tf_op jit(solution)/shard_map/ppermute | solution.py:241
  55.3 11.8 %collective-permute-start.4 = (bf16[24,16,128]{2,1,0:T(8,128)(2,1)S(1)}, bf16[24,16,128]{2,1,0:T(8,128)(2,1)S(1)}, u32[]{:S(2)}, u32[]{:S(2)}) collective-permute-start(bf16[24,16,128]{2,1,0:T(8,128)(2,1)S(1)} %get-tuple-element.47), channel_id=1, source_target_pairs={{2,4},{5,9},{6,8},{7,11},{10,12},{13,17},{14,16},{15,19},{18,20},{... | collective-permute-start | bytes 294920 | tf_op jit(solution)/shard_map/ppermute | solution.py:240
  59.3 7.8 %collective-permute-start.5 = (bf16[24,16,128]{2,1,0:T(8,128)(2,1)S(1)}, bf16[24,16,128]{2,1,0:T(8,128)(2,1)S(1)}, u32[]{:S(2)}, u32[]{:S(2)}) collective-permute-start(bf16[24,16,128]{2,1,0:T(8,128)(2,1)S(1)} %get-tuple-element.48), channel_id=1, source_target_pairs={{1,3},{0,4},{2,6},{5,7},{9,11},{8,12},{10,14},{13,15},{17,19},{16,... | collective-permute-start | bytes 294920 | tf_op jit(solution)/shard_map/ppermute | solution.py:241
  74.7 11.8 %collective-permute-start.6 = (bf16[24,16,128]{2,1,0:T(8,128)(2,1)S(1)}, bf16[24,16,128]{2,1,0:T(8,128)(2,1)S(1)}, u32[]{:S(2)}, u32[]{:S(2)}) collective-permute-start(bf16[24,16,128]{2,1,0:T(8,128)(2,1)S(1)} %get-tuple-element.53), channel_id=1, source_target_pairs={{2,4},{5,9},{6,8},{7,11},{10,12},{13,17},{14,16},{15,19},{18,20},{... | collective-permute-start | bytes 294920 | tf_op jit(solution)/shard_map/ppermute | solution.py:240
  78.4 8.1 %collective-permute-start.7 = (bf16[24,16,128]{2,1,0:T(8,128)(2,1)S(1)}, bf16[24,16,128]{2,1,0:T(8,128)(2,1)S(1)}, u32[]{:S(2)}, u32[]{:S(2)}) collective-permute-start(bf16[24,16,128]{2,1,0:T(8,128)(2,1)S(1)} %get-tuple-element.54), channel_id=1, source_target_pairs={{1,3},{0,4},{2,6},{5,7},{9,11},{8,12},{10,14},{13,15},{17,19},{16,... | collective-permute-start | bytes 294920 | tf_op jit(solution)/shard_map/ppermute | solution.py:241

commit v4 on v3

v4 whole, which is shorter than its diff:
```python
import functools

import jax
import jax.numpy as jnp
from jax import lax
from jax.experimental import pallas as pl
from jax.experimental.pallas import tpu as pltpu
from jax.sharding import PartitionSpec as P

ITERS = 4
ALPHA = 0.8
RB, C, BLK, HB = 32, 16, 128, 8
SENT, PAIR, SIDE, DIRECT, ZERO = 32, 56, 80, 104, 112


SMEM = pl.BlockSpec(memory_space=pltpu.SMEM)
VMEM = pl.BlockSpec(memory_space=pltpu.VMEM)
ANY = pl.BlockSpec(memory_space=pl.ANY)
HBM = pl.BlockSpec(memory_space=pltpu.HBM)


def in_hbm(value):
    return pltpu.with_memory_space_constraint(value, pltpu.HBM)


def bf16(*shape):
    return jax.ShapeDtypeStruct(shape, jnp.bfloat16)


def f32(*shape):
    return jax.ShapeDtypeStruct(shape, jnp.float32)


def role():
    me = lax.axis_index("dom")
    k = me & 1
    chip = me >> 1
    return k, ((chip ^ k) & 1) == 1, (((chip >> 1) ^ k) & 1) == 0


def units():
    k, up1, up2 = role()
    sel = jnp.where
    first = k == 0
    mine = [
        sel(first & ~up1, 1, -1),
        sel(up1, sel(first, 2, 0), -1),
        sel(first & up1, -1, sel(up1, 2, 3)),
        sel(up2, 4, 5),
    ]
    gift = [
        sel(first, sel(up1, 3, 2), sel(up1, -1, 2)),
        sel(first, sel(up1, 1, -1), sel(up1, 3, -1)),
        sel(first | up1, -1, 0),
        sel(up2, 5, 4),
        k,
    ]
    return mine, gift


def pack(lists, x, mine_out, gift_out):
    for out, which in zip((mine_out, gift_out), units()):
        for at, unit in enumerate(which):
            for h in range(HB):
                block = jnp.where(unit < 0, RB, lists[jnp.maximum(unit, 0), 0, h])
                out[at * HB + h] = x[block]


def first_kernel(*refs):
    sources, (x_out, mine_out, gift_out, base_out, scale_out, columns, offsets, lists, seeds, x, sems) = refs[:5], refs[5:]
    copies = []
    for i, target in enumerate((seeds, scale_out, lists, columns, offsets)):
        copies.append(pltpu.make_async_copy(sources[i], target, sems.at[i]))
        copies[-1].start()
    for copy in copies:
        copy.wait()
    for r in range(RB):
        field = seeds[:, r * BLK : (r + 1) * BLK]
        base_out[r] = (1.0 - ALPHA) * field
        x[r] = (field * scale_out[r : r + 1, :]).astype(jnp.bfloat16)
    x[RB] = jnp.zeros((C, BLK), jnp.bfloat16)
    x_out[...] = x[0:RB]
    pack(lists, x, mine_out, gift_out)


def partner():
    me = lax.axis_index("dom")
    return 1 - jnp.where(me & 1 == 0, (me >> 2) & 1, (me >> 1) & 1)


def merge_kernel(mine, chip, cross, inner, both):
    k = role()[0]
    sib = chip.at[1 - k]
    both[0:24] = mine[0:24] + sib[0:24]
    both[24:32] = sib[24:32]
    both[32:40] = mine[24:32]
    both[40:48] = mine[24:32]
    cross[...] = both[pl.ds(24 * k, 24)]
    inner[...] = both[pl.ds(24 - 24 * k, 24)]


def owe_kernel(cross, pair, out, both):
    k = role()[0]
    both[0:24] = cross[...]
    both[24:48] = pair[partner()]
    out[0:16] = both[pl.ds(24 * k, 16)]
    out[16:24] = both[pl.ds(24 - 24 * k, 8)]


def arrange_kernel(offsets_any, blocks_hbm, out, offsets, blocks, sems):
    first = pltpu.make_async_copy(offsets_any, offsets, sems.at[8])
    first.start()
    copies = []
    for g in range(8):
        part = pl.ds(16 * g, 16)
        copies.append(pltpu.make_async_copy(blocks_hbm.at[part], blocks.at[part], sems.at[g]))
        copies[-1].start()
    first.wait()
    for g in range(8):
        copies[g].wait()
        for r in range(4 * g, 4 * g + 4):
            for s in range(4):
                slot = jnp.minimum(offsets[0, r] + s, 4 * r + 3)
                out[r, s * BLK : (s + 1) * BLK, :] = blocks[slot].T


def step_kernel(last, index, lists_any, x_in, chip, cross, pair, side, base, scale, blocks, *rest):
    if last:
        out, src = rest
    else:
        x_out, mine_out, gift_out, src, x, lists, sem = rest
        copy = pltpu.make_async_copy(lists_any, lists, sem)
        copy.start()
    other = 1 - role()[0]
    src[0:SENT] = x_in[...]
    src[SENT:PAIR] = cross[...]
    src[PAIR:SIDE] = pair[partner()]
    src[SIDE:DIRECT] = side[other]
    src[DIRECT:ZERO] = chip[other, 32:40]
    src[ZERO] = jnp.zeros((C, BLK), jnp.bfloat16)
    at = [index[s : s + 1, :] for s in range(4)]
    for r in range(RB):
        lhs = jnp.concatenate([src[at[s][0, r]] for s in range(4)], axis=1)
        total = jnp.dot(lhs, blocks[r], preferred_element_type=jnp.float32)
        s = scale[r : r + 1, :]
        field = ALPHA * s * total + base[r]
        if last:
            out[:, r * BLK : (r + 1) * BLK] = field
        else:
            x[r] = (field * s).astype(jnp.bfloat16)
    if not last:
        x[RB] = jnp.zeros((C, BLK), jnp.bfloat16)
        x_out[...] = x[0:RB]
        copy.wait()
        pack(lists, x, mine_out, gift_out)


def indices(columns, offsets):
    k, up1, up2 = role()
    sel = jnp.where
    first = k == 0
    near, far = sel(first, SENT, PAIR), sel(first, PAIR, SENT)
    base = [
        sel(first, sel(up1, SIDE + 8, near + 16), DIRECT),
        sel(first, DIRECT, sel(up1, near + 8, SIDE)),
        sel(up1, SIDE, sel(first, near + 8, near + 16)),
        sel(up1, near + 16, sel(first, SIDE, SIDE + 8)),
        sel(up2, SIDE + 16, far + 8),
        sel(up2, far + 8, SIDE + 16),
    ]
    where = columns
    for j in range(6):
        where = sel((columns - RB) >> 3 == j, base[j] + ((columns - RB) & (HB - 1)), where)
    slots = jnp.arange(BLK, dtype=jnp.int32)
    at = offsets[None, :RB] + jnp.arange(4, dtype=jnp.int32)[:, None]
    pick = (at[:, :, None] == slots) & (at < offsets[None, 1:])[:, :, None]
    return (jnp.sum(sel(pick, where - ZERO, 0), axis=2) + ZERO).astype(jnp.int32)


def on_device(count, blocks, col_index, row_offsets, send_index, deg_scale, seeds):
    chips = [[2 * c, 2 * c + 1] for c in range(count // 2)]

    def pairs(crossing):
        found = []
        for c in range(len(chips)):
            if (c & 1) == crossing:
                found.append((2 * c + 1 - crossing, 2 * ((c + 1) % len(chips)) + 1 - crossing))
            if (c >> 1 & 1) == crossing:
                found.append((2 * c + crossing, 2 * ((c + 2) % len(chips)) + crossing))
        return found

    def gather(value, groups):
        return lax.all_gather(value, "dom", axis=0, axis_index_groups=[list(g) for g in groups], tiled=False)

    params = pltpu.CompilerParams(vmem_limit_bytes=16 << 20)
    call = functools.partial(pl.pallas_call, compiler_params=params)
    lists = jnp.transpose(send_index, (1, 0, 2))
    score = (C, BLK)

    x, mine, gift, base, scale, columns, offsets = call(
        first_kernel,
        out_shape=(
            bf16(RB, *score),
            bf16(32, *score),
            bf16(40, *score),
            f32(RB, *score),
            f32(RB, BLK),
            jax.ShapeDtypeStruct(col_index.shape, jnp.int32),
            jax.ShapeDtypeStruct(row_offsets.shape, jnp.int32),
        ),
        in_specs=[HBM] * 5,
        out_specs=(VMEM,) * 7,
        scratch_shapes=[
            pltpu.SMEM(lists.shape, jnp.int32),
            pltpu.VMEM(seeds.shape, jnp.float32),
            pltpu.VMEM((RB + 1, *score), jnp.bfloat16),
            pltpu.SemaphoreType.DMA((5,)),
        ],
        name="first",
    )(*map(in_hbm, (seeds, deg_scale.reshape(RB, BLK), lists, col_index, row_offsets)))
    index = arranged = None
    for step in range(ITERS):
        chip = gather(gift, chips)
        cross, inner = call(
            merge_kernel,
            out_shape=(bf16(24, *score), bf16(24, *score)),
            in_specs=[VMEM] * 2,
            out_specs=(VMEM,) * 2,
            scratch_shapes=[pltpu.VMEM((48, *score), jnp.bfloat16)],
            name="merge",
        )(mine, chip)
        crossing = pairs(1)
        cross = lax.ppermute(cross, "dom", crossing + [(b, a) for a, b in crossing])
        pair = gather(inner, pairs(0))
        if arranged is None:
            pair, offsets, columns = lax.optimization_barrier((pair, offsets, columns))
            index = indices(columns[0], offsets[0])
            arranged = call(
                arrange_kernel,
                out_shape=bf16(RB, 4 * BLK, BLK),
                in_specs=[ANY, HBM],
                out_specs=VMEM,
                scratch_shapes=[
                    pltpu.SMEM(row_offsets.shape, jnp.int32),
                    pltpu.VMEM(blocks.shape, jnp.bfloat16),
                    pltpu.SemaphoreType.DMA((9,)),
                ],
                cost_estimate=pl.CostEstimate(flops=0, bytes_accessed=16 << 20, transcendentals=0),
                name="arrange",
            )(offsets, in_hbm(blocks))
        owed = call(
            owe_kernel,
            out_shape=bf16(24, *score),
            in_specs=[VMEM] * 2,
            out_specs=VMEM,
            scratch_shapes=[pltpu.VMEM((48, *score), jnp.bfloat16)],
            name="owe",
        )(cross, pair)
        side = gather(owed, chips)
        last = step == ITERS - 1
        scratch = [pltpu.VMEM((ZERO + 1, *score), jnp.bfloat16)]
        if not last:
            scratch += [
                pltpu.VMEM((RB + 1, *score), jnp.bfloat16),
                pltpu.SMEM(lists.shape, jnp.int32),
                pltpu.SemaphoreType.DMA,
            ]
        result = call(
            functools.partial(step_kernel, last),
            out_shape=f32(*seeds.shape) if last else (bf16(RB, *score), bf16(32, *score), bf16(40, *score)),
            in_specs=[VMEM, ANY] + [VMEM] * 8,
            out_specs=VMEM if last else (VMEM,) * 3,
            scratch_shapes=scratch,
            name="last" if last else "late",
        )(index, lists, x, chip, cross, pair, side, base, scale, arranged)
        if not last:
            x, mine, gift = result
    return result


def solution(mesh):
    in_specs = (
        P("dom", None, None),
        P("dom", None),
        P("dom", None),
        P("dom", None, None),
        P("dom"),
        P(None, "dom"),
    )
    out_specs = P(None, "dom")
    return jax.shard_map(
        functools.partial(on_device, mesh.size), mesh=mesh, in_specs=in_specs, out_specs=out_specs, check_vma=False
    )
```

time: 92.4 us -> 88.7 us (0.960)
  blocking collectives: 28.5 us -> 44.5 us
  starting transfers between devices: 35.3 us -> 27.3 us
  Pallas kernels: 16.9 us -> 9.57 us
  waiting for transfers between devices: 9.1 us -> 6.43 us
    all_gather x8 -> x12, blocking collectives: 28.5 us -> 44.5 us  [gather(): lax.all_gather(value, 'dom', axis=0, axis_index_groups=[list(g) for g in...]
    ppermute x8 -> x4, starting transfers between devices: 35.3 us -> 27.3 us  [on_device(): cross = lax.ppermute(cross, 'dom', crossing + [(b, a) for a, b in crossing])]
    pallas_call x13 -> x9, Pallas kernels: 15.7 us -> 8.34 us  [the longest x4 5.49 us: on_device(): call(functools.partial(step_kernel, last), out_shape=f32(*seeds.shape) if...]
    ppermute x8 -> x4, waiting for transfers between devices: 9.1 us -> 6.43 us  [on_device(): cross = lax.ppermute(cross, 'dom', crossing + [(b, a) for a, b in crossing])]
  transfers between devices with their start and end apart: 8 -> 4, of which waited for: 3 -> 3; matrix products, arithmetic and copies ran while one was open for 2% -> 0% of each run, Pallas kernels for 11% -> 3%
where the time goes in v4:
time: 88.7 us; the launch traced here: 88.4 us
  blocking collectives  44.5 us (50%)
  starting transfers between devices  27.3 us (31%)
  Pallas kernels  9.57 us (11%)
  waiting for transfers between devices  6.43 us (7%)
    all_gather x12, blocking collectives, gather(): lax.all_gather(value, 'dom', axis=0, axis_index_groups=[list(g) for g in...  44.5 us
    ppermute x4, starting transfers between devices, on_device(): cross = lax.ppermute(cross, 'dom', crossing + [(b, a) for a, b in crossing])  27.3 us
    ppermute x4, waiting for transfers between devices, on_device(): cross = lax.ppermute(cross, 'dom', crossing + [(b, a) for a, b in crossing])  6.43 us
    pallas_call x4, Pallas kernels, on_device(): call(functools.partial(step_kernel, last), out_shape=f32(*seeds.shape) if...  5.49 us
    pallas_call x1, Pallas kernels, on_device(): call(arrange_kernel, out_shape=bf16(RB, 4 * BLK, BLK), in_specs=[ANY, HBM...  2.66 us
  transfers between devices with their start and end apart: 4, of which 3 were waited for; matrix products, arithmetic and copies ran while one was open for 0% of the time, Pallas kernels for 3%

profile of v4, /device:TPU:1, one launch (start us, length us, event | category | flops | bytes accessed | tf_op | source)
XLA Modules:
  0.0 88.4 jit_solution(1755457309509338276)
XLA Ops:
  1.1 8.6 %all-gather = bf16[80,16,128]{2,1,0:T(8,128)(2,1)S(1)} all-gather(bf16[40,16,128]{2,1,0:T(8,128)(2,1)S(1)} %get-tuple-element.33), channel_id=2, replica_groups={{0,1},{2,3},{4,5},{6,7},{8,9},{10,11},{12,13},{14,15},{16,17},{18,19},{..., dimensions={0}, use_global_device_ids=true | all-gather | bytes 491520 | tf_op jit(solution)/shard_map/all_gather | solution.py:193
  9.7 11.2 %collective-permute-start = (bf16[24,16,128]{2,1,0:T(8,128)(2,1)S(1)}, bf16[24,16,128]{2,1,0:T(8,128)(2,1)S(1)}, u32[]{:S(2)}, u32[]{:S(2)}) collective-permute-start(bf16[24,16,128]{2,1,0:T(8,128)(2,1)S(1)} %get-tuple-element.40), channel_id=1, source_target_pairs={{2,4},{5,9},{6,8},{7,11},{10,12},{13,17},{14,16},{15,19},{18,20},{... | collective-permute-start | bytes 294920 | tf_op jit(solution)/shard_map/ppermute | solution.py:233
  21.0 4.4 %all-gather.1 = bf16[48,16,128]{2,1,0:T(8,128)(2,1)S(1)} all-gather(bf16[24,16,128]{2,1,0:T(8,128)(2,1)S(1)} %get-tuple-element.34), channel_id=3, replica_groups={{1,3},{0,4},{2,6},{5,7},{9,11},{8,12},{10,14},{13,15},{17,19},{16,20},{..., dimensions={0}, use_global_device_ids=true | all-gather | bytes 294912 | tf_op jit(solution)/shard_map/all_gather | solution.py:193
  25.8 2.7 %arrange.1.blocks = bf16[32,512,128]{2,1,0:T(8,128)(2,1)S(1)} custom-call(s32[1,33]{1,0:T(1,128)S(1)} %get-tuple-element.37.offsets_any, bf16[128,128,128]{2,1,0:T(8,128)(2,1)} %blocks_hbm.1), custom_call_target="tpu_custom_call" | custom-call | bytes 16777216 | tf_op jit(solution)/shard_map/arrange/pallas_call | solution.py:238
  28.5 3.2 %all-gather.2 = bf16[48,16,128]{2,1,0:T(8,128)(2,1)S(1)} all-gather(bf16[24,16,128]{2,1,0:T(8,128)(2,1)S(1)} %owe.4), channel_id=4, replica_groups={{0,1},{2,3},{4,5},{6,7},{8,9},{10,11},{12,13},{14,15},{16,17},{18,19},{..., dimensions={0}, use_global_device_ids=true | all-gather | bytes 294912 | tf_op jit(solution)/shard_map/all_gather | solution.py:193
  31.7 1.3 %late.3 = (bf16[32,16,128]{2,1,0:T(8,128)(2,1)S(1)}, bf16[32,16,128]{2,1,0:T(8,128)(2,1)S(1)}, bf16[40,16,128]{2,1,0:T(8,128)(2,1)S(1)}) custom-call(s32[4,32]{1,0:T(4,128)S(1)} %broadcast_add_fusion.index, s32[6,1,8]{2,1,0:T(1,128)S(1)} %bitcast.44, bf16[32,16,128]{2,1,0:T(8,128)(2,1)S(1)} %get-tuple-element.39.x_in, bf16[2,40,16,128]{3,2,1,0:T(8,128)(2,1)S(1)} %bitcast.24, ...), custom_call_target="tpu_custom_call" | custom-call | tf_op jit(solution)/shard_map/late/pallas_call | solution.py:268
  33.1 2.0 %all-gather.3 = bf16[80,16,128]{2,1,0:T(8,128)(2,1)S(1)} all-gather(bf16[40,16,128]{2,1,0:T(8,128)(2,1)S(1)} %get-tuple-element.45), channel_id=5, replica_groups={{0,1},{2,3},{4,5},{6,7},{8,9},{10,11},{12,13},{14,15},{16,17},{18,19},{..., dimensions={0}, use_global_device_ids=true | all-gather | bytes 491520 | tf_op jit(solution)/shard_map/all_gather | solution.py:193
  35.2 4.9 %collective-permute-start.1 = (bf16[24,16,128]{2,1,0:T(8,128)(2,1)S(1)}, bf16[24,16,128]{2,1,0:T(8,128)(2,1)S(1)}, u32[]{:S(2)}, u32[]{:S(2)}) collective-permute-start(bf16[24,16,128]{2,1,0:T(8,128)(2,1)S(1)} %get-tuple-element.47), channel_id=1, source_target_pairs={{2,4},{5,9},{6,8},{7,11},{10,12},{13,17},{14,16},{15,19},{18,20},{... | collective-permute-start | bytes 294920 | tf_op jit(solution)/shard_map/ppermute | solution.py:233
  40.1 4.1 %all-gather.4 = bf16[48,16,128]{2,1,0:T(8,128)(2,1)S(1)} all-gather(bf16[24,16,128]{2,1,0:T(8,128)(2,1)S(1)} %get-tuple-element.48), channel_id=6, replica_groups={{1,3},{0,4},{2,6},{5,7},{9,11},{8,12},{10,14},{13,15},{17,19},{16,20},{..., dimensions={0}, use_global_device_ids=true | all-gather | bytes 294912 | tf_op jit(solution)/shard_map/all_gather | solution.py:193
  44.3 2.7 %collective-permute-done.1.cross = bf16[24,16,128]{2,1,0:T(8,128)(2,1)S(1)} collective-permute-done((bf16[24,16,128]{2,1,0:T(8,128)(2,1)S(1)}, bf16[24,16,128]{2,1,0:T(8,128)(2,1)S(1)}, u32[]{:S(2)}, u32[]{:S(2)}) %collective-permute-start.1) | collective-permute-done | bytes 98336 | tf_op jit(solution)/shard_map/ppermute | solution.py:233
  47.0 3.2 %all-gather.5 = bf16[48,16,128]{2,1,0:T(8,128)(2,1)S(1)} all-gather(bf16[24,16,128]{2,1,0:T(8,128)(2,1)S(1)} %owe.5), channel_id=7, replica_groups={{0,1},{2,3},{4,5},{6,7},{8,9},{10,11},{12,13},{14,15},{16,17},{18,19},{..., dimensions={0}, use_global_device_ids=true | all-gather | bytes 294912 | tf_op jit(solution)/shard_map/all_gather | solution.py:193
  50.1 1.3 %late.4 = (bf16[32,16,128]{2,1,0:T(8,128)(2,1)S(1)}, bf16[32,16,128]{2,1,0:T(8,128)(2,1)S(1)}, bf16[40,16,128]{2,1,0:T(8,128)(2,1)S(1)}) custom-call(s32[4,32]{1,0:T(4,128)S(1)} %broadcast_add_fusion.index, s32[6,1,8]{2,1,0:T(1,128)S(1)} %bitcast.45, bf16[32,16,128]{2,1,0:T(8,128)(2,1)S(1)} %get-tuple-element.44.x_in, bf16[2,40,16,128]{3,2,1,0:T(8,128)(2,1)S(1)} %bitcast.26, ...), custom_call_target="tpu_custom_call" | custom-call | tf_op jit(solution)/shard_map/late/pallas_call | solution.py:268
  51.5 2.0 %all-gather.6 = bf16[80,16,128]{2,1,0:T(8,128)(2,1)S(1)} all-gather(bf16[40,16,128]{2,1,0:T(8,128)(2,1)S(1)} %get-tuple-element.50), channel_id=8, replica_groups={{0,1},{2,3},{4,5},{6,7},{8,9},{10,11},{12,13},{14,15},{16,17},{18,19},{..., dimensions={0}, use_global_device_ids=true | all-gather | bytes 491520 | tf_op jit(solution)/shard_map/all_gather | solution.py:193
  53.6 5.4 %collective-permute-start.2 = (bf16[24,16,128]{2,1,0:T(8,128)(2,1)S(1)}, bf16[24,16,128]{2,1,0:T(8,128)(2,1)S(1)}, u32[]{:S(2)}, u32[]{:S(2)}) collective-permute-start(bf16[24,16,128]{2,1,0:T(8,128)(2,1)S(1)} %get-tuple-element.52), channel_id=1, source_target_pairs={{2,4},{5,9},{6,8},{7,11},{10,12},{13,17},{14,16},{15,19},{18,20},{... | collective-permute-start | bytes 294920 | tf_op jit(solution)/shard_map/ppermute | solution.py:233
  59.0 4.1 %all-gather.7 = bf16[48,16,128]{2,1,0:T(8,128)(2,1)S(1)} all-gather(bf16[24,16,128]{2,1,0:T(8,128)(2,1)S(1)} %get-tuple-element.53), channel_id=9, replica_groups={{1,3},{0,4},{2,6},{5,7},{9,11},{8,12},{10,14},{13,15},{17,19},{16,20},{..., dimensions={0}, use_global_device_ids=true | all-gather | bytes 294912 | tf_op jit(solution)/shard_map/all_gather | solution.py:193
  63.2 2.2 %collective-permute-done.2.cross = bf16[24,16,128]{2,1,0:T(8,128)(2,1)S(1)} collective-permute-done((bf16[24,16,128]{2,1,0:T(8,128)(2,1)S(1)}, bf16[24,16,128]{2,1,0:T(8,128)(2,1)S(1)}, u32[]{:S(2)}, u32[]{:S(2)}) %collective-permute-start.2) | collective-permute-done | bytes 98336 | tf_op jit(solution)/shard_map/ppermute | solution.py:233
  65.4 3.2 %all-gather.8 = bf16[48,16,128]{2,1,0:T(8,128)(2,1)S(1)} all-gather(bf16[24,16,128]{2,1,0:T(8,128)(2,1)S(1)} %owe.6), channel_id=10, replica_groups={{0,1},{2,3},{4,5},{6,7},{8,9},{10,11},{12,13},{14,15},{16,17},{18,19},{..., dimensions={0}, use_global_device_ids=true | all-gather | bytes 294912 | tf_op jit(solution)/shard_map/all_gather | solution.py:193
  68.6 1.3 %late.5 = (bf16[32,16,128]{2,1,0:T(8,128)(2,1)S(1)}, bf16[32,16,128]{2,1,0:T(8,128)(2,1)S(1)}, bf16[40,16,128]{2,1,0:T(8,128)(2,1)S(1)}) custom-call(s32[4,32]{1,0:T(4,128)S(1)} %broadcast_add_fusion.index, s32[6,1,8]{2,1,0:T(1,128)S(1)} %bitcast.46, bf16[32,16,128]{2,1,0:T(8,128)(2,1)S(1)} %get-tuple-element.49.x_in, bf16[2,40,16,128]{3,2,1,0:T(8,128)(2,1)S(1)} %bitcast.28, ...), custom_call_target="tpu_custom_call" | custom-call | tf_op jit(solution)/shard_map/late/pallas_call | solution.py:268
  69.9 2.0 %all-gather.9 = bf16[80,16,128]{2,1,0:T(8,128)(2,1)S(1)} all-gather(bf16[40,16,128]{2,1,0:T(8,128)(2,1)S(1)} %get-tuple-element.55), channel_id=11, replica_groups={{0,1},{2,3},{4,5},{6,7},{8,9},{10,11},{12,13},{14,15},{16,17},{18,19},{..., dimensions={0}, use_global_device_ids=true | all-gather | bytes 491520 | tf_op jit(solution)/shard_map/all_gather | solution.py:193
  72.0 5.8 %collective-permute-start.3 = (bf16[24,16,128]{2,1,0:T(8,128)(2,1)S(1)}, bf16[24,16,128]{2,1,0:T(8,128)(2,1)S(1)}, u32[]{:S(2)}, u32[]{:S(2)}) collective-permute-start(bf16[24,16,128]{2,1,0:T(8,128)(2,1)S(1)} %get-tuple-element.57), channel_id=1, source_target_pairs={{2,4},{5,9},{6,8},{7,11},{10,12},{13,17},{14,16},{15,19},{18,20},{... | collective-permute-start | bytes 294920 | tf_op jit(solution)/shard_map/ppermute | solution.py:233
  77.8 4.5 %all-gather.10 = bf16[48,16,128]{2,1,0:T(8,128)(2,1)S(1)} all-gather(bf16[24,16,128]{2,1,0:T(8,128)(2,1)S(1)} %get-tuple-element.58), channel_id=12, replica_groups={{1,3},{0,4},{2,6},{5,7},{9,11},{8,12},{10,14},{13,15},{17,19},{16,20},{..., dimensions={0}, use_global_device_ids=true | all-gather | bytes 294912 | tf_op jit(solution)/shard_map/all_gather | solution.py:193
  82.2 1.5 %collective-permute-done.3.cross = bf16[24,16,128]{2,1,0:T(8,128)(2,1)S(1)} collective-permute-done((bf16[24,16,128]{2,1,0:T(8,128)(2,1)S(1)}, bf16[24,16,128]{2,1,0:T(8,128)(2,1)S(1)}, u32[]{:S(2)}, u32[]{:S(2)}) %collective-permute-start.3) | collective-permute-done | bytes 98336 | tf_op jit(solution)/shard_map/ppermute | solution.py:233
  83.8 3.2 %all-gather.11 = bf16[48,16,128]{2,1,0:T(8,128)(2,1)S(1)} all-gather(bf16[24,16,128]{2,1,0:T(8,128)(2,1)S(1)} %owe.7), channel_id=13, replica_groups={{0,1},{2,3},{4,5},{6,7},{8,9},{10,11},{12,13},{14,15},{16,17},{18,19},{..., dimensions={0}, use_global_device_ids=true | all-gather | bytes 294912 | tf_op jit(solution)/shard_map/all_gather | solution.py:193
  87.0 1.5 %last.1 = f32[16,4096]{1,0:T(8,128)} custom-call(s32[4,32]{1,0:T(4,128)S(1)} %broadcast_add_fusion.index, s32[6,1,8]{2,1,0:T(1,128)S(1)} %bitcast.47, bf16[32,16,128]{2,1,0:T(8,128)(2,1)S(1)} %get-tuple-element.54.x_in, bf16[2,40,16,128]{3,2,1,0:T(8,128)(2,1)S(1)} %bitcast.30, bf16[24,16,128]{2,1,0:T(8,128)(2,1)S(1)} %collective-permute-done.3.cross, ...), custom_call_target="tpu_custom_call" | custom-call | tf_op jit(solution)/shard_map/last/pallas_call | solution.py:268
  (18 shorter events, 1.8 us)
Async XLA Ops:
  9.7 18.7 %collective-permute-start = (bf16[24,16,128]{2,1,0:T(8,128)(2,1)S(1)}, bf16[24,16,128]{2,1,0:T(8,128)(2,1)S(1)}, u32[]{:S(2)}, u32[]{:S(2)}) collective-permute-start(bf16[24,16,128]{2,1,0:T(8,128)(2,1)S(1)} %get-tuple-element.40), channel_id=1, source_target_pairs={{2,4},{5,9},{6,8},{7,11},{10,12},{13,17},{14,16},{15,19},{18,20},{... | collective-permute-start | bytes 294920 | tf_op jit(solution)/shard_map/ppermute | solution.py:233
  25.8 5.9 %copy-start = (s32[1,6,8]{2,0,1:T(1,128)S(1)}, s32[1,6,8]{2,0,1:T(1,128)}, u32[]{:S(2)}) copy-start(s32[1,6,8]{2,0,1:T(1,128)} %param.9) | copy-start | bytes 580
  35.2 11.8 %collective-permute-start.1 = (bf16[24,16,128]{2,1,0:T(8,128)(2,1)S(1)}, bf16[24,16,128]{2,1,0:T(8,128)(2,1)S(1)}, u32[]{:S(2)}, u32[]{:S(2)}) collective-permute-start(bf16[24,16,128]{2,1,0:T(8,128)(2,1)S(1)} %get-tuple-element.47), channel_id=1, source_target_pairs={{2,4},{5,9},{6,8},{7,11},{10,12},{13,17},{14,16},{15,19},{18,20},{... | collective-permute-start | bytes 294920 | tf_op jit(solution)/shard_map/ppermute | solution.py:233
  53.6 11.8 %collective-permute-start.2 = (bf16[24,16,128]{2,1,0:T(8,128)(2,1)S(1)}, bf16[24,16,128]{2,1,0:T(8,128)(2,1)S(1)}, u32[]{:S(2)}, u32[]{:S(2)}) collective-permute-start(bf16[24,16,128]{2,1,0:T(8,128)(2,1)S(1)} %get-tuple-element.52), channel_id=1, source_target_pairs={{2,4},{5,9},{6,8},{7,11},{10,12},{13,17},{14,16},{15,19},{18,20},{... | collective-permute-start | bytes 294920 | tf_op jit(solution)/shard_map/ppermute | solution.py:233
  72.0 11.8 %collective-permute-start.3 = (bf16[24,16,128]{2,1,0:T(8,128)(2,1)S(1)}, bf16[24,16,128]{2,1,0:T(8,128)(2,1)S(1)}, u32[]{:S(2)}, u32[]{:S(2)}) collective-permute-start(bf16[24,16,128]{2,1,0:T(8,128)(2,1)S(1)} %get-tuple-element.57), channel_id=1, source_target_pairs={{2,4},{5,9},{6,8},{7,11},{10,12},{13,17},{14,16},{15,19},{18,20},{... | collective-permute-start | bytes 294920 | tf_op jit(solution)/shard_map/ppermute | solution.py:233

commit v5 on v4

--- a/solution.py
+++ b/solution.py
@@ -69,12 +69,18 @@
 def first_kernel(*refs):
     sources, (x_out, mine_out, gift_out, base_out, scale_out, columns, offsets, lists, seeds, x, sems) = refs[:5], refs[5:]
     copies = []
-    for i, target in enumerate((seeds, scale_out, lists, columns, offsets)):
-        copies.append(pltpu.make_async_copy(sources[i], target, sems.at[i]))
-        copies[-1].start()
+    for i, target in enumerate((scale_out, lists, columns, offsets)):
+        copies.append(pltpu.make_async_copy(sources[i + 1], target, sems.at[i]))
+    for i in range(4):
+        part = pl.ds(i * RB * BLK // 4, RB * BLK // 4)
+        copies.append(pltpu.make_async_copy(sources[0].at[:, part], seeds.at[:, part], sems.at[i + 4]))
     for copy in copies:
+        copy.start()
+    for copy in copies[:4]:
         copy.wait()
     for r in range(RB):
+        if r % 8 == 0:
+            copies[4 + r // 8].wait()
         field = seeds[:, r * BLK : (r + 1) * BLK]
         base_out[r] = (1.0 - ALPHA) * field
         x[r] = (field * scale_out[r : r + 1, :]).astype(jnp.bfloat16)
@@ -126,7 +132,11 @@
 
 def step_kernel(last, index, lists_any, x_in, chip, cross, pair, side, base, scale, blocks, *rest):
     if last:
-        out, src = rest
+        out_hbm, src, out, sems = rest
+        parts = []
+        for i in range(4):
+            part = pl.ds(i * 8 * BLK, 8 * BLK)
+            parts.append(pltpu.make_async_copy(out.at[:, part], out_hbm.at[:, part], sems.at[i]))
     else:
         x_out, mine_out, gift_out, src, x, lists, sem = rest
         copy = pltpu.make_async_copy(lists_any, lists, sem)
@@ -139,16 +149,25 @@
     src[DIRECT:ZERO] = chip[other, 32:40]
     src[ZERO] = jnp.zeros((C, BLK), jnp.bfloat16)
     at = [index[s : s + 1, :] for s in range(4)]
-    for r in range(RB):
-        lhs = jnp.concatenate([src[at[s][0, r]] for s in range(4)], axis=1)
-        total = jnp.dot(lhs, blocks[r], preferred_element_type=jnp.float32)
-        s = scale[r : r + 1, :]
-        field = ALPHA * s * total + base[r]
-        if last:
-            out[:, r * BLK : (r + 1) * BLK] = field
-        else:
-            x[r] = (field * s).astype(jnp.bfloat16)
-    if not last:
+
+    @pl.when(other >= 0)
+    def _():
+        for r in range(RB):
+            lhs = jnp.concatenate([src[at[s][0, r]] for s in range(4)], axis=1)
+            total = jnp.dot(lhs, blocks[r], preferred_element_type=jnp.float32)
+            s = scale[r : r + 1, :]
+            field = ALPHA * s * total + base[r]
+            if last:
+                out[:, r * BLK : (r + 1) * BLK] = field
+                if r % 8 == 7:
+                    parts[r // 8].start()
+            else:
+                x[r] = (field * s).astype(jnp.bfloat16)
+
+    if last:
+        for part in parts:
+            part.wait()
+    else:
         x[RB] = jnp.zeros((C, BLK), jnp.bfloat16)
         x_out[...] = x[0:RB]
         copy.wait()
@@ -214,7 +233,7 @@
             pltpu.SMEM(lists.shape, jnp.int32),
             pltpu.VMEM(seeds.shape, jnp.float32),
             pltpu.VMEM((RB + 1, *score), jnp.bfloat16),
-            pltpu.SemaphoreType.DMA((5,)),
+            pltpu.SemaphoreType.DMA((8,)),
         ],
         name="first",
     )(*map(in_hbm, (seeds, deg_scale.reshape(RB, BLK), lists, col_index, row_offsets)))
@@ -259,7 +278,9 @@
         side = gather(owed, chips)
         last = step == ITERS - 1
         scratch = [pltpu.VMEM((ZERO + 1, *score), jnp.bfloat16)]
-        if not last:
+        if last:
+            scratch += [pltpu.VMEM(seeds.shape, jnp.float32), pltpu.SemaphoreType.DMA((4,))]
+        else:
             scratch += [
                 pltpu.VMEM((RB + 1, *score), jnp.bfloat16),
                 pltpu.SMEM(lists.shape, jnp.int32),
@@ -269,7 +290,7 @@
             functools.partial(step_kernel, last),
             out_shape=f32(*seeds.shape) if last else (bf16(RB, *score), bf16(32, *score), bf16(40, *score)),
             in_specs=[VMEM, ANY] + [VMEM] * 8,
-            out_specs=VMEM if last else (VMEM,) * 3,
+            out_specs=HBM if last else (VMEM,) * 3,
             scratch_shapes=scratch,
             name="last" if last else "late",
         )(index, lists, x, chip, cross, pair, side, base, scale, arranged)

time: 88.7 us -> 87.7 us (0.989)
  Pallas kernels: 9.57 us -> 8.41 us
    pallas_call x4, Pallas kernels: 5.49 us -> 4.3 us  [on_device(): call(functools.partial(step_kernel, last), out_shape=f32(*seeds.shape) if...]
where the time goes in v5:
time: 87.7 us; the launch traced here: 87.3 us
  blocking collectives  44.5 us (51%)
  starting transfers between devices  27.4 us (31%)
  Pallas kernels  8.41 us (10%)
  waiting for transfers between devices  6.42 us (7%)
    all_gather x12, blocking collectives, gather(): lax.all_gather(value, 'dom', axis=0, axis_index_groups=[list(g) for g in...  44.5 us
    ppermute x4, starting transfers between devices, on_device(): cross = lax.ppermute(cross, 'dom', crossing + [(b, a) for a, b in crossing])  27.4 us
    ppermute x4, waiting for transfers between devices, on_device(): cross = lax.ppermute(cross, 'dom', crossing + [(b, a) for a, b in crossing])  6.42 us
    pallas_call x4, Pallas kernels, on_device(): call(functools.partial(step_kernel, last), out_shape=f32(*seeds.shape) if...  4.3 us
    pallas_call x1, Pallas kernels, on_device(): call(arrange_kernel, out_shape=bf16(RB, 4 * BLK, BLK), in_specs=[ANY, HBM...  2.66 us
  transfers between devices with their start and end apart: 4, of which 3 were waited for; matrix products, arithmetic and copies ran while one was open for 0% of the time, Pallas kernels for 3%

profile of v5, /device:TPU:1, one launch (start us, length us, event | category | flops | bytes accessed | tf_op | source)
XLA Modules:
  0.0 87.3 jit_solution(6792336893517979877)
XLA Ops:
  0.0 1.2 %first.1 = (bf16[32,16,128]{2,1,0:T(8,128)(2,1)S(1)}, bf16[32,16,128]{2,1,0:T(8,128)(2,1)S(1)}, bf16[40,16,128]{2,1,0:T(8,128)(2,1)S(1)}, f32[32,16,128]{2,1,0:T...) custom-call(f32[16,4096]{1,0:T(8,128)} %refs_0_.1, f32[32,128]{1,0:T(8,128)} %bitcast.48, ...), custom_call_target="tpu_custom_call" | custom-call | tf_op jit(solution)/shard_map/first/pallas_call | solution.py:219
  1.2 8.6 %all-gather = bf16[80,16,128]{2,1,0:T(8,128)(2,1)S(1)} all-gather(bf16[40,16,128]{2,1,0:T(8,128)(2,1)S(1)} %get-tuple-element.33), channel_id=2, replica_groups={{0,1},{2,3},{4,5},{6,7},{8,9},{10,11},{12,13},{14,15},{16,17},{18,19},{..., dimensions={0}, use_global_device_ids=true | all-gather | bytes 491520 | tf_op jit(solution)/shard_map/all_gather | solution.py:212
  9.8 11.2 %collective-permute-start = (bf16[24,16,128]{2,1,0:T(8,128)(2,1)S(1)}, bf16[24,16,128]{2,1,0:T(8,128)(2,1)S(1)}, u32[]{:S(2)}, u32[]{:S(2)}) collective-permute-start(bf16[24,16,128]{2,1,0:T(8,128)(2,1)S(1)} %get-tuple-element.40), channel_id=1, source_target_pairs={{2,4},{5,9},{6,8},{7,11},{10,12},{13,17},{14,16},{15,19},{18,20},{... | collective-permute-start | bytes 294920 | tf_op jit(solution)/shard_map/ppermute | solution.py:252
  21.0 4.4 %all-gather.1 = bf16[48,16,128]{2,1,0:T(8,128)(2,1)S(1)} all-gather(bf16[24,16,128]{2,1,0:T(8,128)(2,1)S(1)} %get-tuple-element.34), channel_id=3, replica_groups={{1,3},{0,4},{2,6},{5,7},{9,11},{8,12},{10,14},{13,15},{17,19},{16,20},{..., dimensions={0}, use_global_device_ids=true | all-gather | bytes 294912 | tf_op jit(solution)/shard_map/all_gather | solution.py:212
  25.8 2.7 %arrange.1.blocks = bf16[32,512,128]{2,1,0:T(8,128)(2,1)S(1)} custom-call(s32[1,33]{1,0:T(1,128)S(1)} %get-tuple-element.37.offsets_any, bf16[128,128,128]{2,1,0:T(8,128)(2,1)} %blocks_hbm.1), custom_call_target="tpu_custom_call" | custom-call | bytes 16777216 | tf_op jit(solution)/shard_map/arrange/pallas_call | solution.py:257
  28.5 3.2 %all-gather.2 = bf16[48,16,128]{2,1,0:T(8,128)(2,1)S(1)} all-gather(bf16[24,16,128]{2,1,0:T(8,128)(2,1)S(1)} %owe.4), channel_id=4, replica_groups={{0,1},{2,3},{4,5},{6,7},{8,9},{10,11},{12,13},{14,15},{16,17},{18,19},{..., dimensions={0}, use_global_device_ids=true | all-gather | bytes 294912 | tf_op jit(solution)/shard_map/all_gather | solution.py:212
  31.7 0.9 %late.3 = (bf16[32,16,128]{2,1,0:T(8,128)(2,1)S(1)}, bf16[32,16,128]{2,1,0:T(8,128)(2,1)S(1)}, bf16[40,16,128]{2,1,0:T(8,128)(2,1)S(1)}) custom-call(s32[4,32]{1,0:T(4,128)S(1)} %broadcast_add_fusion.index, s32[6,1,8]{2,1,0:T(1,128)S(1)} %bitcast.44, bf16[32,16,128]{2,1,0:T(8,128)(2,1)S(1)} %get-tuple-element.39.x_in, bf16[2,40,16,128]{3,2,1,0:T(8,128)(2,1)S(1)} %bitcast.24, ...), custom_call_target="tpu_custom_call" | custom-call | tf_op jit(solution)/shard_map/late/pallas_call | solution.py:289
  32.7 2.0 %all-gather.3 = bf16[80,16,128]{2,1,0:T(8,128)(2,1)S(1)} all-gather(bf16[40,16,128]{2,1,0:T(8,128)(2,1)S(1)} %get-tuple-element.45), channel_id=5, replica_groups={{0,1},{2,3},{4,5},{6,7},{8,9},{10,11},{12,13},{14,15},{16,17},{18,19},{..., dimensions={0}, use_global_device_ids=true | all-gather | bytes 491520 | tf_op jit(solution)/shard_map/all_gather | solution.py:212
  34.8 4.9 %collective-permute-start.1 = (bf16[24,16,128]{2,1,0:T(8,128)(2,1)S(1)}, bf16[24,16,128]{2,1,0:T(8,128)(2,1)S(1)}, u32[]{:S(2)}, u32[]{:S(2)}) collective-permute-start(bf16[24,16,128]{2,1,0:T(8,128)(2,1)S(1)} %get-tuple-element.47), channel_id=1, source_target_pairs={{2,4},{5,9},{6,8},{7,11},{10,12},{13,17},{14,16},{15,19},{18,20},{... | collective-permute-start | bytes 294920 | tf_op jit(solution)/shard_map/ppermute | solution.py:252
  39.7 4.1 %all-gather.4 = bf16[48,16,128]{2,1,0:T(8,128)(2,1)S(1)} all-gather(bf16[24,16,128]{2,1,0:T(8,128)(2,1)S(1)} %get-tuple-element.48), channel_id=6, replica_groups={{1,3},{0,4},{2,6},{5,7},{9,11},{8,12},{10,14},{13,15},{17,19},{16,20},{..., dimensions={0}, use_global_device_ids=true | all-gather | bytes 294912 | tf_op jit(solution)/shard_map/all_gather | solution.py:212
  43.9 2.7 %collective-permute-done.1.cross = bf16[24,16,128]{2,1,0:T(8,128)(2,1)S(1)} collective-permute-done((bf16[24,16,128]{2,1,0:T(8,128)(2,1)S(1)}, bf16[24,16,128]{2,1,0:T(8,128)(2,1)S(1)}, u32[]{:S(2)}, u32[]{:S(2)}) %collective-permute-start.1) | collective-permute-done | bytes 98336 | tf_op jit(solution)/shard_map/ppermute | solution.py:252
  46.6 3.1 %all-gather.5 = bf16[48,16,128]{2,1,0:T(8,128)(2,1)S(1)} all-gather(bf16[24,16,128]{2,1,0:T(8,128)(2,1)S(1)} %owe.5), channel_id=7, replica_groups={{0,1},{2,3},{4,5},{6,7},{8,9},{10,11},{12,13},{14,15},{16,17},{18,19},{..., dimensions={0}, use_global_device_ids=true | all-gather | bytes 294912 | tf_op jit(solution)/shard_map/all_gather | solution.py:212
  49.8 0.9 %late.4 = (bf16[32,16,128]{2,1,0:T(8,128)(2,1)S(1)}, bf16[32,16,128]{2,1,0:T(8,128)(2,1)S(1)}, bf16[40,16,128]{2,1,0:T(8,128)(2,1)S(1)}) custom-call(s32[4,32]{1,0:T(4,128)S(1)} %broadcast_add_fusion.index, s32[6,1,8]{2,1,0:T(1,128)S(1)} %bitcast.45, bf16[32,16,128]{2,1,0:T(8,128)(2,1)S(1)} %get-tuple-element.44.x_in, bf16[2,40,16,128]{3,2,1,0:T(8,128)(2,1)S(1)} %bitcast.26, ...), custom_call_target="tpu_custom_call" | custom-call | tf_op jit(solution)/shard_map/late/pallas_call | solution.py:289
  50.7 2.0 %all-gather.6 = bf16[80,16,128]{2,1,0:T(8,128)(2,1)S(1)} all-gather(bf16[40,16,128]{2,1,0:T(8,128)(2,1)S(1)} %get-tuple-element.50), channel_id=8, replica_groups={{0,1},{2,3},{4,5},{6,7},{8,9},{10,11},{12,13},{14,15},{16,17},{18,19},{..., dimensions={0}, use_global_device_ids=true | all-gather | bytes 491520 | tf_op jit(solution)/shard_map/all_gather | solution.py:212
  52.8 5.5 %collective-permute-start.2 = (bf16[24,16,128]{2,1,0:T(8,128)(2,1)S(1)}, bf16[24,16,128]{2,1,0:T(8,128)(2,1)S(1)}, u32[]{:S(2)}, u32[]{:S(2)}) collective-permute-start(bf16[24,16,128]{2,1,0:T(8,128)(2,1)S(1)} %get-tuple-element.52), channel_id=1, source_target_pairs={{2,4},{5,9},{6,8},{7,11},{10,12},{13,17},{14,16},{15,19},{18,20},{... | collective-permute-start | bytes 294920 | tf_op jit(solution)/shard_map/ppermute | solution.py:252
  58.3 4.1 %all-gather.7 = bf16[48,16,128]{2,1,0:T(8,128)(2,1)S(1)} all-gather(bf16[24,16,128]{2,1,0:T(8,128)(2,1)S(1)} %get-tuple-element.53), channel_id=9, replica_groups={{1,3},{0,4},{2,6},{5,7},{9,11},{8,12},{10,14},{13,15},{17,19},{16,20},{..., dimensions={0}, use_global_device_ids=true | all-gather | bytes 294912 | tf_op jit(solution)/shard_map/all_gather | solution.py:212
  62.4 2.2 %collective-permute-done.2.cross = bf16[24,16,128]{2,1,0:T(8,128)(2,1)S(1)} collective-permute-done((bf16[24,16,128]{2,1,0:T(8,128)(2,1)S(1)}, bf16[24,16,128]{2,1,0:T(8,128)(2,1)S(1)}, u32[]{:S(2)}, u32[]{:S(2)}) %collective-permute-start.2) | collective-permute-done | bytes 98336 | tf_op jit(solution)/shard_map/ppermute | solution.py:252
  64.6 3.1 %all-gather.8 = bf16[48,16,128]{2,1,0:T(8,128)(2,1)S(1)} all-gather(bf16[24,16,128]{2,1,0:T(8,128)(2,1)S(1)} %owe.6), channel_id=10, replica_groups={{0,1},{2,3},{4,5},{6,7},{8,9},{10,11},{12,13},{14,15},{16,17},{18,19},{..., dimensions={0}, use_global_device_ids=true | all-gather | bytes 294912 | tf_op jit(solution)/shard_map/all_gather | solution.py:212
  68.7 2.0 %all-gather.9 = bf16[80,16,128]{2,1,0:T(8,128)(2,1)S(1)} all-gather(bf16[40,16,128]{2,1,0:T(8,128)(2,1)S(1)} %get-tuple-element.55), channel_id=11, replica_groups={{0,1},{2,3},{4,5},{6,7},{8,9},{10,11},{12,13},{14,15},{16,17},{18,19},{..., dimensions={0}, use_global_device_ids=true | all-gather | bytes 491520 | tf_op jit(solution)/shard_map/all_gather | solution.py:212
  70.8 5.8 %collective-permute-start.3 = (bf16[24,16,128]{2,1,0:T(8,128)(2,1)S(1)}, bf16[24,16,128]{2,1,0:T(8,128)(2,1)S(1)}, u32[]{:S(2)}, u32[]{:S(2)}) collective-permute-start(bf16[24,16,128]{2,1,0:T(8,128)(2,1)S(1)} %get-tuple-element.57), channel_id=1, source_target_pairs={{2,4},{5,9},{6,8},{7,11},{10,12},{13,17},{14,16},{15,19},{18,20},{... | collective-permute-start | bytes 294920 | tf_op jit(solution)/shard_map/ppermute | solution.py:252
  76.6 4.5 %all-gather.10 = bf16[48,16,128]{2,1,0:T(8,128)(2,1)S(1)} all-gather(bf16[24,16,128]{2,1,0:T(8,128)(2,1)S(1)} %get-tuple-element.58), channel_id=12, replica_groups={{1,3},{0,4},{2,6},{5,7},{9,11},{8,12},{10,14},{13,15},{17,19},{16,20},{..., dimensions={0}, use_global_device_ids=true | all-gather | bytes 294912 | tf_op jit(solution)/shard_map/all_gather | solution.py:212
  81.1 1.5 %collective-permute-done.3.cross = bf16[24,16,128]{2,1,0:T(8,128)(2,1)S(1)} collective-permute-done((bf16[24,16,128]{2,1,0:T(8,128)(2,1)S(1)}, bf16[24,16,128]{2,1,0:T(8,128)(2,1)S(1)}, u32[]{:S(2)}, u32[]{:S(2)}) %collective-permute-start.3) | collective-permute-done | bytes 98336 | tf_op jit(solution)/shard_map/ppermute | solution.py:252
  82.6 3.1 %all-gather.11 = bf16[48,16,128]{2,1,0:T(8,128)(2,1)S(1)} all-gather(bf16[24,16,128]{2,1,0:T(8,128)(2,1)S(1)} %owe.7), channel_id=13, replica_groups={{0,1},{2,3},{4,5},{6,7},{8,9},{10,11},{12,13},{14,15},{16,17},{18,19},{..., dimensions={0}, use_global_device_ids=true | all-gather | bytes 294912 | tf_op jit(solution)/shard_map/all_gather | solution.py:212
  85.8 1.5 %last.1 = f32[16,4096]{1,0:T(8,128)} custom-call(s32[4,32]{1,0:T(4,128)S(1)} %broadcast_add_fusion.index, s32[6,1,8]{2,1,0:T(1,128)S(1)} %bitcast.47, bf16[32,16,128]{2,1,0:T(8,128)(2,1)S(1)} %get-tuple-element.54.x_in, bf16[2,40,16,128]{3,2,1,0:T(8,128)(2,1)S(1)} %bitcast.30, bf16[24,16,128]{2,1,0:T(8,128)(2,1)S(1)} %collective-permute-done.3.cross, ...), custom_call_target="tpu_custom_call" | custom-call | tf_op jit(solution)/shard_map/last/pallas_call | solution.py:289
  (18 shorter events, 1.6 us)
Async XLA Ops:
  9.8 18.7 %collective-permute-start = (bf16[24,16,128]{2,1,0:T(8,128)(2,1)S(1)}, bf16[24,16,128]{2,1,0:T(8,128)(2,1)S(1)}, u32[]{:S(2)}, u32[]{:S(2)}) collective-permute-start(bf16[24,16,128]{2,1,0:T(8,128)(2,1)S(1)} %get-tuple-element.40), channel_id=1, source_target_pairs={{2,4},{5,9},{6,8},{7,11},{10,12},{13,17},{14,16},{15,19},{18,20},{... | collective-permute-start | bytes 294920 | tf_op jit(solution)/shard_map/ppermute | solution.py:252
  25.8 5.9 %copy-start = (s32[1,6,8]{2,0,1:T(1,128)S(1)}, s32[1,6,8]{2,0,1:T(1,128)}, u32[]{:S(2)}) copy-start(s32[1,6,8]{2,0,1:T(1,128)} %param.9) | copy-start | bytes 580
  34.8 11.8 %collective-permute-start.1 = (bf16[24,16,128]{2,1,0:T(8,128)(2,1)S(1)}, bf16[24,16,128]{2,1,0:T(8,128)(2,1)S(1)}, u32[]{:S(2)}, u32[]{:S(2)}) collective-permute-start(bf16[24,16,128]{2,1,0:T(8,128)(2,1)S(1)} %get-tuple-element.47), channel_id=1, source_target_pairs={{2,4},{5,9},{6,8},{7,11},{10,12},{13,17},{14,16},{15,19},{18,20},{... | collective-permute-start | bytes 294920 | tf_op jit(solution)/shard_map/ppermute | solution.py:252
  52.8 11.8 %collective-permute-start.2 = (bf16[24,16,128]{2,1,0:T(8,128)(2,1)S(1)}, bf16[24,16,128]{2,1,0:T(8,128)(2,1)S(1)}, u32[]{:S(2)}, u32[]{:S(2)}) collective-permute-start(bf16[24,16,128]{2,1,0:T(8,128)(2,1)S(1)} %get-tuple-element.52), channel_id=1, source_target_pairs={{2,4},{5,9},{6,8},{7,11},{10,12},{13,17},{14,16},{15,19},{18,20},{... | collective-permute-start | bytes 294920 | tf_op jit(solution)/shard_map/ppermute | solution.py:252
  70.8 11.8 %collective-permute-start.3 = (bf16[24,16,128]{2,1,0:T(8,128)(2,1)S(1)}, bf16[24,16,128]{2,1,0:T(8,128)(2,1)S(1)}, u32[]{:S(2)}, u32[]{:S(2)}) collective-permute-start(bf16[24,16,128]{2,1,0:T(8,128)(2,1)S(1)} %get-tuple-element.57), channel_id=1, source_target_pairs={{2,4},{5,9},{6,8},{7,11},{10,12},{13,17},{14,16},{15,19},{18,20},{... | collective-permute-start | bytes 294920 | tf_op jit(solution)/shard_map/ppermute | solution.py:252

commit v6 on v5

--- a/solution.py
+++ b/solution.py
@@ -66,8 +66,35 @@
                 out[at * HB + h] = x[block]
 
 
+def places(columns, offsets):
+    k, up1, up2 = role()
+    sel = jnp.where
+    first = k == 0
+    near, far = sel(first, SENT, PAIR), sel(first, PAIR, SENT)
+    base = [
+        sel(first, sel(up1, SIDE + 8, near + 16), DIRECT),
+        sel(first, DIRECT, sel(up1, near + 8, SIDE)),
+        sel(up1, SIDE, sel(first, near + 8, near + 16)),
+        sel(up1, near + 16, sel(first, SIDE, SIDE + 8)),
+        sel(up2, SIDE + 16, far + 8),
+        sel(up2, far + 8, SIDE + 16),
+    ]
+    where = columns
+    for j in range(6):
+        where = sel((columns - RB) >> 3 == j, base[j] + ((columns - RB) & (HB - 1)), where)
+    where = jnp.broadcast_to((where - ZERO).astype(jnp.float32), (8, BLK)).astype(jnp.bfloat16)
+    start, end = offsets[:, :RB], offsets[:, 1:]
+    slots = lax.broadcasted_iota(jnp.int32, (BLK, RB), 0)
+    rows = []
+    for s in range(4):
+        pick = sel((slots == start + s) & (slots < end), 1.0, 0.0).astype(jnp.bfloat16)
+        rows.append(jnp.dot(where, pick, preferred_element_type=jnp.float32)[0:1].astype(jnp.int32) + ZERO)
+    return rows
+
+
 def first_kernel(*refs):
-    sources, (x_out, mine_out, gift_out, base_out, scale_out, columns, offsets, lists, seeds, x, sems) = refs[:5], refs[5:]
+    sources, (x_out, mine_out, gift_out, base_out, scale_out, index_out) = refs[:5], refs[5:11]
+    lists, columns, offsets, seeds, x, sems = refs[11:]
     copies = []
     for i, target in enumerate((scale_out, lists, columns, offsets)):
         copies.append(pltpu.make_async_copy(sources[i + 1], target, sems.at[i]))
@@ -78,6 +105,8 @@
         copy.start()
     for copy in copies[:4]:
         copy.wait()
+    for s, row in enumerate(places(columns[...], offsets[...])):
+        index_out[s : s + 1, :] = row
     for r in range(RB):
         if r % 8 == 0:
             copies[4 + r // 8].wait()
@@ -174,28 +203,6 @@
         pack(lists, x, mine_out, gift_out)
 
 
-def indices(columns, offsets):
-    k, up1, up2 = role()
-    sel = jnp.where
-    first = k == 0
-    near, far = sel(first, SENT, PAIR), sel(first, PAIR, SENT)
-    base = [
-        sel(first, sel(up1, SIDE + 8, near + 16), DIRECT),
-        sel(first, DIRECT, sel(up1, near + 8, SIDE)),
-        sel(up1, SIDE, sel(first, near + 8, near + 16)),
-        sel(up1, near + 16, sel(first, SIDE, SIDE + 8)),
-        sel(up2, SIDE + 16, far + 8),
-        sel(up2, far + 8, SIDE + 16),
-    ]
-    where = columns
-    for j in range(6):
-        where = sel((columns - RB) >> 3 == j, base[j] + ((columns - RB) & (HB - 1)), where)
-    slots = jnp.arange(BLK, dtype=jnp.int32)
-    at = offsets[None, :RB] + jnp.arange(4, dtype=jnp.int32)[:, None]
-    pick = (at[:, :, None] == slots) & (at < offsets[None, 1:])[:, :, None]
-    return (jnp.sum(sel(pick, where - ZERO, 0), axis=2) + ZERO).astype(jnp.int32)
-
-
 def on_device(count, blocks, col_index, row_offsets, send_index, deg_scale, seeds):
     chips = [[2 * c, 2 * c + 1] for c in range(count // 2)]
 
@@ -216,7 +223,7 @@
     lists = jnp.transpose(send_index, (1, 0, 2))
     score = (C, BLK)
 
-    x, mine, gift, base, scale, columns, offsets = call(
+    x, mine, gift, base, scale, index = call(
         first_kernel,
         out_shape=(
             bf16(RB, *score),
@@ -224,20 +231,21 @@
             bf16(40, *score),
             f32(RB, *score),
             f32(RB, BLK),
-            jax.ShapeDtypeStruct(col_index.shape, jnp.int32),
-            jax.ShapeDtypeStruct(row_offsets.shape, jnp.int32),
+            jax.ShapeDtypeStruct((4, RB), jnp.int32),
         ),
         in_specs=[HBM] * 5,
-        out_specs=(VMEM,) * 7,
+        out_specs=(VMEM,) * 6,
         scratch_shapes=[
             pltpu.SMEM(lists.shape, jnp.int32),
+            pltpu.VMEM(col_index.shape, jnp.int32),
+            pltpu.VMEM(row_offsets.shape, jnp.int32),
             pltpu.VMEM(seeds.shape, jnp.float32),
             pltpu.VMEM((RB + 1, *score), jnp.bfloat16),
             pltpu.SemaphoreType.DMA((8,)),
         ],
         name="first",
     )(*map(in_hbm, (seeds, deg_scale.reshape(RB, BLK), lists, col_index, row_offsets)))
-    index = arranged = None
+    arranged = None
     for step in range(ITERS):
         chip = gather(gift, chips)
         cross, inner = call(
@@ -252,12 +260,11 @@
         cross = lax.ppermute(cross, "dom", crossing + [(b, a) for a, b in crossing])
         pair = gather(inner, pairs(0))
         if arranged is None:
-            pair, offsets, columns = lax.optimization_barrier((pair, offsets, columns))
-            index = indices(columns[0], offsets[0])
+            pair, row_offsets = lax.optimization_barrier((pair, row_offsets))
             arranged = call(
                 arrange_kernel,
                 out_shape=bf16(RB, 4 * BLK, BLK),
-                in_specs=[ANY, HBM],
+                in_specs=[HBM, HBM],
                 out_specs=VMEM,
                 scratch_shapes=[
                     pltpu.SMEM(row_offsets.shape, jnp.int32),
@@ -266,7 +273,7 @@
                 ],
                 cost_estimate=pl.CostEstimate(flops=0, bytes_accessed=16 << 20, transcendentals=0),
                 name="arrange",
-            )(offsets, in_hbm(blocks))
+            )(in_hbm(row_offsets), in_hbm(blocks))
         owed = call(
             owe_kernel,
             out_shape=bf16(24, *score),

time: 87.7 us -> 87.4 us (level)
  waiting for transfers between devices: 6.42 us -> 4.58 us
  starting transfers between devices: 27.4 us -> 28.6 us
    ppermute x4, waiting for transfers between devices: 6.42 us -> 4.58 us  [on_device(): cross = lax.ppermute(cross, 'dom', crossing + [(b, a) for a, b in crossing])]
    ppermute x4, starting transfers between devices: 27.4 us -> 28.6 us  [on_device(): cross = lax.ppermute(cross, 'dom', crossing + [(b, a) for a, b in crossing])]
where the time goes in v6:
time: 87.4 us; the launch traced here: 86.9 us
  blocking collectives  45.1 us (52%)
  starting transfers between devices  28.6 us (33%)
  Pallas kernels  8.5 us (10%)
  waiting for transfers between devices  4.58 us (5%)
    all_gather x12, blocking collectives, gather(): lax.all_gather(value, 'dom', axis=0, axis_index_groups=[list(g) for g in...  45.1 us
    ppermute x4, starting transfers between devices, on_device(): cross = lax.ppermute(cross, 'dom', crossing + [(b, a) for a, b in crossing])  28.6 us
    ppermute x4, waiting for transfers between devices, on_device(): cross = lax.ppermute(cross, 'dom', crossing + [(b, a) for a, b in crossing])  4.58 us
    pallas_call x4, Pallas kernels, on_device(): call(functools.partial(step_kernel, last), out_shape=f32(*seeds.shape) if...  4.26 us
    pallas_call x1, Pallas kernels, on_device(): call(arrange_kernel, out_shape=bf16(RB, 4 * BLK, BLK), in_specs=[HBM, HBM...  2.67 us
  transfers between devices with their start and end apart: 4, of which 3 were waited for; matrix products, arithmetic and copies ran while one was open for 0% of the time, Pallas kernels for 3%

profile of v6, /device:TPU:1, one launch (start us, length us, event | category | flops | bytes accessed | tf_op | source)
XLA Modules:
  0.0 86.9 jit_solution(16032535603999100416)
XLA Ops:
  0.0 1.3 %first.1 = (bf16[32,16,128]{2,1,0:T(8,128)(2,1)S(1)}, bf16[32,16,128]{2,1,0:T(8,128)(2,1)S(1)}, bf16[40,16,128]{2,1,0:T(8,128)(2,1)S(1)}, f32[32,16,128]{2,1,0:T...) custom-call(f32[16,4096]{1,0:T(8,128)} %refs_0_.1, f32[32,128]{1,0:T(8,128)} %bitcast.39, s32[6,1,8]{2,1,0:T(1,128)} %bitcast.34, ...), custom_call_target="tpu_custom_call" | custom-call | tf_op jit(solution)/shard_map/first/pallas_call | solution.py:226
  1.3 8.6 %all-gather = bf16[80,16,128]{2,1,0:T(8,128)(2,1)S(1)} all-gather(bf16[40,16,128]{2,1,0:T(8,128)(2,1)S(1)} %get-tuple-element.32), channel_id=2, replica_groups={{0,1},{2,3},{4,5},{6,7},{8,9},{10,11},{12,13},{14,15},{16,17},{18,19},{..., dimensions={0}, use_global_device_ids=true | all-gather | bytes 491520 | tf_op jit(solution)/shard_map/all_gather | solution.py:219
  9.9 11.2 %collective-permute-start = (bf16[24,16,128]{2,1,0:T(8,128)(2,1)S(1)}, bf16[24,16,128]{2,1,0:T(8,128)(2,1)S(1)}, u32[]{:S(2)}, u32[]{:S(2)}) collective-permute-start(bf16[24,16,128]{2,1,0:T(8,128)(2,1)S(1)} %get-tuple-element.34), channel_id=1, source_target_pairs={{2,4},{5,9},{6,8},{7,11},{10,12},{13,17},{14,16},{15,19},{18,20},{... | collective-permute-start | bytes 294920 | tf_op jit(solution)/shard_map/ppermute | solution.py:260
  21.1 4.4 %all-gather.1 = bf16[48,16,128]{2,1,0:T(8,128)(2,1)S(1)} all-gather(bf16[24,16,128]{2,1,0:T(8,128)(2,1)S(1)} %get-tuple-element.35), channel_id=3, replica_groups={{1,3},{0,4},{2,6},{5,7},{9,11},{8,12},{10,14},{13,15},{17,19},{16,20},{..., dimensions={0}, use_global_device_ids=true | all-gather | bytes 294912 | tf_op jit(solution)/shard_map/all_gather | solution.py:219
  25.5 2.7 %arrange.1.blocks = bf16[32,512,128]{2,1,0:T(8,128)(2,1)S(1)} custom-call(s32[1,33]{1,0:T(1,128)} %offsets_any, bf16[128,128,128]{2,1,0:T(8,128)(2,1)} %blocks_hbm.1), custom_call_target="tpu_custom_call" | custom-call | bytes 16777216 | tf_op jit(solution)/shard_map/arrange/pallas_call | solution.py:264
  28.2 3.2 %all-gather.2 = bf16[48,16,128]{2,1,0:T(8,128)(2,1)S(1)} all-gather(bf16[24,16,128]{2,1,0:T(8,128)(2,1)S(1)} %owe.4), channel_id=4, replica_groups={{0,1},{2,3},{4,5},{6,7},{8,9},{10,11},{12,13},{14,15},{16,17},{18,19},{..., dimensions={0}, use_global_device_ids=true | all-gather | bytes 294912 | tf_op jit(solution)/shard_map/all_gather | solution.py:219
  32.4 2.0 %all-gather.3 = bf16[80,16,128]{2,1,0:T(8,128)(2,1)S(1)} all-gather(bf16[40,16,128]{2,1,0:T(8,128)(2,1)S(1)} %get-tuple-element.41), channel_id=5, replica_groups={{0,1},{2,3},{4,5},{6,7},{8,9},{10,11},{12,13},{14,15},{16,17},{18,19},{..., dimensions={0}, use_global_device_ids=true | all-gather | bytes 491520 | tf_op jit(solution)/shard_map/all_gather | solution.py:219
  34.5 5.4 %collective-permute-start.1 = (bf16[24,16,128]{2,1,0:T(8,128)(2,1)S(1)}, bf16[24,16,128]{2,1,0:T(8,128)(2,1)S(1)}, u32[]{:S(2)}, u32[]{:S(2)}) collective-permute-start(bf16[24,16,128]{2,1,0:T(8,128)(2,1)S(1)} %get-tuple-element.43), channel_id=1, source_target_pairs={{2,4},{5,9},{6,8},{7,11},{10,12},{13,17},{14,16},{15,19},{18,20},{... | collective-permute-start | bytes 294920 | tf_op jit(solution)/shard_map/ppermute | solution.py:260
  39.9 4.1 %all-gather.4 = bf16[48,16,128]{2,1,0:T(8,128)(2,1)S(1)} all-gather(bf16[24,16,128]{2,1,0:T(8,128)(2,1)S(1)} %get-tuple-element.44), channel_id=6, replica_groups={{1,3},{0,4},{2,6},{5,7},{9,11},{8,12},{10,14},{13,15},{17,19},{16,20},{..., dimensions={0}, use_global_device_ids=true | all-gather | bytes 294912 | tf_op jit(solution)/shard_map/all_gather | solution.py:219
  44.0 2.3 %collective-permute-done.1.cross = bf16[24,16,128]{2,1,0:T(8,128)(2,1)S(1)} collective-permute-done((bf16[24,16,128]{2,1,0:T(8,128)(2,1)S(1)}, bf16[24,16,128]{2,1,0:T(8,128)(2,1)S(1)}, u32[]{:S(2)}, u32[]{:S(2)}) %collective-permute-start.1) | collective-permute-done | bytes 98336 | tf_op jit(solution)/shard_map/ppermute | solution.py:260
  46.3 3.1 %all-gather.5 = bf16[48,16,128]{2,1,0:T(8,128)(2,1)S(1)} all-gather(bf16[24,16,128]{2,1,0:T(8,128)(2,1)S(1)} %owe.5), channel_id=7, replica_groups={{0,1},{2,3},{4,5},{6,7},{8,9},{10,11},{12,13},{14,15},{16,17},{18,19},{..., dimensions={0}, use_global_device_ids=true | all-gather | bytes 294912 | tf_op jit(solution)/shard_map/all_gather | solution.py:219
  49.5 0.9 %late.4 = (bf16[32,16,128]{2,1,0:T(8,128)(2,1)S(1)}, bf16[32,16,128]{2,1,0:T(8,128)(2,1)S(1)}, bf16[40,16,128]{2,1,0:T(8,128)(2,1)S(1)}) custom-call(s32[4,32]{1,0:T(4,128)S(1)} %get-tuple-element.30.index, s32[6,1,8]{2,1,0:T(1,128)S(1)} %bitcast.36, bf16[32,16,128]{2,1,0:T(8,128)(2,1)S(1)} %get-tuple-element.40.x_in, bf16[2,40,16,128]{3,2,1,0:T(8,128)(2,1)S(1)} %bitcast.17, ...), custom_call_target="tpu_custom_call" | custom-call | tf_op jit(solution)/shard_map/late/pallas_call | solution.py:296
  50.4 2.0 %all-gather.6 = bf16[80,16,128]{2,1,0:T(8,128)(2,1)S(1)} all-gather(bf16[40,16,128]{2,1,0:T(8,128)(2,1)S(1)} %get-tuple-element.46), channel_id=8, replica_groups={{0,1},{2,3},{4,5},{6,7},{8,9},{10,11},{12,13},{14,15},{16,17},{18,19},{..., dimensions={0}, use_global_device_ids=true | all-gather | bytes 491520 | tf_op jit(solution)/shard_map/all_gather | solution.py:219
  52.5 5.9 %collective-permute-start.2 = (bf16[24,16,128]{2,1,0:T(8,128)(2,1)S(1)}, bf16[24,16,128]{2,1,0:T(8,128)(2,1)S(1)}, u32[]{:S(2)}, u32[]{:S(2)}) collective-permute-start(bf16[24,16,128]{2,1,0:T(8,128)(2,1)S(1)} %get-tuple-element.48), channel_id=1, source_target_pairs={{2,4},{5,9},{6,8},{7,11},{10,12},{13,17},{14,16},{15,19},{18,20},{... | collective-permute-start | bytes 294920 | tf_op jit(solution)/shard_map/ppermute | solution.py:260
  58.4 4.8 %all-gather.7 = bf16[48,16,128]{2,1,0:T(8,128)(2,1)S(1)} all-gather(bf16[24,16,128]{2,1,0:T(8,128)(2,1)S(1)} %get-tuple-element.49), channel_id=9, replica_groups={{1,3},{0,4},{2,6},{5,7},{9,11},{8,12},{10,14},{13,15},{17,19},{16,20},{..., dimensions={0}, use_global_device_ids=true | all-gather | bytes 294912 | tf_op jit(solution)/shard_map/all_gather | solution.py:219
  63.1 1.2 %collective-permute-done.2.cross = bf16[24,16,128]{2,1,0:T(8,128)(2,1)S(1)} collective-permute-done((bf16[24,16,128]{2,1,0:T(8,128)(2,1)S(1)}, bf16[24,16,128]{2,1,0:T(8,128)(2,1)S(1)}, u32[]{:S(2)}, u32[]{:S(2)}) %collective-permute-start.2) | collective-permute-done | bytes 98336 | tf_op jit(solution)/shard_map/ppermute | solution.py:260
  64.3 3.1 %all-gather.8 = bf16[48,16,128]{2,1,0:T(8,128)(2,1)S(1)} all-gather(bf16[24,16,128]{2,1,0:T(8,128)(2,1)S(1)} %owe.6), channel_id=10, replica_groups={{0,1},{2,3},{4,5},{6,7},{8,9},{10,11},{12,13},{14,15},{16,17},{18,19},{..., dimensions={0}, use_global_device_ids=true | all-gather | bytes 294912 | tf_op jit(solution)/shard_map/all_gather | solution.py:219
  67.5 0.9 %late.5 = (bf16[32,16,128]{2,1,0:T(8,128)(2,1)S(1)}, bf16[32,16,128]{2,1,0:T(8,128)(2,1)S(1)}, bf16[40,16,128]{2,1,0:T(8,128)(2,1)S(1)}) custom-call(s32[4,32]{1,0:T(4,128)S(1)} %get-tuple-element.30.index, s32[6,1,8]{2,1,0:T(1,128)S(1)} %bitcast.37, bf16[32,16,128]{2,1,0:T(8,128)(2,1)S(1)} %get-tuple-element.45.x_in, bf16[2,40,16,128]{3,2,1,0:T(8,128)(2,1)S(1)} %bitcast.19, ...), custom_call_target="tpu_custom_call" | custom-call | tf_op jit(solution)/shard_map/late/pallas_call | solution.py:296
  68.4 2.0 %all-gather.9 = bf16[80,16,128]{2,1,0:T(8,128)(2,1)S(1)} all-gather(bf16[40,16,128]{2,1,0:T(8,128)(2,1)S(1)} %get-tuple-element.51), channel_id=11, replica_groups={{0,1},{2,3},{4,5},{6,7},{8,9},{10,11},{12,13},{14,15},{16,17},{18,19},{..., dimensions={0}, use_global_device_ids=true | all-gather | bytes 491520 | tf_op jit(solution)/shard_map/all_gather | solution.py:219
  70.5 6.2 %collective-permute-start.3 = (bf16[24,16,128]{2,1,0:T(8,128)(2,1)S(1)}, bf16[24,16,128]{2,1,0:T(8,128)(2,1)S(1)}, u32[]{:S(2)}, u32[]{:S(2)}) collective-permute-start(bf16[24,16,128]{2,1,0:T(8,128)(2,1)S(1)} %get-tuple-element.53), channel_id=1, source_target_pairs={{2,4},{5,9},{6,8},{7,11},{10,12},{13,17},{14,16},{15,19},{18,20},{... | collective-permute-start | bytes 294920 | tf_op jit(solution)/shard_map/ppermute | solution.py:260
  76.7 4.5 %all-gather.10 = bf16[48,16,128]{2,1,0:T(8,128)(2,1)S(1)} all-gather(bf16[24,16,128]{2,1,0:T(8,128)(2,1)S(1)} %get-tuple-element.54), channel_id=12, replica_groups={{1,3},{0,4},{2,6},{5,7},{9,11},{8,12},{10,14},{13,15},{17,19},{16,20},{..., dimensions={0}, use_global_device_ids=true | all-gather | bytes 294912 | tf_op jit(solution)/shard_map/all_gather | solution.py:219
  81.2 1.1 %collective-permute-done.3.cross = bf16[24,16,128]{2,1,0:T(8,128)(2,1)S(1)} collective-permute-done((bf16[24,16,128]{2,1,0:T(8,128)(2,1)S(1)}, bf16[24,16,128]{2,1,0:T(8,128)(2,1)S(1)}, u32[]{:S(2)}, u32[]{:S(2)}) %collective-permute-start.3) | collective-permute-done | bytes 98336 | tf_op jit(solution)/shard_map/ppermute | solution.py:260
  82.3 3.1 %all-gather.11 = bf16[48,16,128]{2,1,0:T(8,128)(2,1)S(1)} all-gather(bf16[24,16,128]{2,1,0:T(8,128)(2,1)S(1)} %owe.7), channel_id=13, replica_groups={{0,1},{2,3},{4,5},{6,7},{8,9},{10,11},{12,13},{14,15},{16,17},{18,19},{..., dimensions={0}, use_global_device_ids=true | all-gather | bytes 294912 | tf_op jit(solution)/shard_map/all_gather | solution.py:219
  85.5 1.5 %last.1 = f32[16,4096]{1,0:T(8,128)} custom-call(s32[4,32]{1,0:T(4,128)S(1)} %get-tuple-element.30.index, s32[6,1,8]{2,1,0:T(1,128)S(1)} %bitcast.38, bf16[32,16,128]{2,1,0:T(8,128)(2,1)S(1)} %get-tuple-element.50.x_in, bf16[2,40,16,128]{3,2,1,0:T(8,128)(2,1)S(1)} %bitcast.21, bf16[24,16,128]{2,1,0:T(8,128)(2,1)S(1)} %collective-permute-done.3.cross, ...), custom_call_target="tpu_custom_call" | custom-call | tf_op jit(solution)/shard_map/last/pallas_call | solution.py:296
  (12 shorter events, 1.2 us)
Async XLA Ops:
  9.9 18.3 %collective-permute-start = (bf16[24,16,128]{2,1,0:T(8,128)(2,1)S(1)}, bf16[24,16,128]{2,1,0:T(8,128)(2,1)S(1)}, u32[]{:S(2)}, u32[]{:S(2)}) collective-permute-start(bf16[24,16,128]{2,1,0:T(8,128)(2,1)S(1)} %get-tuple-element.34), channel_id=1, source_target_pairs={{2,4},{5,9},{6,8},{7,11},{10,12},{13,17},{14,16},{15,19},{18,20},{... | collective-permute-start | bytes 294920 | tf_op jit(solution)/shard_map/ppermute | solution.py:260
  25.5 5.9 %copy-start = (s32[1,6,8]{2,0,1:T(1,128)S(1)}, s32[1,6,8]{2,0,1:T(1,128)}, u32[]{:S(2)}) copy-start(s32[1,6,8]{2,0,1:T(1,128)} %param.9) | copy-start | bytes 580
  34.5 11.8 %collective-permute-start.1 = (bf16[24,16,128]{2,1,0:T(8,128)(2,1)S(1)}, bf16[24,16,128]{2,1,0:T(8,128)(2,1)S(1)}, u32[]{:S(2)}, u32[]{:S(2)}) collective-permute-start(bf16[24,16,128]{2,1,0:T(8,128)(2,1)S(1)} %get-tuple-element.43), channel_id=1, source_target_pairs={{2,4},{5,9},{6,8},{7,11},{10,12},{13,17},{14,16},{15,19},{18,20},{... | collective-permute-start | bytes 294920 | tf_op jit(solution)/shard_map/ppermute | solution.py:260
  52.5 11.8 %collective-permute-start.2 = (bf16[24,16,128]{2,1,0:T(8,128)(2,1)S(1)}, bf16[24,16,128]{2,1,0:T(8,128)(2,1)S(1)}, u32[]{:S(2)}, u32[]{:S(2)}) collective-permute-start(bf16[24,16,128]{2,1,0:T(8,128)(2,1)S(1)} %get-tuple-element.48), channel_id=1, source_target_pairs={{2,4},{5,9},{6,8},{7,11},{10,12},{13,17},{14,16},{15,19},{18,20},{... | collective-permute-start | bytes 294920 | tf_op jit(solution)/shard_map/ppermute | solution.py:260
  70.5 11.8 %collective-permute-start.3 = (bf16[24,16,128]{2,1,0:T(8,128)(2,1)S(1)}, bf16[24,16,128]{2,1,0:T(8,128)(2,1)S(1)}, u32[]{:S(2)}, u32[]{:S(2)}) collective-permute-start(bf16[24,16,128]{2,1,0:T(8,128)(2,1)S(1)} %get-tuple-element.53), channel_id=1, source_target_pairs={{2,4},{5,9},{6,8},{7,11},{10,12},{13,17},{14,16},{15,19},{18,20},{... | collective-permute-start | bytes 294920 | tf_op jit(solution)/shard_map/ppermute | solution.py:260

commit v7 on v6

--- a/solution.py
+++ b/solution.py
@@ -118,9 +118,11 @@
     pack(lists, x, mine_out, gift_out)
 
 
-def partner():
+def partner(opening):
     me = lax.axis_index("dom")
-    return 1 - jnp.where(me & 1 == 0, (me >> 2) & 1, (me >> 1) & 1)
+    if opening:
+        return 1 - jnp.where(me & 1 == 0, (me >> 2) & 1, (me >> 1) & 1)
+    return ((me >> 1) ^ me) & 1
 
 
 def merge_kernel(mine, chip, cross, inner, both):
@@ -134,10 +136,22 @@
     inner[...] = both[pl.ds(24 - 24 * k, 24)]
 
 
+def split_kernel(mine, chip, far, near):
+    sib = chip.at[1 - role()[0]]
+    near[...] = mine[0:24] + sib[0:24]
+    far[0:8] = sib[24:32]
+    far[8:16] = mine[24:32]
+
+
+def owe_later_kernel(far, pair, out):
+    out[0:16] = pair[partner(False), 0:16]
+    out[16:24] = far[0:8]
+
+
 def owe_kernel(cross, pair, out, both):
     k = role()[0]
     both[0:24] = cross[...]
-    both[24:48] = pair[partner()]
+    both[24:48] = pair[partner(True)]
     out[0:16] = both[pl.ds(24 * k, 16)]
     out[16:24] = both[pl.ds(24 - 24 * k, 8)]
 
@@ -159,7 +173,7 @@
                 out[r, s * BLK : (s + 1) * BLK, :] = blocks[slot].T
 
 
-def step_kernel(last, index, lists_any, x_in, chip, cross, pair, side, base, scale, blocks, *rest):
+def step_kernel(opening, last, index, lists_any, x_in, chip, cross, pair, side, base, scale, blocks, *rest):
     if last:
         out_hbm, src, out, sems = rest
         parts = []
@@ -170,10 +184,15 @@
         x_out, mine_out, gift_out, src, x, lists, sem = rest
         copy = pltpu.make_async_copy(lists_any, lists, sem)
         copy.start()
-    other = 1 - role()[0]
+    k = role()[0]
+    other = 1 - k
     src[0:SENT] = x_in[...]
-    src[SENT:PAIR] = cross[...]
-    src[PAIR:SIDE] = pair[partner()]
+    if opening:
+        src[SENT:PAIR] = cross[...]
+        src[PAIR:SIDE] = pair[partner(True)]
+    else:
+        src[pl.ds(SENT + 24 * k, 24)] = pair[partner(False)]
+        src[pl.ds(PAIR - 24 * k, 16)] = cross[...]
     src[SIDE:DIRECT] = side[other]
     src[DIRECT:ZERO] = chip[other, 32:40]
     src[ZERO] = jnp.zeros((C, BLK), jnp.bfloat16)
@@ -213,6 +232,13 @@
                 found.append((2 * c + 1 - crossing, 2 * ((c + 1) % len(chips)) + 1 - crossing))
             if (c >> 1 & 1) == crossing:
                 found.append((2 * c + crossing, 2 * ((c + 2) % len(chips)) + crossing))
+        return found
+
+    def all_pairs(step):
+        found = []
+        for c in range(len(chips)):
+            core = (c >> 1) & 1 if step == 2 else 1 - (c & 1)
+            found.append((2 * c + core, 2 * ((c + step) % len(chips)) + core))
         return found
 
     def gather(value, groups):
@@ -248,17 +274,18 @@
     arranged = None
     for step in range(ITERS):
         chip = gather(gift, chips)
+        opening = step == 0
         cross, inner = call(
-            merge_kernel,
-            out_shape=(bf16(24, *score), bf16(24, *score)),
+            merge_kernel if opening else split_kernel,
+            out_shape=(bf16(24 if opening else 16, *score), bf16(24, *score)),
             in_specs=[VMEM] * 2,
             out_specs=(VMEM,) * 2,
-            scratch_shapes=[pltpu.VMEM((48, *score), jnp.bfloat16)],
+            scratch_shapes=[pltpu.VMEM((48, *score), jnp.bfloat16)] * opening,
             name="merge",
         )(mine, chip)
-        crossing = pairs(1)
-        cross = lax.ppermute(cross, "dom", crossing + [(b, a) for a, b in crossing])
-        pair = gather(inner, pairs(0))
+        sent, gathered = (pairs(1), pairs(0)) if opening else (all_pairs(2), all_pairs(1))
+        cross = lax.ppermute(cross, "dom", sent + [(b, a) for a, b in sent])
+        pair = gather(inner, gathered)
         if arranged is None:
             pair, row_offsets = lax.optimization_barrier((pair, row_offsets))
             arranged = call(
@@ -275,11 +302,11 @@
                 name="arrange",
             )(in_hbm(row_offsets), in_hbm(blocks))
         owed = call(
-            owe_kernel,
+            owe_kernel if opening else owe_later_kernel,
             out_shape=bf16(24, *score),
             in_specs=[VMEM] * 2,
             out_specs=VMEM,
-            scratch_shapes=[pltpu.VMEM((48, *score), jnp.bfloat16)],
+            scratch_shapes=[pltpu.VMEM((48, *score), jnp.bfloat16)] * opening,
             name="owe",
         )(cross, pair)
         side = gather(owed, chips)
@@ -294,7 +321,7 @@
                 pltpu.SemaphoreType.DMA,
             ]
         result = call(
-            functools.partial(step_kernel, last),
+            functools.partial(step_kernel, opening, last),
             out_shape=f32(*seeds.shape) if last else (bf16(RB, *score), bf16(32, *score), bf16(40, *score)),
             in_specs=[VMEM, ANY] + [VMEM] * 8,
             out_specs=HBM if last else (VMEM,) * 3,

time: 87.4 us -> 87.1 us (level)
  starting transfers between devices: 28.6 us -> 23.7 us
  waiting for transfers between devices: 4.58 us -> 7.26 us
  blocking collectives: 45.1 us -> 47.2 us
    ppermute x4, starting transfers between devices: 28.6 us -> 23.7 us  [on_device(): cross = lax.ppermute(cross, 'dom', sent + [(b, a) for a, b in sent])]
    ppermute x4, waiting for transfers between devices: 4.58 us -> 7.26 us  [on_device(): cross = lax.ppermute(cross, 'dom', sent + [(b, a) for a, b in sent])]
    all_gather x12, blocking collectives: 45.1 us -> 47.2 us  [gather(): lax.all_gather(value, 'dom', axis=0, axis_index_groups=[list(g) for g in...]
where the time goes in v7:
time: 87.1 us; the launch traced here: 86.6 us
  blocking collectives  47.2 us (54%)
  starting transfers between devices  23.7 us (27%)
  Pallas kernels  8.35 us (10%)
  waiting for transfers between devices  7.26 us (8%)
    all_gather x12, blocking collectives, gather(): lax.all_gather(value, 'dom', axis=0, axis_index_groups=[list(g) for g in...  47.2 us
    ppermute x4, starting transfers between devices, on_device(): cross = lax.ppermute(cross, 'dom', sent + [(b, a) for a, b in sent])  23.7 us
    ppermute x4, waiting for transfers between devices, on_device(): cross = lax.ppermute(cross, 'dom', sent + [(b, a) for a, b in sent])  7.26 us
    pallas_call x4, Pallas kernels, on_device(): call(functools.partial(step_kernel, opening, last), out_shape=f32(*seeds....  4.23 us
    pallas_call x1, Pallas kernels, on_device(): call(arrange_kernel, out_shape=bf16(RB, 4 * BLK, BLK), in_specs=[HBM, HBM...  2.67 us
  transfers between devices with their start and end apart: 4, of which 3 were waited for; matrix products, arithmetic and copies ran while one was open for 0% of the time, Pallas kernels for 3%

profile of v7, /device:TPU:1, one launch (start us, length us, event | category | flops | bytes accessed | tf_op | source)
XLA Modules:
  0.0 86.6 jit_solution(16405510344640421411)
XLA Ops:
  0.0 1.3 %first.1 = (bf16[32,16,128]{2,1,0:T(8,128)(2,1)S(1)}, bf16[32,16,128]{2,1,0:T(8,128)(2,1)S(1)}, bf16[40,16,128]{2,1,0:T(8,128)(2,1)S(1)}, f32[32,16,128]{2,1,0:T...) custom-call(f32[16,4096]{1,0:T(8,128)} %refs_0_.1, f32[32,128]{1,0:T(8,128)} %bitcast.39, s32[6,1,8]{2,1,0:T(1,128)} %bitcast.34, ...), custom_call_target="tpu_custom_call" | custom-call | tf_op jit(solution)/shard_map/first/pallas_call | solution.py:252
  1.3 8.6 %all-gather = bf16[80,16,128]{2,1,0:T(8,128)(2,1)S(1)} all-gather(bf16[40,16,128]{2,1,0:T(8,128)(2,1)S(1)} %get-tuple-element.32), channel_id=2, replica_groups={{0,1},{2,3},{4,5},{6,7},{8,9},{10,11},{12,13},{14,15},{16,17},{18,19},{..., dimensions={0}, use_global_device_ids=true | all-gather | bytes 491520 | tf_op jit(solution)/shard_map/all_gather | solution.py:245
  9.9 11.2 %collective-permute-start = (bf16[24,16,128]{2,1,0:T(8,128)(2,1)S(1)}, bf16[24,16,128]{2,1,0:T(8,128)(2,1)S(1)}, u32[]{:S(2)}, u32[]{:S(2)}) collective-permute-start(bf16[24,16,128]{2,1,0:T(8,128)(2,1)S(1)} %get-tuple-element.34), channel_id=1, source_target_pairs={{2,4},{5,9},{6,8},{7,11},{10,12},{13,17},{14,16},{15,19},{18,20},{... | collective-permute-start | bytes 294920 | tf_op jit(solution)/shard_map/ppermute | solution.py:287
  21.1 4.4 %all-gather.1 = bf16[48,16,128]{2,1,0:T(8,128)(2,1)S(1)} all-gather(bf16[24,16,128]{2,1,0:T(8,128)(2,1)S(1)} %get-tuple-element.35), channel_id=3, replica_groups={{1,3},{0,4},{2,6},{5,7},{9,11},{8,12},{10,14},{13,15},{17,19},{16,20},{..., dimensions={0}, use_global_device_ids=true | all-gather | bytes 294912 | tf_op jit(solution)/shard_map/all_gather | solution.py:245
  25.5 2.7 %arrange.1.blocks = bf16[32,512,128]{2,1,0:T(8,128)(2,1)S(1)} custom-call(s32[1,33]{1,0:T(1,128)} %offsets_any, bf16[128,128,128]{2,1,0:T(8,128)(2,1)} %blocks_hbm.1), custom_call_target="tpu_custom_call" | custom-call | bytes 16777216 | tf_op jit(solution)/shard_map/arrange/pallas_call | solution.py:291
  28.2 3.2 %all-gather.2 = bf16[48,16,128]{2,1,0:T(8,128)(2,1)S(1)} all-gather(bf16[24,16,128]{2,1,0:T(8,128)(2,1)S(1)} %owe.4), channel_id=4, replica_groups={{0,1},{2,3},{4,5},{6,7},{8,9},{10,11},{12,13},{14,15},{16,17},{18,19},{..., dimensions={0}, use_global_device_ids=true | all-gather | bytes 294912 | tf_op jit(solution)/shard_map/all_gather | solution.py:245
  31.5 0.9 %late.3 = (bf16[32,16,128]{2,1,0:T(8,128)(2,1)S(1)}, bf16[32,16,128]{2,1,0:T(8,128)(2,1)S(1)}, bf16[40,16,128]{2,1,0:T(8,128)(2,1)S(1)}) custom-call(s32[4,32]{1,0:T(4,128)S(1)} %get-tuple-element.30.index, s32[6,1,8]{2,1,0:T(1,128)S(1)} %bitcast.35, bf16[32,16,128]{2,1,0:T(8,128)(2,1)S(1)} %get-tuple-element.31.x_in, bf16[2,40,16,128]{3,2,1,0:T(8,128)(2,1)S(1)} %bitcast.15, ...), custom_call_target="tpu_custom_call" | custom-call | tf_op jit(solution)/shard_map/late/pallas_call | solution.py:323
  32.4 2.0 %all-gather.3 = bf16[80,16,128]{2,1,0:T(8,128)(2,1)S(1)} all-gather(bf16[40,16,128]{2,1,0:T(8,128)(2,1)S(1)} %get-tuple-element.41), channel_id=5, replica_groups={{0,1},{2,3},{4,5},{6,7},{8,9},{10,11},{12,13},{14,15},{16,17},{18,19},{..., dimensions={0}, use_global_device_ids=true | all-gather | bytes 491520 | tf_op jit(solution)/shard_map/all_gather | solution.py:245
  34.5 5.4 %collective-permute-start.1 = (bf16[16,16,128]{2,1,0:T(8,128)(2,1)S(1)}, bf16[16,16,128]{2,1,0:T(8,128)(2,1)S(1)}, u32[]{:S(2)}, u32[]{:S(2)}) collective-permute-start(bf16[16,16,128]{2,1,0:T(8,128)(2,1)S(1)} %get-tuple-element.43), channel_id=1, source_target_pairs={{0,4},{2,6},{5,9},{7,11},{8,12},{10,14},{13,17},{15,19},{16,20},{1... | collective-permute-start | bytes 196616 | tf_op jit(solution)/shard_map/ppermute | solution.py:287
  39.8 4.4 %all-gather.4 = bf16[48,16,128]{2,1,0:T(8,128)(2,1)S(1)} all-gather(bf16[24,16,128]{2,1,0:T(8,128)(2,1)S(1)} %get-tuple-element.44), channel_id=6, replica_groups={{1,3},{2,4},{5,7},{6,8},{9,11},{10,12},{13,15},{14,16},{17,19},{18,20},..., dimensions={0}, use_global_device_ids=true | all-gather | bytes 294912 | tf_op jit(solution)/shard_map/all_gather | solution.py:245
  44.3 1.5 %collective-permute-done.1.far.cross = bf16[16,16,128]{2,1,0:T(8,128)(2,1)S(1)} collective-permute-done((bf16[16,16,128]{2,1,0:T(8,128)(2,1)S(1)}, bf16[16,16,128]{2,1,0:T(8,128)(2,1)S(1)}, u32[]{:S(2)}, u32[]{:S(2)}) %collective-permute-start.1) | collective-permute-done | bytes 65568 | tf_op jit(solution)/shard_map/ppermute | solution.py:287
  45.8 4.0 %all-gather.5 = bf16[48,16,128]{2,1,0:T(8,128)(2,1)S(1)} all-gather(bf16[24,16,128]{2,1,0:T(8,128)(2,1)S(1)} %owe.5), channel_id=7, replica_groups={{0,1},{2,3},{4,5},{6,7},{8,9},{10,11},{12,13},{14,15},{16,17},{18,19},{..., dimensions={0}, use_global_device_ids=true | all-gather | bytes 294912 | tf_op jit(solution)/shard_map/all_gather | solution.py:245
  49.8 0.9 %late.4 = (bf16[32,16,128]{2,1,0:T(8,128)(2,1)S(1)}, bf16[32,16,128]{2,1,0:T(8,128)(2,1)S(1)}, bf16[40,16,128]{2,1,0:T(8,128)(2,1)S(1)}) custom-call(s32[4,32]{1,0:T(4,128)S(1)} %get-tuple-element.30.index, s32[6,1,8]{2,1,0:T(1,128)S(1)} %bitcast.36, bf16[32,16,128]{2,1,0:T(8,128)(2,1)S(1)} %get-tuple-element.40.x_in, bf16[2,40,16,128]{3,2,1,0:T(8,128)(2,1)S(1)} %bitcast.17, ...), custom_call_target="tpu_custom_call" | custom-call | tf_op jit(solution)/shard_map/late/pallas_call | solution.py:323
  50.7 2.0 %all-gather.6 = bf16[80,16,128]{2,1,0:T(8,128)(2,1)S(1)} all-gather(bf16[40,16,128]{2,1,0:T(8,128)(2,1)S(1)} %get-tuple-element.46), channel_id=8, replica_groups={{0,1},{2,3},{4,5},{6,7},{8,9},{10,11},{12,13},{14,15},{16,17},{18,19},{..., dimensions={0}, use_global_device_ids=true | all-gather | bytes 491520 | tf_op jit(solution)/shard_map/all_gather | solution.py:245
  52.8 4.1 %collective-permute-start.2 = (bf16[16,16,128]{2,1,0:T(8,128)(2,1)S(1)}, bf16[16,16,128]{2,1,0:T(8,128)(2,1)S(1)}, u32[]{:S(2)}, u32[]{:S(2)}) collective-permute-start(bf16[16,16,128]{2,1,0:T(8,128)(2,1)S(1)} %get-tuple-element.48), channel_id=1, source_target_pairs={{0,4},{2,6},{5,9},{7,11},{8,12},{10,14},{13,17},{15,19},{16,20},{1... | collective-permute-start | bytes 196616 | tf_op jit(solution)/shard_map/ppermute | solution.py:287
  56.9 4.4 %all-gather.7 = bf16[48,16,128]{2,1,0:T(8,128)(2,1)S(1)} all-gather(bf16[24,16,128]{2,1,0:T(8,128)(2,1)S(1)} %get-tuple-element.49), channel_id=9, replica_groups={{1,3},{2,4},{5,7},{6,8},{9,11},{10,12},{13,15},{14,16},{17,19},{18,20},..., dimensions={0}, use_global_device_ids=true | all-gather | bytes 294912 | tf_op jit(solution)/shard_map/all_gather | solution.py:245
  61.3 2.9 %collective-permute-done.2.far.cross = bf16[16,16,128]{2,1,0:T(8,128)(2,1)S(1)} collective-permute-done((bf16[16,16,128]{2,1,0:T(8,128)(2,1)S(1)}, bf16[16,16,128]{2,1,0:T(8,128)(2,1)S(1)}, u32[]{:S(2)}, u32[]{:S(2)}) %collective-permute-start.2) | collective-permute-done | bytes 65568 | tf_op jit(solution)/shard_map/ppermute | solution.py:287
  64.2 3.3 %all-gather.8 = bf16[48,16,128]{2,1,0:T(8,128)(2,1)S(1)} all-gather(bf16[24,16,128]{2,1,0:T(8,128)(2,1)S(1)} %owe.6), channel_id=10, replica_groups={{0,1},{2,3},{4,5},{6,7},{8,9},{10,11},{12,13},{14,15},{16,17},{18,19},{..., dimensions={0}, use_global_device_ids=true | all-gather | bytes 294912 | tf_op jit(solution)/shard_map/all_gather | solution.py:245
  68.4 2.0 %all-gather.9 = bf16[80,16,128]{2,1,0:T(8,128)(2,1)S(1)} all-gather(bf16[40,16,128]{2,1,0:T(8,128)(2,1)S(1)} %get-tuple-element.51), channel_id=11, replica_groups={{0,1},{2,3},{4,5},{6,7},{8,9},{10,11},{12,13},{14,15},{16,17},{18,19},{..., dimensions={0}, use_global_device_ids=true | all-gather | bytes 491520 | tf_op jit(solution)/shard_map/all_gather | solution.py:245
  70.5 3.0 %collective-permute-start.3 = (bf16[16,16,128]{2,1,0:T(8,128)(2,1)S(1)}, bf16[16,16,128]{2,1,0:T(8,128)(2,1)S(1)}, u32[]{:S(2)}, u32[]{:S(2)}) collective-permute-start(bf16[16,16,128]{2,1,0:T(8,128)(2,1)S(1)} %get-tuple-element.53), channel_id=1, source_target_pairs={{0,4},{2,6},{5,9},{7,11},{8,12},{10,14},{13,17},{15,19},{16,20},{1... | collective-permute-start | bytes 196616 | tf_op jit(solution)/shard_map/ppermute | solution.py:287
  73.6 5.4 %all-gather.10 = bf16[48,16,128]{2,1,0:T(8,128)(2,1)S(1)} all-gather(bf16[24,16,128]{2,1,0:T(8,128)(2,1)S(1)} %get-tuple-element.54), channel_id=12, replica_groups={{1,3},{2,4},{5,7},{6,8},{9,11},{10,12},{13,15},{14,16},{17,19},{18,20},..., dimensions={0}, use_global_device_ids=true | all-gather | bytes 294912 | tf_op jit(solution)/shard_map/all_gather | solution.py:245
  79.0 2.9 %collective-permute-done.3.far.cross = bf16[16,16,128]{2,1,0:T(8,128)(2,1)S(1)} collective-permute-done((bf16[16,16,128]{2,1,0:T(8,128)(2,1)S(1)}, bf16[16,16,128]{2,1,0:T(8,128)(2,1)S(1)}, u32[]{:S(2)}, u32[]{:S(2)}) %collective-permute-start.3) | collective-permute-done | bytes 65568 | tf_op jit(solution)/shard_map/ppermute | solution.py:287
  81.9 3.3 %all-gather.11 = bf16[48,16,128]{2,1,0:T(8,128)(2,1)S(1)} all-gather(bf16[24,16,128]{2,1,0:T(8,128)(2,1)S(1)} %owe.7), channel_id=13, replica_groups={{0,1},{2,3},{4,5},{6,7},{8,9},{10,11},{12,13},{14,15},{16,17},{18,19},{..., dimensions={0}, use_global_device_ids=true | all-gather | bytes 294912 | tf_op jit(solution)/shard_map/all_gather | solution.py:245
  85.2 1.4 %last.1 = f32[16,4096]{1,0:T(8,128)} custom-call(s32[4,32]{1,0:T(4,128)S(1)} %get-tuple-element.30.index, s32[6,1,8]{2,1,0:T(1,128)S(1)} %bitcast.38, bf16[32,16,128]{2,1,0:T(8,128)(2,1)S(1)} %get-tuple-element.50.x_in, bf16[2,40,16,128]{3,2,1,0:T(8,128)(2,1)S(1)} %bitcast.21, bf16[16,16,128]{2,1,0:T(8,128)(2,1)S(1)} %collective-permute-done.3.far.cross, ...), custom_call_target="tpu_custom_call" | custom-call | tf_op jit(solution)/shard_map/last/pallas_call | solution.py:323
  (12 shorter events, 1.1 us)
Async XLA Ops:
  9.9 18.3 %collective-permute-start = (bf16[24,16,128]{2,1,0:T(8,128)(2,1)S(1)}, bf16[24,16,128]{2,1,0:T(8,128)(2,1)S(1)}, u32[]{:S(2)}, u32[]{:S(2)}) collective-permute-start(bf16[24,16,128]{2,1,0:T(8,128)(2,1)S(1)} %get-tuple-element.34), channel_id=1, source_target_pairs={{2,4},{5,9},{6,8},{7,11},{10,12},{13,17},{14,16},{15,19},{18,20},{... | collective-permute-start | bytes 294920 | tf_op jit(solution)/shard_map/ppermute | solution.py:287
  25.5 5.9 %copy-start = (s32[1,6,8]{2,0,1:T(1,128)S(1)}, s32[1,6,8]{2,0,1:T(1,128)}, u32[]{:S(2)}) copy-start(s32[1,6,8]{2,0,1:T(1,128)} %param.9) | copy-start | bytes 580
  34.5 11.3 %collective-permute-start.1 = (bf16[16,16,128]{2,1,0:T(8,128)(2,1)S(1)}, bf16[16,16,128]{2,1,0:T(8,128)(2,1)S(1)}, u32[]{:S(2)}, u32[]{:S(2)}) collective-permute-start(bf16[16,16,128]{2,1,0:T(8,128)(2,1)S(1)} %get-tuple-element.43), channel_id=1, source_target_pairs={{0,4},{2,6},{5,9},{7,11},{8,12},{10,14},{13,17},{15,19},{16,20},{1... | collective-permute-start | bytes 196616 | tf_op jit(solution)/shard_map/ppermute | solution.py:287
  52.8 11.3 %collective-permute-start.2 = (bf16[16,16,128]{2,1,0:T(8,128)(2,1)S(1)}, bf16[16,16,128]{2,1,0:T(8,128)(2,1)S(1)}, u32[]{:S(2)}, u32[]{:S(2)}) collective-permute-start(bf16[16,16,128]{2,1,0:T(8,128)(2,1)S(1)} %get-tuple-element.48), channel_id=1, source_target_pairs={{0,4},{2,6},{5,9},{7,11},{8,12},{10,14},{13,17},{15,19},{16,20},{1... | collective-permute-start | bytes 196616 | tf_op jit(solution)/shard_map/ppermute | solution.py:287
  70.5 11.3 %collective-permute-start.3 = (bf16[16,16,128]{2,1,0:T(8,128)(2,1)S(1)}, bf16[16,16,128]{2,1,0:T(8,128)(2,1)S(1)}, u32[]{:S(2)}, u32[]{:S(2)}) collective-permute-start(bf16[16,16,128]{2,1,0:T(8,128)(2,1)S(1)} %get-tuple-element.53), channel_id=1, source_target_pairs={{0,4},{2,6},{5,9},{7,11},{8,12},{10,14},{13,17},{15,19},{16,20},{1... | collective-permute-start | bytes 196616 | tf_op jit(solution)/shard_map/ppermute | solution.py:287

commit v8 on v7

--- a/solution.py
+++ b/solution.py
@@ -93,23 +93,21 @@
 
 
 def first_kernel(*refs):
-    sources, (x_out, mine_out, gift_out, base_out, scale_out, index_out) = refs[:5], refs[5:11]
-    lists, columns, offsets, seeds, x, sems = refs[11:]
+    sources, (x_out, mine_out, gift_out, base_out, scale_out) = refs[:3], refs[3:8]
+    lists, seeds, x, sems = refs[8:]
     copies = []
-    for i, target in enumerate((scale_out, lists, columns, offsets)):
+    for i, target in enumerate((scale_out, lists)):
         copies.append(pltpu.make_async_copy(sources[i + 1], target, sems.at[i]))
     for i in range(4):
         part = pl.ds(i * RB * BLK // 4, RB * BLK // 4)
-        copies.append(pltpu.make_async_copy(sources[0].at[:, part], seeds.at[:, part], sems.at[i + 4]))
+        copies.append(pltpu.make_async_copy(sources[0].at[:, part], seeds.at[:, part], sems.at[i + 2]))
     for copy in copies:
         copy.start()
-    for copy in copies[:4]:
+    for copy in copies[:2]:
         copy.wait()
-    for s, row in enumerate(places(columns[...], offsets[...])):
-        index_out[s : s + 1, :] = row
     for r in range(RB):
         if r % 8 == 0:
-            copies[4 + r // 8].wait()
+            copies[2 + r // 8].wait()
         field = seeds[:, r * BLK : (r + 1) * BLK]
         base_out[r] = (1.0 - ALPHA) * field
         x[r] = (field * scale_out[r : r + 1, :]).astype(jnp.bfloat16)
@@ -156,15 +154,25 @@
     out[16:24] = both[pl.ds(24 - 24 * k, 8)]
 
 
-def arrange_kernel(offsets_any, blocks_hbm, out, offsets, blocks, sems):
+def arrange_kernel(offsets_any, columns_hbm, blocks_hbm, out, index_out, offsets, starts, columns, blocks, sems):
     first = pltpu.make_async_copy(offsets_any, offsets, sems.at[8])
     first.start()
+    tables = [
+        pltpu.make_async_copy(offsets_any, starts, sems.at[9]),
+        pltpu.make_async_copy(columns_hbm, columns, sems.at[10]),
+    ]
+    for table in tables:
+        table.start()
     copies = []
     for g in range(8):
         part = pl.ds(16 * g, 16)
         copies.append(pltpu.make_async_copy(blocks_hbm.at[part], blocks.at[part], sems.at[g]))
         copies[-1].start()
     first.wait()
+    for table in tables:
+        table.wait()
+    for s, row in enumerate(places(columns[...], starts[...])):
+        index_out[s : s + 1, :] = row
     for g in range(8):
         copies[g].wait()
         for r in range(4 * g, 4 * g + 4):
@@ -249,7 +257,7 @@
     lists = jnp.transpose(send_index, (1, 0, 2))
     score = (C, BLK)
 
-    x, mine, gift, base, scale, index = call(
+    x, mine, gift, base, scale = call(
         first_kernel,
         out_shape=(
             bf16(RB, *score),
@@ -257,20 +265,17 @@
             bf16(40, *score),
             f32(RB, *score),
             f32(RB, BLK),
-            jax.ShapeDtypeStruct((4, RB), jnp.int32),
         ),
-        in_specs=[HBM] * 5,
-        out_specs=(VMEM,) * 6,
+        in_specs=[HBM] * 3,
+        out_specs=(VMEM,) * 5,
         scratch_shapes=[
             pltpu.SMEM(lists.shape, jnp.int32),
-            pltpu.VMEM(col_index.shape, jnp.int32),
-            pltpu.VMEM(row_offsets.shape, jnp.int32),
             pltpu.VMEM(seeds.shape, jnp.float32),
             pltpu.VMEM((RB + 1, *score), jnp.bfloat16),
-            pltpu.SemaphoreType.DMA((8,)),
+            pltpu.SemaphoreType.DMA((6,)),
         ],
         name="first",
-    )(*map(in_hbm, (seeds, deg_scale.reshape(RB, BLK), lists, col_index, row_offsets)))
+    )(*map(in_hbm, (seeds, deg_scale.reshape(RB, BLK), lists)))
     arranged = None
     for step in range(ITERS):
         chip = gather(gift, chips)
@@ -288,19 +293,21 @@
         pair = gather(inner, gathered)
         if arranged is None:
             pair, row_offsets = lax.optimization_barrier((pair, row_offsets))
-            arranged = call(
+            arranged, index = call(
                 arrange_kernel,
-                out_shape=bf16(RB, 4 * BLK, BLK),
-                in_specs=[HBM, HBM],
-                out_specs=VMEM,
+                out_shape=(bf16(RB, 4 * BLK, BLK), jax.ShapeDtypeStruct((4, RB), jnp.int32)),
+                in_specs=[HBM] * 3,
+                out_specs=(VMEM,) * 2,
                 scratch_shapes=[
                     pltpu.SMEM(row_offsets.shape, jnp.int32),
+                    pltpu.VMEM(row_offsets.shape, jnp.int32),
+                    pltpu.VMEM(col_index.shape, jnp.int32),
                     pltpu.VMEM(blocks.shape, jnp.bfloat16),
-                    pltpu.SemaphoreType.DMA((9,)),
+                    pltpu.SemaphoreType.DMA((11,)),
                 ],
                 cost_estimate=pl.CostEstimate(flops=0, bytes_accessed=16 << 20, transcendentals=0),
                 name="arrange",
-            )(in_hbm(row_offsets), in_hbm(blocks))
+            )(*map(in_hbm, (row_offsets, col_index, blocks)))
         owed = call(
             owe_kernel if opening else owe_later_kernel,
             out_shape=bf16(24, *score),

time: 87.1 us -> 86.9 us (level)
  no operation moved by 1% of the time
where the time goes in v8:
time: 86.9 us; the launch traced here: 86.6 us
  blocking collectives  47.3 us (54%)
  starting transfers between devices  23.5 us (27%)
  Pallas kernels  8.28 us (10%)
  waiting for transfers between devices  7.31 us (8%)
    all_gather x12, blocking collectives, gather(): lax.all_gather(value, 'dom', axis=0, axis_index_groups=[list(g) for g in...  47.3 us
    ppermute x4, starting transfers between devices, on_device(): cross = lax.ppermute(cross, 'dom', sent + [(b, a) for a, b in sent])  23.5 us
    ppermute x4, waiting for transfers between devices, on_device(): cross = lax.ppermute(cross, 'dom', sent + [(b, a) for a, b in sent])  7.31 us
    pallas_call x4, Pallas kernels, on_device(): call(functools.partial(step_kernel, opening, last), out_shape=f32(*seeds....  4.27 us
    pallas_call x1, Pallas kernels, on_device(): call(arrange_kernel, out_shape=(bf16(RB, 4 * BLK, BLK), jax.ShapeDtypeStr...  2.71 us
  transfers between devices with their start and end apart: 4, of which 3 were waited for; matrix products, arithmetic and copies ran while one was open for 0% of the time, Pallas kernels for 3%

profile of v8, /device:TPU:1, one launch (start us, length us, event | category | flops | bytes accessed | tf_op | source)
XLA Modules:
  0.0 86.6 jit_solution(3328957824398015331)
XLA Ops:
  0.0 1.1 %first.1 = (bf16[32,16,128]{2,1,0:T(8,128)(2,1)S(1)}, bf16[32,16,128]{2,1,0:T(8,128)(2,1)S(1)}, bf16[40,16,128]{2,1,0:T(8,128)(2,1)S(1)}, f32[32,16,128]{2,1,0:T(8,128)S(1)}, f32[32,128]{1,0:T(8,128)S(1)}) custom-call(f32[16,4096]{1,0:T(8,128)} %refs_0_.1, f32[32,128]{1,0:T(8,128)} %bitcast.39, s32[6,1,8]{2,1,0:T(1,128)} %bitcast.34), custom_call_target="tpu_custom_call" | custom-call | tf_op jit(solution)/shard_map/first/pallas_call | solution.py:260
  1.1 8.6 %all-gather = bf16[80,16,128]{2,1,0:T(8,128)(2,1)S(1)} all-gather(bf16[40,16,128]{2,1,0:T(8,128)(2,1)S(1)} %get-tuple-element.32), channel_id=2, replica_groups={{0,1},{2,3},{4,5},{6,7},{8,9},{10,11},{12,13},{14,15},{16,17},{18,19},{..., dimensions={0}, use_global_device_ids=true | all-gather | bytes 491520 | tf_op jit(solution)/shard_map/all_gather | solution.py:253
  9.7 11.2 %collective-permute-start = (bf16[24,16,128]{2,1,0:T(8,128)(2,1)S(1)}, bf16[24,16,128]{2,1,0:T(8,128)(2,1)S(1)}, u32[]{:S(2)}, u32[]{:S(2)}) collective-permute-start(bf16[24,16,128]{2,1,0:T(8,128)(2,1)S(1)} %get-tuple-element.37), channel_id=1, source_target_pairs={{2,4},{5,9},{6,8},{7,11},{10,12},{13,17},{14,16},{15,19},{18,20},{... | collective-permute-start | bytes 294920 | tf_op jit(solution)/shard_map/ppermute | solution.py:292
  20.9 4.4 %all-gather.1 = bf16[48,16,128]{2,1,0:T(8,128)(2,1)S(1)} all-gather(bf16[24,16,128]{2,1,0:T(8,128)(2,1)S(1)} %get-tuple-element.33), channel_id=3, replica_groups={{1,3},{0,4},{2,6},{5,7},{9,11},{8,12},{10,14},{13,15},{17,19},{16,20},{..., dimensions={0}, use_global_device_ids=true | all-gather | bytes 294912 | tf_op jit(solution)/shard_map/all_gather | solution.py:253
  25.4 2.7 %arrange.1 = (bf16[32,512,128]{2,1,0:T(8,128)(2,1)S(1)}, s32[4,32]{1,0:T(4,128)S(1)}) custom-call(s32[1,33]{1,0:T(1,128)} %offsets_any, s32[1,128]{1,0:T(1,128)} %columns_hbm.1, bf16[128,128,128]{2,1,0:T(8,128)(2,1)} %blocks_hbm.1), custom_call_target="tpu_custom_call" | custom-call | bytes 16777216 | tf_op jit(solution)/shard_map/arrange/pallas_call | solution.py:296
  28.1 3.2 %all-gather.2 = bf16[48,16,128]{2,1,0:T(8,128)(2,1)S(1)} all-gather(bf16[24,16,128]{2,1,0:T(8,128)(2,1)S(1)} %owe.4), channel_id=4, replica_groups={{0,1},{2,3},{4,5},{6,7},{8,9},{10,11},{12,13},{14,15},{16,17},{18,19},{..., dimensions={0}, use_global_device_ids=true | all-gather | bytes 294912 | tf_op jit(solution)/shard_map/all_gather | solution.py:253
  31.3 0.9 %late.3 = (bf16[32,16,128]{2,1,0:T(8,128)(2,1)S(1)}, bf16[32,16,128]{2,1,0:T(8,128)(2,1)S(1)}, bf16[40,16,128]{2,1,0:T(8,128)(2,1)S(1)}) custom-call(s32[4,32]{1,0:T(4,128)S(1)} %get-tuple-element.35.index, s32[6,1,8]{2,1,0:T(1,128)S(1)} %bitcast.35, bf16[32,16,128]{2,1,0:T(8,128)(2,1)S(1)} %get-tuple-element.36.x_in, bf16[2,40,16,128]{3,2,1,0:T(8,128)(2,1)S(1)} %bitcast.15, ...), custom_call_target="tpu_custom_call" | custom-call | tf_op jit(solution)/shard_map/late/pallas_call | solution.py:330
  32.3 2.0 %all-gather.3 = bf16[80,16,128]{2,1,0:T(8,128)(2,1)S(1)} all-gather(bf16[40,16,128]{2,1,0:T(8,128)(2,1)S(1)} %get-tuple-element.43), channel_id=5, replica_groups={{0,1},{2,3},{4,5},{6,7},{8,9},{10,11},{12,13},{14,15},{16,17},{18,19},{..., dimensions={0}, use_global_device_ids=true | all-gather | bytes 491520 | tf_op jit(solution)/shard_map/all_gather | solution.py:253
  34.4 5.3 %collective-permute-start.1 = (bf16[16,16,128]{2,1,0:T(8,128)(2,1)S(1)}, bf16[16,16,128]{2,1,0:T(8,128)(2,1)S(1)}, u32[]{:S(2)}, u32[]{:S(2)}) collective-permute-start(bf16[16,16,128]{2,1,0:T(8,128)(2,1)S(1)} %get-tuple-element.45), channel_id=1, source_target_pairs={{0,4},{2,6},{5,9},{7,11},{8,12},{10,14},{13,17},{15,19},{16,20},{1... | collective-permute-start | bytes 196616 | tf_op jit(solution)/shard_map/ppermute | solution.py:292
  39.7 4.4 %all-gather.4 = bf16[48,16,128]{2,1,0:T(8,128)(2,1)S(1)} all-gather(bf16[24,16,128]{2,1,0:T(8,128)(2,1)S(1)} %get-tuple-element.46), channel_id=6, replica_groups={{1,3},{2,4},{5,7},{6,8},{9,11},{10,12},{13,15},{14,16},{17,19},{18,20},..., dimensions={0}, use_global_device_ids=true | all-gather | bytes 294912 | tf_op jit(solution)/shard_map/all_gather | solution.py:253
  44.1 1.6 %collective-permute-done.1.far.cross = bf16[16,16,128]{2,1,0:T(8,128)(2,1)S(1)} collective-permute-done((bf16[16,16,128]{2,1,0:T(8,128)(2,1)S(1)}, bf16[16,16,128]{2,1,0:T(8,128)(2,1)S(1)}, u32[]{:S(2)}, u32[]{:S(2)}) %collective-permute-start.1) | collective-permute-done | bytes 65568 | tf_op jit(solution)/shard_map/ppermute | solution.py:292
  45.7 4.0 %all-gather.5 = bf16[48,16,128]{2,1,0:T(8,128)(2,1)S(1)} all-gather(bf16[24,16,128]{2,1,0:T(8,128)(2,1)S(1)} %owe.5), channel_id=7, replica_groups={{0,1},{2,3},{4,5},{6,7},{8,9},{10,11},{12,13},{14,15},{16,17},{18,19},{..., dimensions={0}, use_global_device_ids=true | all-gather | bytes 294912 | tf_op jit(solution)/shard_map/all_gather | solution.py:253
  49.7 0.9 %late.4 = (bf16[32,16,128]{2,1,0:T(8,128)(2,1)S(1)}, bf16[32,16,128]{2,1,0:T(8,128)(2,1)S(1)}, bf16[40,16,128]{2,1,0:T(8,128)(2,1)S(1)}) custom-call(s32[4,32]{1,0:T(4,128)S(1)} %get-tuple-element.35.index, s32[6,1,8]{2,1,0:T(1,128)S(1)} %bitcast.36, bf16[32,16,128]{2,1,0:T(8,128)(2,1)S(1)} %get-tuple-element.42.x_in, bf16[2,40,16,128]{3,2,1,0:T(8,128)(2,1)S(1)} %bitcast.17, ...), custom_call_target="tpu_custom_call" | custom-call | tf_op jit(solution)/shard_map/late/pallas_call | solution.py:330
  50.7 2.0 %all-gather.6 = bf16[80,16,128]{2,1,0:T(8,128)(2,1)S(1)} all-gather(bf16[40,16,128]{2,1,0:T(8,128)(2,1)S(1)} %get-tuple-element.48), channel_id=8, replica_groups={{0,1},{2,3},{4,5},{6,7},{8,9},{10,11},{12,13},{14,15},{16,17},{18,19},{..., dimensions={0}, use_global_device_ids=true | all-gather | bytes 491520 | tf_op jit(solution)/shard_map/all_gather | solution.py:253
  52.7 4.0 %collective-permute-start.2 = (bf16[16,16,128]{2,1,0:T(8,128)(2,1)S(1)}, bf16[16,16,128]{2,1,0:T(8,128)(2,1)S(1)}, u32[]{:S(2)}, u32[]{:S(2)}) collective-permute-start(bf16[16,16,128]{2,1,0:T(8,128)(2,1)S(1)} %get-tuple-element.50), channel_id=1, source_target_pairs={{0,4},{2,6},{5,9},{7,11},{8,12},{10,14},{13,17},{15,19},{16,20},{1... | collective-permute-start | bytes 196616 | tf_op jit(solution)/shard_map/ppermute | solution.py:292
  56.7 4.5 %all-gather.7 = bf16[48,16,128]{2,1,0:T(8,128)(2,1)S(1)} all-gather(bf16[24,16,128]{2,1,0:T(8,128)(2,1)S(1)} %get-tuple-element.51), channel_id=9, replica_groups={{1,3},{2,4},{5,7},{6,8},{9,11},{10,12},{13,15},{14,16},{17,19},{18,20},..., dimensions={0}, use_global_device_ids=true | all-gather | bytes 294912 | tf_op jit(solution)/shard_map/all_gather | solution.py:253
  61.2 2.9 %collective-permute-done.2.far.cross = bf16[16,16,128]{2,1,0:T(8,128)(2,1)S(1)} collective-permute-done((bf16[16,16,128]{2,1,0:T(8,128)(2,1)S(1)}, bf16[16,16,128]{2,1,0:T(8,128)(2,1)S(1)}, u32[]{:S(2)}, u32[]{:S(2)}) %collective-permute-start.2) | collective-permute-done | bytes 65568 | tf_op jit(solution)/shard_map/ppermute | solution.py:292
  64.1 3.3 %all-gather.8 = bf16[48,16,128]{2,1,0:T(8,128)(2,1)S(1)} all-gather(bf16[24,16,128]{2,1,0:T(8,128)(2,1)S(1)} %owe.6), channel_id=10, replica_groups={{0,1},{2,3},{4,5},{6,7},{8,9},{10,11},{12,13},{14,15},{16,17},{18,19},{..., dimensions={0}, use_global_device_ids=true | all-gather | bytes 294912 | tf_op jit(solution)/shard_map/all_gather | solution.py:253
  68.4 2.0 %all-gather.9 = bf16[80,16,128]{2,1,0:T(8,128)(2,1)S(1)} all-gather(bf16[40,16,128]{2,1,0:T(8,128)(2,1)S(1)} %get-tuple-element.53), channel_id=11, replica_groups={{0,1},{2,3},{4,5},{6,7},{8,9},{10,11},{12,13},{14,15},{16,17},{18,19},{..., dimensions={0}, use_global_device_ids=true | all-gather | bytes 491520 | tf_op jit(solution)/shard_map/all_gather | solution.py:253
  70.4 3.0 %collective-permute-start.3 = (bf16[16,16,128]{2,1,0:T(8,128)(2,1)S(1)}, bf16[16,16,128]{2,1,0:T(8,128)(2,1)S(1)}, u32[]{:S(2)}, u32[]{:S(2)}) collective-permute-start(bf16[16,16,128]{2,1,0:T(8,128)(2,1)S(1)} %get-tuple-element.55), channel_id=1, source_target_pairs={{0,4},{2,6},{5,9},{7,11},{8,12},{10,14},{13,17},{15,19},{16,20},{1... | collective-permute-start | bytes 196616 | tf_op jit(solution)/shard_map/ppermute | solution.py:292
  73.5 5.4 %all-gather.10 = bf16[48,16,128]{2,1,0:T(8,128)(2,1)S(1)} all-gather(bf16[24,16,128]{2,1,0:T(8,128)(2,1)S(1)} %get-tuple-element.56), channel_id=12, replica_groups={{1,3},{2,4},{5,7},{6,8},{9,11},{10,12},{13,15},{14,16},{17,19},{18,20},..., dimensions={0}, use_global_device_ids=true | all-gather | bytes 294912 | tf_op jit(solution)/shard_map/all_gather | solution.py:253
  78.9 2.9 %collective-permute-done.3.far.cross = bf16[16,16,128]{2,1,0:T(8,128)(2,1)S(1)} collective-permute-done((bf16[16,16,128]{2,1,0:T(8,128)(2,1)S(1)}, bf16[16,16,128]{2,1,0:T(8,128)(2,1)S(1)}, u32[]{:S(2)}, u32[]{:S(2)}) %collective-permute-start.3) | collective-permute-done | bytes 65568 | tf_op jit(solution)/shard_map/ppermute | solution.py:292
  81.8 3.3 %all-gather.11 = bf16[48,16,128]{2,1,0:T(8,128)(2,1)S(1)} all-gather(bf16[24,16,128]{2,1,0:T(8,128)(2,1)S(1)} %owe.7), channel_id=13, replica_groups={{0,1},{2,3},{4,5},{6,7},{8,9},{10,11},{12,13},{14,15},{16,17},{18,19},{..., dimensions={0}, use_global_device_ids=true | all-gather | bytes 294912 | tf_op jit(solution)/shard_map/all_gather | solution.py:253
  85.1 1.5 %last.1 = f32[16,4096]{1,0:T(8,128)} custom-call(s32[4,32]{1,0:T(4,128)S(1)} %get-tuple-element.35.index, s32[6,1,8]{2,1,0:T(1,128)S(1)} %bitcast.38, bf16[32,16,128]{2,1,0:T(8,128)(2,1)S(1)} %get-tuple-element.52.x_in, bf16[2,40,16,128]{3,2,1,0:T(8,128)(2,1)S(1)} %bitcast.21, bf16[16,16,128]{2,1,0:T(8,128)(2,1)S(1)} %collective-permute-done.3.far.cross, ...), custom_call_target="tpu_custom_call" | custom-call | tf_op jit(solution)/shard_map/last/pallas_call | solution.py:330
  (12 shorter events, 1.1 us)
Async XLA Ops:
  0.0 31.3 %copy-start = (s32[1,6,8]{2,0,1:T(1,128)S(1)}, s32[1,6,8]{2,0,1:T(1,128)}, u32[]{:S(2)}) copy-start(s32[1,6,8]{2,0,1:T(1,128)} %param.9) | copy-start | bytes 580
  9.7 18.3 %collective-permute-start = (bf16[24,16,128]{2,1,0:T(8,128)(2,1)S(1)}, bf16[24,16,128]{2,1,0:T(8,128)(2,1)S(1)}, u32[]{:S(2)}, u32[]{:S(2)}) collective-permute-start(bf16[24,16,128]{2,1,0:T(8,128)(2,1)S(1)} %get-tuple-element.37), channel_id=1, source_target_pairs={{2,4},{5,9},{6,8},{7,11},{10,12},{13,17},{14,16},{15,19},{18,20},{... | collective-permute-start | bytes 294920 | tf_op jit(solution)/shard_map/ppermute | solution.py:292
  34.4 11.3 %collective-permute-start.1 = (bf16[16,16,128]{2,1,0:T(8,128)(2,1)S(1)}, bf16[16,16,128]{2,1,0:T(8,128)(2,1)S(1)}, u32[]{:S(2)}, u32[]{:S(2)}) collective-permute-start(bf16[16,16,128]{2,1,0:T(8,128)(2,1)S(1)} %get-tuple-element.45), channel_id=1, source_target_pairs={{0,4},{2,6},{5,9},{7,11},{8,12},{10,14},{13,17},{15,19},{16,20},{1... | collective-permute-start | bytes 196616 | tf_op jit(solution)/shard_map/ppermute | solution.py:292
  52.7 11.3 %collective-permute-start.2 = (bf16[16,16,128]{2,1,0:T(8,128)(2,1)S(1)}, bf16[16,16,128]{2,1,0:T(8,128)(2,1)S(1)}, u32[]{:S(2)}, u32[]{:S(2)}) collective-permute-start(bf16[16,16,128]{2,1,0:T(8,128)(2,1)S(1)} %get-tuple-element.50), channel_id=1, source_target_pairs={{0,4},{2,6},{5,9},{7,11},{8,12},{10,14},{13,17},{15,19},{16,20},{1... | collective-permute-start | bytes 196616 | tf_op jit(solution)/shard_map/ppermute | solution.py:292
  70.4 11.3 %collective-permute-start.3 = (bf16[16,16,128]{2,1,0:T(8,128)(2,1)S(1)}, bf16[16,16,128]{2,1,0:T(8,128)(2,1)S(1)}, u32[]{:S(2)}, u32[]{:S(2)}) collective-permute-start(bf16[16,16,128]{2,1,0:T(8,128)(2,1)S(1)} %get-tuple-element.55), channel_id=1, source_target_pairs={{0,4},{2,6},{5,9},{7,11},{8,12},{10,14},{13,17},{15,19},{16,20},{1... | collective-permute-start | bytes 196616 | tf_op jit(solution)/shard_map/ppermute | solution.py:292
